TPU v7x, 32 devices: a whole 2x2x4 slice. The times are simulated.
32 devices in a mesh: fsdp: 4 (over y, core), ctx: 4 (over z), tp: 2 (over x).
Axes of the slice: x: 2, y: 2, z: 4, core: 2. Of those that a mesh axis runs over, the one named last changes fastest.
Arguments:
- tokens: bfloat16 [4, 4096, 1024], P('fsdp', 'ctx'), may hold values from -6 to 6
- cotangent: bfloat16 [4, 4096, 1024], P('fsdp', 'ctx'), may hold values from -6 to 6
- block_order: int32 [8], replicated, may hold values from 0 to 7, as said below
- positions: int32 [4, 4096], P('fsdp', 'ctx'), may hold values from 0 to 8190, as said below
- attn_gain: bfloat16 [1024], P('fsdp'), may hold values from 0.5 to 1.5
- w_query: bfloat16 [1024, 1024], P('fsdp', 'tp'), may hold values from -0.1875 to 0.1875
- key_weight: bfloat16 [1024, 512], P('fsdp', 'tp'), may hold values from -0.1875 to 0.1875
- value_weight: bfloat16 [1024, 512], P('fsdp', 'tp'), may hold values from -0.1875 to 0.1875
- query_gain: bfloat16 [64], P('fsdp'), may hold values from 0.25 to 1.75
- key_gain: bfloat16 [64], P('fsdp'), may hold values from 0.25 to 1.75
- w_out: bfloat16 [1024, 1024], P('tp', 'fsdp'), may hold values from -1.5 to 1.5
- ffn_gain: bfloat16 [1024], P('fsdp'), may hold values from 0.5 to 1.5
- w_gate: bfloat16 [1024, 4608], P('fsdp', 'tp'), may hold values from -0.1875 to 0.1875
- w_up: bfloat16 [1024, 4608], P('fsdp', 'tp'), may hold values from -0.1875 to 0.1875
- w_down: bfloat16 [4608, 1024], P('tp', 'fsdp'), may hold values from -0.09375 to 0.09375
Outputs:
- output: bfloat16 [4, 4096, 1024], P('fsdp', 'ctx')
- input_grad: float32 [4, 4096, 1024], P('fsdp', 'ctx')
- attn_gain_grad: float32 [1024], P('fsdp')
- w_query_grad: float32 [1024, 1024], P('fsdp', 'tp')
- w_key_grad: float32 [1024, 512], P('fsdp', 'tp')
- w_value_grad: float32 [1024, 512], P('fsdp', 'tp')
- query_gain_grad: float32 [64], P('fsdp')
- key_gain_grad: float32 [64], P('fsdp')
- w_out_grad: float32 [1024, 1024], P('tp', 'fsdp')
- ffn_gain_grad: float32 [1024], P('fsdp')
- w_gate_grad: float32 [1024, 4608], P('fsdp', 'tp')
- w_up_grad: float32 [1024, 4608], P('fsdp', 'tp')
- w_down_grad: float32 [4608, 1024], P('tp', 'fsdp')
Inputs may be any that keep to these rules, and one draw needn't show every extreme that they name: `block_order`: every block number appears once; the slot pair 2c, 2c + 1 holds blocks b and 7 - b for some b. `positions`: in a sequence's natural token order (see block_order) the first position is 0, each next one is larger by 1, 2 or 3, and the last is 8190; stored in the slot order of tokens.
All inputs are finite; a program needn't handle non-finite values.
Results may differ from a plain program's by a relative error of at most 0.023.
Values may be sent and summed in bfloat16 or wider, within the bound.
No kernel may reach another device: no remote copies, remote signals or barrier semaphores. Data moves between devices by JAX's collectives and lax.ppermute only.
A program may use at most 192 MiB of HBM per device.

v0:
```python
import jax
import jax.numpy as jnp
from jax import lax
from jax.sharding import PartitionSpec as P

HEAD_SIZE = 64


EPSILON = 1e-05
ROPE_BASE = 1000000.0
SCORE_SCALE = 0.125
MASKED = -1e30


def norm_rows(value, gain):
    inverse = lax.rsqrt(jnp.mean(value * value, axis=-1, keepdims=True) + EPSILON)
    return (value * inverse * gain, inverse)


def norm_back(value, inverse, gain, upstream):
    scaled = upstream * gain
    d_value = inverse * scaled - value * inverse * inverse * inverse * jnp.mean(
        value * scaled, axis=-1, keepdims=True
    )
    return (d_value, upstream * value * inverse)


def rotate_half(value):
    middle = value.shape[-1] // 2
    return jnp.concatenate([-value[..., middle:], value[..., :middle]], axis=-1)


def rotate_back(value):
    middle = value.shape[-1] // 2
    return jnp.concatenate([value[..., middle:], -value[..., :middle]], axis=-1)


def rope_tables(positions):
    middle = HEAD_SIZE // 2
    freqs = ROPE_BASE ** (-(jnp.arange(middle, dtype=jnp.float32) * 2.0) / HEAD_SIZE)
    angles = positions.astype(jnp.float32)[..., None] * freqs
    angles = jnp.concatenate([angles, angles], axis=-1)
    return (jnp.cos(angles), jnp.sin(angles))


def apply_rotary(value, cosine, sine):
    return value * cosine + rotate_half(value) * sine


def natural_index(ordering, slot_ids, block_len):
    block_ids = slot_ids // block_len
    matches = block_ids[:, None] == jnp.arange(ordering.shape[0], dtype=jnp.int32)[None, :]
    return (
        jnp.sum(jnp.where(matches, ordering[None, :], 0), axis=1) * block_len + slot_ids % block_len
    )


def key_block(row_count):
    block_size = min(row_count, 512)
    while row_count % block_size:
        block_size = block_size - 1
    return block_size


def per_device(
    tokens,
    cotangent,
    block_order,
    positions,
    attn_gain,
    w_query,
    key_weight,
    value_weight,
    query_gain,
    key_gain,
    w_out,
    ffn_gain,
    w_gate,
    w_up,
    w_down,
):
    seq_count, local_len, width = tokens.shape
    block_len = local_len // 2
    gathered = (
        lax.all_gather(attn_gain, "fsdp", axis=0, tiled=True),
        lax.all_gather(w_query, "fsdp", axis=0, tiled=True),
        lax.all_gather(key_weight, "fsdp", axis=0, tiled=True),
        lax.all_gather(value_weight, "fsdp", axis=0, tiled=True),
        lax.all_gather(query_gain, "fsdp", axis=0, tiled=True),
        lax.all_gather(key_gain, "fsdp", axis=0, tiled=True),
        lax.all_gather(w_out, "fsdp", axis=1, tiled=True),
        lax.all_gather(ffn_gain, "fsdp", axis=0, tiled=True),
        lax.all_gather(w_gate, "fsdp", axis=0, tiled=True),
        lax.all_gather(w_up, "fsdp", axis=0, tiled=True),
        lax.all_gather(w_down, "fsdp", axis=1, tiled=True),
    )
    (
        gain_attn,
        query_mat,
        key_matrix,
        value_matrix,
        gain_query,
        gain_key,
        out_mat,
        gain_ffn,
        gate_mat,
        up_mat,
        down_mat,
    ) = gathered
    gain_attn = gain_attn.astype(jnp.float32)
    gain_query = gain_query.astype(jnp.float32)
    gain_key = gain_key.astype(jnp.float32)
    gain_ffn = gain_ffn.astype(jnp.float32)
    query_heads = query_mat.shape[1] // HEAD_SIZE
    pair_heads = key_matrix.shape[1] // HEAD_SIZE
    group_width = query_heads // pair_heads
    query_slots = lax.axis_index("ctx") * local_len + jnp.arange(local_len, dtype=jnp.int32)
    query_pos = natural_index(block_order, query_slots, block_len)
    cosine, sine = rope_tables(positions)
    cosine = cosine[:, :, None, :]
    sine = sine[:, :, None, :]
    inputs_f = tokens.astype(jnp.float32)
    normed_input, inv_one = norm_rows(inputs_f, gain_attn)
    normed_b = normed_input.astype(jnp.bfloat16)
    query_raw = jnp.dot(normed_b, query_mat, preferred_element_type=jnp.float32).reshape(
        seq_count, local_len, query_heads, HEAD_SIZE
    )
    key_unrotated = jnp.dot(normed_b, key_matrix, preferred_element_type=jnp.float32).reshape(
        seq_count, local_len, pair_heads, HEAD_SIZE
    )
    value_b = jnp.dot(normed_b, value_matrix, preferred_element_type=jnp.float32).astype(
        jnp.bfloat16
    )
    query_normed, query_inv = norm_rows(query_raw, gain_query)
    key_normed, key_inv = norm_rows(key_unrotated, gain_key)
    query_b = apply_rotary(query_normed, cosine, sine).astype(jnp.bfloat16)
    key_b = (
        apply_rotary(key_normed, cosine, sine)
        .astype(jnp.bfloat16)
        .reshape(seq_count, local_len, pair_heads * HEAD_SIZE)
    )
    query_grouped = query_b.reshape(seq_count, local_len, pair_heads, group_width, HEAD_SIZE)
    stat_shape = (seq_count, pair_heads, group_width, local_len)
    initial = (
        jnp.full(stat_shape, MASKED, jnp.float32),
        jnp.zeros(stat_shape, jnp.float32),
        jnp.zeros(stat_shape + (HEAD_SIZE,), jnp.float32),
    )
    key_rows = lax.all_gather(key_b, "ctx", axis=1, tiled=True)
    value_tokens = lax.all_gather(value_b, "ctx", axis=1, tiled=True)
    row_count = key_rows.shape[1]
    block_size = key_block(row_count)
    key_pos = natural_index(block_order, jnp.arange(row_count, dtype=jnp.int32), block_len)

    def advance(state, block_id):
        run_max, totals, accum = state
        offset = block_id * block_size
        key_blk = lax.dynamic_slice_in_dim(key_rows, offset, block_size, 1).reshape(
            seq_count, block_size, pair_heads, HEAD_SIZE
        )
        value_blk = lax.dynamic_slice_in_dim(value_tokens, offset, block_size, 1).reshape(
            seq_count, block_size, pair_heads, HEAD_SIZE
        )
        pos_blk = lax.dynamic_slice_in_dim(key_pos, offset, block_size, 0)
        scores = (
            jnp.einsum(
                "sqgrd,skgd->sgrqk", query_grouped, key_blk, preferred_element_type=jnp.float32
            )
            * SCORE_SCALE
        )
        visible = pos_blk[None, :] <= query_pos[:, None]
        scores = jnp.where(visible, scores, MASKED)
        new_max = jnp.maximum(run_max, jnp.max(scores, axis=-1))
        weights_blk = jnp.where(visible, jnp.exp(scores - new_max[..., None]), 0.0)
        fading = jnp.exp(run_max - new_max)
        totals = totals * fading + jnp.sum(weights_blk, axis=-1)
        accum = accum * fading[..., None] + jnp.einsum(
            "sgrqk,skgd->sgrqd",
            weights_blk.astype(jnp.bfloat16),
            value_blk,
            preferred_element_type=jnp.float32,
        )
        return ((new_max, totals, accum), None)

    state_out, unused_out = lax.scan(advance, initial, jnp.arange(row_count // block_size))
    state = state_out
    run_max, totals, accum = state
    attn_mix = accum / totals[..., None]
    log_total = run_max + jnp.log(totals)
    mixed = jnp.transpose(attn_mix, (0, 3, 1, 2, 4)).reshape(
        seq_count, local_len, query_heads * HEAD_SIZE
    )
    mixed_b = mixed.astype(jnp.bfloat16)
    attn_out = lax.psum(
        jnp.dot(mixed_b, out_mat, preferred_element_type=jnp.float32).astype(jnp.bfloat16), "tp"
    ).astype(jnp.float32)
    resid = inputs_f + attn_out
    normed_two, inv_two = norm_rows(resid, gain_ffn)
    normed_two_b = normed_two.astype(jnp.bfloat16)
    gate_val = jnp.dot(normed_two_b, gate_mat, preferred_element_type=jnp.float32)
    up_val = jnp.dot(normed_two_b, up_mat, preferred_element_type=jnp.float32)
    hidden_b = (jax.nn.silu(gate_val) * up_val).astype(jnp.bfloat16)
    down_sum = lax.psum(
        jnp.dot(hidden_b, down_mat, preferred_element_type=jnp.float32).astype(jnp.bfloat16), "tp"
    ).astype(jnp.float32)
    output = (resid + down_sum).astype(jnp.bfloat16)
    grad_out = cotangent.astype(jnp.float32)
    down_w_grad = jnp.einsum("stf,std->fd", hidden_b, cotangent, preferred_element_type=jnp.float32)
    hidden_grad = jnp.einsum("std,fd->stf", cotangent, down_mat, preferred_element_type=jnp.float32)
    sigmoid_g = jax.nn.sigmoid(gate_val)
    gate_grad_b = (hidden_grad * up_val * sigmoid_g * (1.0 + gate_val * (1.0 - sigmoid_g))).astype(
        jnp.bfloat16
    )
    up_grad_b = (hidden_grad * jax.nn.silu(gate_val)).astype(jnp.bfloat16)
    gate_w_grad = jnp.einsum(
        "std,stf->df", normed_two_b, gate_grad_b, preferred_element_type=jnp.float32
    )
    up_w_grad = jnp.einsum(
        "std,stf->df", normed_two_b, up_grad_b, preferred_element_type=jnp.float32
    )
    normed_two_part = jnp.einsum(
        "stf,df->std", gate_grad_b, gate_mat, preferred_element_type=jnp.float32
    ) + jnp.einsum("stf,df->std", up_grad_b, up_mat, preferred_element_type=jnp.float32)
    normed_two_grad = lax.psum(normed_two_part.astype(jnp.bfloat16), "tp").astype(jnp.float32)
    resid_part, ffn_term = norm_back(resid, inv_two, gain_ffn, normed_two_grad)
    ffn_gain_grad = jnp.sum(ffn_term, axis=(0, 1))
    resid_grad = grad_out + resid_part
    resid_grad_b = resid_grad.astype(jnp.bfloat16)
    out_w_grad = jnp.einsum(
        "stc,std->cd", mixed_b, resid_grad_b, preferred_element_type=jnp.float32
    )
    mixed_grad_b = jnp.einsum(
        "std,cd->stc", resid_grad_b, out_mat, preferred_element_type=jnp.float32
    ).astype(jnp.bfloat16)
    grad_grouped = mixed_grad_b.reshape(seq_count, local_len, pair_heads, group_width, HEAD_SIZE)
    delta = jnp.transpose(
        jnp.sum(
            grad_grouped.astype(jnp.float32)
            * mixed.reshape(seq_count, local_len, pair_heads, group_width, HEAD_SIZE),
            axis=-1,
        ),
        (0, 2, 3, 1),
    )
    key_back, value_back = (
        lax.all_gather(key_b, "ctx", axis=1, tiled=True),
        lax.all_gather(value_b, "ctx", axis=1, tiled=True),
    )
    total_rows = key_back.shape[1]
    back_size = key_block(total_rows)
    key_pos_all = natural_index(block_order, jnp.arange(total_rows, dtype=jnp.int32), block_len)

    def retrace(query_acc, block_id):
        offset = block_id * back_size
        key_blk = lax.dynamic_slice_in_dim(key_back, offset, back_size, 1).reshape(
            seq_count, back_size, pair_heads, HEAD_SIZE
        )
        value_blk = lax.dynamic_slice_in_dim(value_back, offset, back_size, 1).reshape(
            seq_count, back_size, pair_heads, HEAD_SIZE
        )
        pos_blk = lax.dynamic_slice_in_dim(key_pos_all, offset, back_size, 0)
        scores = (
            jnp.einsum(
                "sqgrd,skgd->sgrqk", query_grouped, key_blk, preferred_element_type=jnp.float32
            )
            * SCORE_SCALE
        )
        visible = pos_blk[None, :] <= query_pos[:, None]
        probs = jnp.where(
            visible, jnp.exp(jnp.where(visible, scores, MASKED) - log_total[..., None]), 0.0
        )
        prob_grad = jnp.einsum(
            "sqgrd,skgd->sgrqk", grad_grouped, value_blk, preferred_element_type=jnp.float32
        )
        score_grad = (probs * (prob_grad - delta[..., None])).astype(jnp.bfloat16)
        value_part = jnp.einsum(
            "sgrqk,sqgrd->skgd",
            probs.astype(jnp.bfloat16),
            grad_grouped,
            preferred_element_type=jnp.float32,
        )
        key_part = (
            jnp.einsum(
                "sgrqk,sqgrd->skgd", score_grad, query_grouped, preferred_element_type=jnp.float32
            )
            * SCORE_SCALE
        )
        query_acc = (
            query_acc
            + jnp.einsum(
                "sgrqk,skgd->sqgrd", score_grad, key_blk, preferred_element_type=jnp.float32
            )
            * SCORE_SCALE
        )
        return (
            query_acc,
            (
                key_part.reshape(seq_count, back_size, pair_heads * HEAD_SIZE),
                value_part.reshape(seq_count, back_size, pair_heads * HEAD_SIZE),
            ),
        )

    query_zero = jnp.zeros((seq_count, local_len, pair_heads, group_width, HEAD_SIZE), jnp.float32)
    query_acc, (key_parts, value_parts) = lax.scan(
        retrace, query_zero, jnp.arange(total_rows // back_size)
    )
    key_terms = jnp.moveaxis(key_parts, 0, 1).reshape(seq_count, total_rows, pair_heads * HEAD_SIZE)
    value_terms = jnp.moveaxis(value_parts, 0, 1).reshape(
        seq_count, total_rows, pair_heads * HEAD_SIZE
    )
    key_grad, value_grad = (
        lax.psum_scatter(
            key_terms.astype(jnp.bfloat16), "ctx", scatter_dimension=1, tiled=True
        ).astype(jnp.float32),
        lax.psum_scatter(
            value_terms.astype(jnp.bfloat16), "ctx", scatter_dimension=1, tiled=True
        ).astype(jnp.float32),
    )
    value_grad_b = value_grad.astype(jnp.bfloat16)
    key_rot_grad = key_grad.reshape(seq_count, local_len, pair_heads, HEAD_SIZE)
    key_norm_grad = key_rot_grad * cosine + rotate_back(key_rot_grad * sine)
    key_raw_grad, key_term = norm_back(key_unrotated, key_inv, gain_key, key_norm_grad)
    key_raw_b = key_raw_grad.reshape(seq_count, local_len, pair_heads * HEAD_SIZE).astype(
        jnp.bfloat16
    )
    query_rot_grad = query_acc.reshape(seq_count, local_len, query_heads, HEAD_SIZE)
    query_norm_grad = query_rot_grad * cosine + rotate_back(query_rot_grad * sine)
    query_raw_grad, query_term = norm_back(query_raw, query_inv, gain_query, query_norm_grad)
    query_raw_b = query_raw_grad.reshape(seq_count, local_len, query_heads * HEAD_SIZE).astype(
        jnp.bfloat16
    )
    query_w_grad = jnp.einsum(
        "std,stc->dc", normed_b, query_raw_b, preferred_element_type=jnp.float32
    )
    key_w_grad = jnp.einsum("std,stc->dc", normed_b, key_raw_b, preferred_element_type=jnp.float32)
    value_w_grad = jnp.einsum(
        "std,stc->dc", normed_b, value_grad_b, preferred_element_type=jnp.float32
    )
    normed_part = jnp.einsum(
        "stc,dc->std", query_raw_b, query_mat, preferred_element_type=jnp.float32
    )
    normed_part = normed_part + jnp.einsum(
        "stc,dc->std", key_raw_b, key_matrix, preferred_element_type=jnp.float32
    )
    normed_part = normed_part + jnp.einsum(
        "stc,dc->std", value_grad_b, value_matrix, preferred_element_type=jnp.float32
    )
    normed_grad, query_gain_part, key_gain_part = (
        lax.psum(normed_part.astype(jnp.bfloat16), "tp").astype(jnp.float32),
        lax.psum(jnp.sum(query_term, axis=(0, 1, 2)).astype(jnp.bfloat16), "tp").astype(
            jnp.float32
        ),
        lax.psum(jnp.sum(key_term, axis=(0, 1, 2)).astype(jnp.bfloat16), "tp").astype(jnp.float32),
    )
    input_part, attn_term = norm_back(inputs_f, inv_one, gain_attn, normed_grad)
    input_grad = resid_grad + input_part
    attn_gain_part = jnp.sum(attn_term, axis=(0, 1))
    (
        g_attn_s,
        g_query_s,
        g_key_s,
        g_value_s,
        g_qgain_s,
        g_kgain_s,
        g_out_s,
        g_ffn_s,
        g_gate_s,
        g_up_s,
        g_down_s,
    ) = (
        lax.psum_scatter(
            attn_gain_part.astype(jnp.bfloat16), "fsdp", scatter_dimension=0, tiled=True
        ).astype(jnp.float32),
        lax.psum_scatter(
            query_w_grad.astype(jnp.bfloat16), "fsdp", scatter_dimension=0, tiled=True
        ).astype(jnp.float32),
        lax.psum_scatter(
            key_w_grad.astype(jnp.bfloat16), "fsdp", scatter_dimension=0, tiled=True
        ).astype(jnp.float32),
        lax.psum_scatter(
            value_w_grad.astype(jnp.bfloat16), "fsdp", scatter_dimension=0, tiled=True
        ).astype(jnp.float32),
        lax.psum_scatter(
            query_gain_part.astype(jnp.bfloat16), "fsdp", scatter_dimension=0, tiled=True
        ).astype(jnp.float32),
        lax.psum_scatter(
            key_gain_part.astype(jnp.bfloat16), "fsdp", scatter_dimension=0, tiled=True
        ).astype(jnp.float32),
        lax.psum_scatter(
            out_w_grad.astype(jnp.bfloat16), "fsdp", scatter_dimension=1, tiled=True
        ).astype(jnp.float32),
        lax.psum_scatter(
            ffn_gain_grad.astype(jnp.bfloat16), "fsdp", scatter_dimension=0, tiled=True
        ).astype(jnp.float32),
        lax.psum_scatter(
            gate_w_grad.astype(jnp.bfloat16), "fsdp", scatter_dimension=0, tiled=True
        ).astype(jnp.float32),
        lax.psum_scatter(
            up_w_grad.astype(jnp.bfloat16), "fsdp", scatter_dimension=0, tiled=True
        ).astype(jnp.float32),
        lax.psum_scatter(
            down_w_grad.astype(jnp.bfloat16), "fsdp", scatter_dimension=1, tiled=True
        ).astype(jnp.float32),
    )
    (
        attn_gain_grad,
        w_query_grad,
        w_key_grad,
        w_value_grad,
        query_gain_grad,
        key_gain_grad,
        w_out_grad,
        ffn_gain_final,
        w_gate_grad,
        w_up_grad,
        w_down_grad,
    ) = (
        lax.psum(g_attn_s.astype(jnp.bfloat16), "ctx").astype(jnp.float32),
        lax.psum(g_query_s.astype(jnp.bfloat16), "ctx").astype(jnp.float32),
        lax.psum(g_key_s.astype(jnp.bfloat16), "ctx").astype(jnp.float32),
        lax.psum(g_value_s.astype(jnp.bfloat16), "ctx").astype(jnp.float32),
        lax.psum(g_qgain_s.astype(jnp.bfloat16), "ctx").astype(jnp.float32),
        lax.psum(g_kgain_s.astype(jnp.bfloat16), "ctx").astype(jnp.float32),
        lax.psum(g_out_s.astype(jnp.bfloat16), "ctx").astype(jnp.float32),
        lax.psum(g_ffn_s.astype(jnp.bfloat16), "ctx").astype(jnp.float32),
        lax.psum(g_gate_s.astype(jnp.bfloat16), "ctx").astype(jnp.float32),
        lax.psum(g_up_s.astype(jnp.bfloat16), "ctx").astype(jnp.float32),
        lax.psum(g_down_s.astype(jnp.bfloat16), "ctx").astype(jnp.float32),
    )
    return (
        output,
        input_grad,
        attn_gain_grad,
        w_query_grad,
        w_key_grad,
        w_value_grad,
        query_gain_grad,
        key_gain_grad,
        w_out_grad,
        ffn_gain_final,
        w_gate_grad,
        w_up_grad,
        w_down_grad,
    )


def solution(mesh):
    placed = (
        P("fsdp", "ctx", None),
        P("fsdp", "ctx", None),
        P(),
        P("fsdp", "ctx"),
        P("fsdp"),
        P("fsdp", "tp"),
        P("fsdp", "tp"),
        P("fsdp", "tp"),
        P("fsdp"),
        P("fsdp"),
        P("tp", "fsdp"),
        P("fsdp"),
        P("fsdp", "tp"),
        P("fsdp", "tp"),
        P("tp", "fsdp"),
    )
    return jax.shard_map(
        per_device,
        mesh=mesh,
        in_specs=placed,
        out_specs=(
            P("fsdp", "ctx", None),
            P("fsdp", "ctx", None),
            P("fsdp"),
            P("fsdp", "tp"),
            P("fsdp", "tp"),
            P("fsdp", "tp"),
            P("fsdp"),
            P("fsdp"),
            P("tp", "fsdp"),
            P("fsdp"),
            P("fsdp", "tp"),
            P("fsdp", "tp"),
            P("tp", "fsdp"),
        ),
        check_vma=False,
    )
```

profile of v0, /device:TPU:0, one launch (start us, length us, event | category | flops | bytes accessed | tf_op | source)
XLA Modules:
  0.0 1634.6 jit_solution(2799738813197259804)
XLA Ops:
  58.4 19.8 %all-gather.24.cloned.1.call-done = bf16[4096,256]{1,0:T(8,128)(2,1)} async-done(((bf16[1024,256]{1,0:T(8,128)(2,1)}), bf16[4096,256]{1,0:T(8,128)(2,1)}) %all-gather.24.cloned.1.call-update) | async-done | bytes 2097168 | tf_op jit(solution)/shard_map/all_gather | solution.py:150
  82.3 42.7 %all-gather.22.cloned.1.call-done = bf16[4096,256]{0,1:T(8,128)(2,1)} async-done(((bf16[1024,256]{0,1:T(8,128)(2,1)}), bf16[4096,256]{0,1:T(8,128)(2,1)}) %all-gather.22.cloned.1.call-update) | async-done | bytes 2097168 | tf_op jit(solution)/shard_map/all_gather | solution.py:149
  125.0 229.2 %while.30 = (s32[]{:T(128)}, f32[1,4,2,1024]{3,2,1,0:T(2,128)S(1)}, f32[1,4,2,1024]{3,2,1,0:T(2,128)S(1)}, f32[1,4,2,1024,64]{3,4,2,1,0:T(8,128)}, s32[8]{0:T(12...) while((s32[]{:T(128)}, f32[1,4,2,1024]{3,2,1,0:T(2,128)S(1)}, ...), condition=%wide.region_8.9_spmd.clone, body=%wide.region_5.8_spmd.clone.sunk | while | flops 1130414080 | bytes 131082544 | solution.py:185
  369.2 54.2 %all-reduce.17.cloned.1.call-done = bf16[1,1024,1024]{2,1,0:T(8,128)(2,1)} async-done(((bf16[1,1024,1024]{2,1,0:T(8,128)(2,1)}), bf16[1,1024,1024]{2,1,0:T(8,128)(2,1)}) %all-reduce.17.cloned.1.call-update) | async-done | bytes 2097168 | tf_op jit(solution)/shard_map/psum | solution.py:194
  428.0 34.4 %all-gather.16.cloned.1.call-done = bf16[1024,2304]{1,0:T(8,128)(2,1)} async-done(((bf16[256,2304]{1,0:T(8,128)(2,1)}), bf16[1024,2304]{1,0:T(8,128)(2,1)}) %all-gather.16.cloned.1.call-update) | async-done | bytes 4718608 | tf_op jit(solution)/shard_map/all_gather | solution.py:93
  472.4 29.1 %all-gather.18.cloned.1.call-done = bf16[1024,2304]{1,0:T(8,128)(2,1)} async-done(((bf16[256,2304]{1,0:T(8,128)(2,1)}), bf16[1024,2304]{1,0:T(8,128)(2,1)}) %all-gather.18.cloned.1.call-update) | async-done | bytes 4718608 | tf_op jit(solution)/shard_map/all_gather | solution.py:94
  511.6 29.6 %all-gather.20.cloned.1.call-done = bf16[2304,1024]{1,0:T(8,128)(2,1)} async-done(((bf16[2304,256]{1,0:T(8,128)(2,1)}), bf16[2304,1024]{1,0:T(8,128)(2,1)}) %all-gather.20.cloned.1.call-update) | async-done | bytes 4718608 | tf_op jit(solution)/shard_map/all_gather | solution.py:95
  541.2 18.2 %multiply_convert_fusion = (bf16[1024,2304]{1,0:T(8,128)(2,1)}, bf16[1024,2304]{1,0:T(8,128)(2,1)}, bf16[1024,2304]{1,0:T(8,128)(2,1)}) fusion(f32[1024,2304]{1,0:T(8,128)} %fusion.128, f32[1024,2304]{1,0:T(8,128)} %fusion.129, bf16[2304,1024]{1,0:T(8,128)(2,1)} %all-gather.20.cloned.1.call-done, bf16[1,1024,1024]{2,1,0:T(8,128)(2,1)S(1)} %copy-done.30), kind=kOutput, calls=%fused_computation.55 | convolution fusion | flops 4867227648 | bytes 39845888 | tf_op jit(solution)/shard_map/std,fd->stf/dot_general | solution.py:209
  575.0 62.4 %all-reduce.19.cloned.1.call-done = bf16[1,1024,1024]{2,1,0:T(8,128)(2,1)} async-done(((bf16[1,1024,1024]{2,1,0:T(8,128)(2,1)}), bf16[1,1024,1024]{2,1,0:T(8,128)(2,1)}) %all-reduce.19.cloned.1.call-update) | async-done | bytes 2097168 | tf_op jit(solution)/shard_map/psum | solution.py:224
  650.2 340.5 %while.31 = (s32[]{:T(128)}, f32[1,1024,4,2,64]{1,4,3,2,0:T(8,128)S(1)}, bf16[8,1,512,256]{2,3,1,0:T(8,128)(2,1)}, bf16[8,1,512,256]{3,2,0,1:T(8,128)(2,1)}, s32...) while((s32[]{:T(128)}, ...), condition=%wide.region_16.17_spmd.clone, body=%wide.region_15.16_spmd.clone.sunk | while | flops 2737045504 | bytes 196585872 | solution.py:303
  681.6 10.5 fusion.206
  766.5 10.5 fusion.206
  809.0 10.5 fusion.206
  894.0 10.5 fusion.206
  1006.8 31.2 %reduce-scatter.10.cloned.1.call-done = bf16[1,1024,256]{1,2,0:T(8,128)(2,1)} async-done(((bf16[1,4096,256]{1,2,0:T(8,128)(2,1)}), bf16[1,1024,256]{1,2,0:T(8,128)(2,1)}) %reduce-scatter.10.cloned.1.call-update) | async-done | bytes 524304 | tf_op jit(solution)/shard_map/reduce_scatter | solution.py:311
  1043.2 40.5 %reduce-scatter.12.cloned.1.call-done = bf16[1,1024,256]{2,1,0:T(8,128)(2,1)} async-done(((bf16[1,4096,256]{2,1,0:T(8,128)(2,1)}), bf16[1,1024,256]{2,1,0:T(8,128)(2,1)}) %reduce-scatter.12.cloned.1.call-update) | async-done | bytes 524304 | tf_op jit(solution)/shard_map/reduce_scatter | solution.py:314
  1138.5 24.6 %reduce-scatter.16.cloned.1.call-done = bf16[256,256]{1,0:T(8,128)(2,1)} async-done(((bf16[1024,256]{1,0:T(8,128)(2,1)}), bf16[256,256]{1,0:T(8,128)(2,1)}) %reduce-scatter.16.cloned.1.call-update) | async-done | bytes 131088 | tf_op jit(solution)/shard_map/reduce_scatter | solution.py:376
  1163.1 24.1 %reduce-scatter.18.cloned.1.call-done = bf16[256,256]{1,0:T(8,128)(2,1)} async-done(((bf16[1024,256]{1,0:T(8,128)(2,1)}), bf16[256,256]{1,0:T(8,128)(2,1)}) %reduce-scatter.18.cloned.1.call-update) | async-done | bytes 131088 | tf_op jit(solution)/shard_map/reduce_scatter | solution.py:379
  1187.2 50.2 %reduce-scatter.22.cloned.1.call-done = bf16[256,2304]{1,0:T(8,128)(2,1)} async-done(((bf16[1024,2304]{1,0:T(8,128)(2,1)}), bf16[256,2304]{1,0:T(8,128)(2,1)}) %reduce-scatter.22.cloned.1.call-update) | async-done | bytes 1179664 | tf_op jit(solution)/shard_map/reduce_scatter | solution.py:394
  1237.5 50.4 %reduce-scatter.24.cloned.1.call-done = bf16[256,2304]{1,0:T(8,128)(2,1)} async-done(((bf16[1024,2304]{1,0:T(8,128)(2,1)}), bf16[256,2304]{1,0:T(8,128)(2,1)}) %reduce-scatter.24.cloned.1.call-update) | async-done | bytes 1179664 | tf_op jit(solution)/shard_map/reduce_scatter | solution.py:397
  1287.9 50.2 %reduce-scatter.26.cloned.1.call-done = bf16[2304,256]{1,0:T(8,128)(2,1)} async-done(((bf16[2304,1024]{1,0:T(8,128)(2,1)}), bf16[2304,256]{1,0:T(8,128)(2,1)}) %reduce-scatter.26.cloned.1.call-update) | async-done | bytes 1179664 | tf_op jit(solution)/shard_map/reduce_scatter | solution.py:400
  1339.0 111.2 %all-reduce.23.cloned.1.call-done = (bf16[1,1024,1024]{2,1,0:T(8,128)(2,1)}, bf16[1,1024,1024]{2,1,0:T(8,128)(2,1)}) async-done(((bf16[1,1024,1024]{2,1,0:T(8,128)(2,1)}, bf16[1,1024,1024]{2,1,0:T(8,128)(2,1)}), (bf16[1,1024,1024]{2,1,0:T(8,128)(2,1)}, bf16[1,1024,1024]{2,1,0:T(8,128)(2,1)})) %all-reduce.23.cloned.1.call-update) | async-done | bytes 4194320 | tf_op jit(solution)/shard_map/psum | solution.py:203
  1466.4 12.0 all-reduce.6
  1487.4 127.2 %all-reduce.21.cloned.1.call-done = (bf16[256,512]{1,0:T(8,128)(2,1)}, bf16[256,256]{1,0:T(8,128)(2,1)}, bf16[256,256]{1,0:T(8,128)(2,1)}, bf16[512,256]{1,0:T(8...) async-done(((bf16[256,512]{1,0:T(8,128)(2,1)}, bf16[256,256]{1,0:T(8,128)(2,1)}, bf16[256,256]{1,0:T(8,128)(2,1)}, ...) | async-done | bytes 4325392 | tf_op jit(solution)/shard_map/psum | solution.py:418
  (587 shorter events, 751.1 us)
Async XLA Ops:
  7.2 43.7 %all-gather.12.cloned.1.call-start = ((), (), s32[]{:S(2)}) async-start(), calls=%async_computation.9 | async-start | bytes 1310720 | tf_op jit(solution)/shard_map/all_gather | solution.py:86
  7.9 70.3 %all-gather.24.cloned.1.call-start = ((), (), s32[]{:S(2)}) async-start(), calls=%async_computation.26 | async-start | bytes 2621440 | tf_op jit(solution)/shard_map/all_gather | solution.py:150
  14.6 36.2 %copy-start.48 = (f32[4,1,256]{2,1,0:T(1,128)}, f32[4,1,256]{2,1,0:T(1,128)S(1)}, u32[]{:S(2)}) copy-start(f32[4,1,256]{2,1,0:T(1,128)S(1)} %convert_element_type.340) | copy-start | bytes 12292
  28.3 96.7 %all-gather.22.cloned.1.call-start = ((), (), s32[]{:S(2)}) async-start(), calls=%async_computation.25 | async-start | bytes 2621440 | tf_op jit(solution)/shard_map/all_gather | solution.py:149
  49.7 307.7 %all-gather.14.cloned.1.call-start = ((), (), s32[]{:S(2)}) async-start(), calls=%async_computation.10 | async-start | bytes 1310720 | tf_op jit(solution)/shard_map/all_gather | solution.py:91
  50.3 373.1 %all-reduce.17.cloned.1.call-start = ((), (), s32[]{:S(2)}) async-start(), calls=%async_computation.11 | async-start | bytes 4194304 | tf_op jit(solution)/shard_map/psum | solution.py:194
  354.2 73.8 %copy-start.3 = (bf16[1,1024,4,2,64]{1,4,3,2,0:T(8,128)(2,1)}, bf16[1,1024,4,2,64]{1,4,3,2,0:T(8,128)(2,1)S(1)}, u32[]{:S(2)}) copy-start(bf16[1,1024,4,2,64]{1,4,3,2,0:T(8,128)(2,1)S(1)} %get-tuple-element.698) | copy-start | bytes 3145732
  361.6 100.8 %all-gather.16.cloned.1.call-start = ((), (), s32[]{:S(2)}) async-start(), calls=%async_computation.12 | async-start | bytes 5898240 | tf_op jit(solution)/shard_map/all_gather | solution.py:93
  362.2 139.3 %all-gather.18.cloned.1.call-start = ((), (), s32[]{:S(2)}) async-start(), calls=%async_computation.13 | async-start | bytes 5898240 | tf_op jit(solution)/shard_map/all_gather | solution.py:94
  362.9 178.3 %all-gather.20.cloned.1.call-start = ((), (), s32[]{:S(2)}) async-start(), calls=%async_computation.14 | async-start | bytes 5898240 | tf_op jit(solution)/shard_map/all_gather | solution.py:95
  363.7 273.7 %all-reduce.19.cloned.1.call-start = ((), (), s32[]{:S(2)}) async-start(), calls=%async_computation.15 | async-start | bytes 4194304 | tf_op jit(solution)/shard_map/psum | solution.py:224
  472.4 68.8 %copy-start.30 = (bf16[1,1024,1024]{2,1,0:T(8,128)(2,1)S(1)}, bf16[1,1024,1024]{2,1,0:T(8,128)(2,1)}, u32[]{:S(2)}) copy-start(bf16[1,1024,1024]{2,1,0:T(8,128)(2,1)} %param.20) | copy-start | bytes 6291460
  574.3 463.7 %reduce-scatter.10.cloned.1.call-start = ((), (), s32[]{:S(2)}) async-start(), calls=%async_computation.16 | async-start | bytes 2621440 | tf_op jit(solution)/shard_map/reduce_scatter | solution.py:311
  994.0 89.7 %reduce-scatter.12.cloned.1.call-start = ((), (), s32[]{:S(2)}) async-start(), calls=%async_computation.17 | async-start | bytes 2621440 | tf_op jit(solution)/shard_map/reduce_scatter | solution.py:314
  994.7 134.7 %reduce-scatter.14.cloned.1.call-start = ((), (), s32[]{:S(2)}) async-start(), calls=%async_computation.18 | async-start | bytes 1310720 | tf_op jit(solution)/shard_map/reduce_scatter | solution.py:373
  1002.2 136.3 %reduce-scatter.20.cloned.1.call-start = ((), (), s32[]{:S(2)}) async-start(), calls=%async_computation.21 | async-start | bytes 1310720 | tf_op jit(solution)/shard_map/reduce_scatter | solution.py:388
  1006.7 156.4 %reduce-scatter.16.cloned.1.call-start = ((), (), s32[]{:S(2)}) async-start(), calls=%async_computation.19 | async-start | bytes 655360 | tf_op jit(solution)/shard_map/reduce_scatter | solution.py:376
  1043.1 144.1 %reduce-scatter.18.cloned.1.call-start = ((), (), s32[]{:S(2)}) async-start(), calls=%async_computation.20 | async-start | bytes 655360 | tf_op jit(solution)/shard_map/reduce_scatter | solution.py:379
  1086.5 151.0 %reduce-scatter.22.cloned.1.call-start = ((), (), s32[]{:S(2)}) async-start(), calls=%async_computation.22 | async-start | bytes 5898240 | tf_op jit(solution)/shard_map/reduce_scatter | solution.py:394
  1096.0 191.9 %reduce-scatter.24.cloned.1.call-start = ((), (), s32[]{:S(2)}) async-start(), calls=%async_computation.23 | async-start | bytes 5898240 | tf_op jit(solution)/shard_map/reduce_scatter | solution.py:397
  1105.7 232.4 %reduce-scatter.26.cloned.1.call-start = ((), (), s32[]{:S(2)}) async-start(), calls=%async_computation.24 | async-start | bytes 5898240 | tf_op jit(solution)/shard_map/reduce_scatter | solution.py:400
  1115.3 334.9 %all-reduce.23.cloned.1.call-start = ((), (), s32[]{:S(2)}) async-start(), calls=%async_computation.28 | async-start | bytes 8388608 | tf_op jit(solution)/shard_map/psum | solution.py:203
  1129.4 485.2 %all-reduce.21.cloned.1.call-start = ((), (), s32[]{:S(2)}) async-start(), calls=%async_computation.27 | async-start | bytes 8650752 | tf_op jit(solution)/shard_map/psum | solution.py:418
  1338.2 115.3 %copy-start.55 = (bf16[1024]{0:T(1024)(128)(2,1)S(1)}, bf16[1024]{0:T(1024)(128)(2,1)}, u32[]{:S(2)}) copy-start(bf16[1024]{0:T(1024)(128)(2,1)} %get-tuple-element.309) | copy-start | bytes 6148
  (123 other events, 870.7 us)
Sparse Core Ops, SparseCore 0:
  9.6 19.4 all-gather.11
  31.2 46.9 all-gather.23
  80.4 44.6 all-gather.21
  126.4 15.5 all-gather.13
  361.7 61.6 all-reduce.16
  424.9 37.4 all-gather.15
  464.0 37.4 all-gather.17
  503.1 38.0 all-gather.19
  574.4 62.9 all-reduce.18
  994.1 43.8 reduce-scatter.9
  1040.4 43.1 reduce-scatter.11
  1086.6 24.2 reduce-scatter.13
  1113.5 24.9 reduce-scatter.19
  1141.4 21.6 reduce-scatter.15
  1165.6 21.6 reduce-scatter.17
  1189.6 47.8 reduce-scatter.21
  1240.0 47.8 reduce-scatter.23
  1290.3 47.8 reduce-scatter.25
  1341.9 108.2 all-reduce.22
  1453.0 161.5 all-reduce.20
where the time goes:
time: 1640 us; the launch traced here: 1630 us
  waiting for transfers between devices  795 us (48%)
  matrix products  493 us (30%)
  other arithmetic  143 us (9%)
  local copies, waits for them, and re-layouts  114 us (7%)
  blocking collectives  58.6 us (4%)
  between operations  17.5 us (1%)
    psum x1, waiting for transfers between devices, per_device(): lax.psum(g_query_s.astype(jnp.bfloat16), 'ctx').astype(jnp.float32)  127 us
    psum x1, waiting for transfers between devices, per_device(): lax.psum(jnp.dot(hidden_b, down_mat, preferred_element_type=jnp.float32)....  111 us
    dot_general x8, matrix products, retrace(): jnp.einsum('sgrqk,sqgrd->skgd', probs.astype(jnp.bfloat16), grad_grouped,...  83.6 us
    dot_general x8, matrix products, retrace(): jnp.einsum('sqgrd,skgd->sgrqk', grad_grouped, value_blk, preferred_elemen...  79.5 us
    reduce_sum x8, other arithmetic, advance(): totals = totals * fading + jnp.sum(weights_blk, axis=-1)  70.5 us
    psum x1, waiting for transfers between devices, per_device(): lax.psum(normed_two_part.astype(jnp.bfloat16), 'tp').astype(jnp.float32)  62.4 us
    dot_general x8, matrix products, advance(): jnp.einsum('sgrqk,skgd->sgrqd', weights_blk.astype(jnp.bfloat16), value_b...  59.2 us
    dot_general x8, matrix products, advance(): jnp.einsum('sqgrd,skgd->sgrqk', query_grouped, key_blk, preferred_element...  58.5 us
  transfers between devices with their start and end apart: 20, of which 17 were waited for; matrix products, arithmetic and copies ran while one was open for 20% of the time, Pallas kernels for 0%

commit v1 on v0

v1 whole, which is shorter than its diff:
```python
import functools

import jax
import jax.numpy as jnp
from jax import lax
from jax.experimental import pallas as pl
from jax.experimental.pallas import tpu as pltpu
from jax.sharding import PartitionSpec as P

HD = 64
EPSILON = 1e-05
ROPE_BASE = 1000000.0
LOG2E = 1.4426950408889634
SCALE2 = 0.125 * LOG2E
NT = (((1,), (1,)), ((), ()))
NN = (((1,), (0,)), ((), ()))
TN = (((0,), (0,)), ((), ()))
F32, BF16 = jnp.float32, jnp.bfloat16


def mm(a, b, dims=NN):
    return lax.dot_general(a, b, dims, preferred_element_type=F32)


def half(shape, which):
    lane = lax.broadcasted_iota(jnp.int32, shape, len(shape) - 1)
    return (lane < HD) if which == 0 else (lane >= HD)


def pieces(own, meta, block):
    at = [pl.multiple_of(meta[n], block) for n in range(4)]
    if own:
        return [(at[0], at[0], True), (at[1], at[0], False), (at[1], at[1], True)]
    return [(at[0], at[1], False), (at[2], at[3], False)]


def attend_body(own, first, last, block, meta, q_ref, kv_ref, *rest):
    rest = list(rest)
    given = None if first else rest.pop(0)
    if last:
        mixb_ref, mix_ref, lse_ref, acc = rest
    else:
        (acc,) = rest
    acc[...] = jnp.zeros_like(acc) if first else given[...]
    for q_at, k_at, diagonal in pieces(own, meta, block):
        kt = kv_ref[pl.ds(k_at, block), 0:128]
        vt = kv_ref[pl.ds(k_at, block), 128:256]
        one = jnp.ones((block, HD), BF16)
        for hh in range(2):
            kh = kt[:, HD * hh : HD * hh + HD]
            vh = vt[:, HD * hh : HD * hh + HD]
            kd = jnp.concatenate([kh, kh], axis=1)
            vx = (jnp.concatenate([vh, one], axis=1), jnp.concatenate([one, vh], axis=1))
            qt = q_ref[pl.ds(q_at, block), 128 * hh : 128 * hh + 128]
            for r in range(2):
                qr = jnp.where(half((block, 128), r), qt, jnp.zeros_like(qt))
                p = jnp.exp2(mm(qr, kd, NT) * SCALE2)
                if diagonal:
                    row = lax.broadcasted_iota(jnp.int32, p.shape, 0)
                    col = lax.broadcasted_iota(jnp.int32, p.shape, 1)
                    p = jnp.where(col <= row, p, 0.0)
                c = 256 * hh + 128 * r
                acc[pl.ds(q_at, block), c : c + 128] += mm(p.astype(BF16), vx[r])
    if last:
        rows = acc.shape[0]
        lane = lax.broadcasted_iota(jnp.int32, (8, 128), 1)
        sub = lax.broadcasted_iota(jnp.int32, (8, 128), 0)
        total = jnp.zeros((8, rows), F32)
        for hh in range(2):
            out = []
            for r in range(2):
                a = acc[:, 256 * hh + 128 * r : 256 * hh + 128 * r + 128]
                out.append(a / pltpu.roll(a, HD, 1))
                pick = jnp.where((lane == (HD if r == 0 else 0)) & (sub == 2 * hh + r), 1.0, 0.0)
                total += lax.dot_general(
                    pick, a, NT, precision=lax.Precision.HIGHEST, preferred_element_type=F32
                )
            mix = jnp.where(half((rows, 128), 0), out[0], out[1])
            mix_ref[:, 128 * hh : 128 * hh + 128] = mix
            mixb_ref[:, 128 * hh : 128 * hh + 128] = mix.astype(BF16)
        lse_ref[0] = jnp.log2(jnp.where(sub[:, 0:1] < 4, total, 1.0))


def attend(meta, q, kv, acc, own, last, block):
    rows = q.shape[0]
    pairs = kv.shape[1] // 256
    first = acc is None
    args = [meta, q, kv]
    wide = pl.BlockSpec((rows, 512), lambda g, m: (0, g))
    slim = pl.BlockSpec((rows, 256), lambda g, m: (0, g))
    in_specs = [slim, slim]
    if not first:
        in_specs.append(wide)
        args.append(acc)
    if last:
        out_shape = (
            jax.ShapeDtypeStruct((rows, pairs * 256), BF16),
            jax.ShapeDtypeStruct((rows, pairs * 256), F32),
            jax.ShapeDtypeStruct((pairs, 8, rows), F32),
        )
        out_specs = (slim, slim, pl.BlockSpec((1, 8, rows), lambda g, m: (g, 0, 0)))
        scratch = [pltpu.VMEM((rows, 512), F32)]
    else:
        out_shape = jax.ShapeDtypeStruct((rows, pairs * 512), F32)
        out_specs = wide
        scratch = []
    work = 2 * block * block * pairs * 4
    return pl.pallas_call(
        functools.partial(attend_body, own, first, last, block),
        out_shape=out_shape,
        grid_spec=pltpu.PrefetchScalarGridSpec(
            num_scalar_prefetch=1,
            grid=(pairs,),
            in_specs=in_specs,
            out_specs=out_specs,
            scratch_shapes=scratch,
        ),
        compiler_params=pltpu.CompilerParams(vmem_limit_bytes=40 << 20),
        cost_estimate=pl.CostEstimate(
            flops=work * 1024, bytes_accessed=12 << 20, transcendentals=work
        ),
        name="attend",
    )(*args)


def attend_back_body(own, first, block, meta, q_ref, do_ref, kv_ref, lse_ref, dlt_ref, *rest):
    rest = list(rest)
    given = None if first else rest.pop(0)
    dq, dkv_ref, dka, dva = rest
    dq[...] = jnp.zeros_like(dq) if first else given[...]
    dka[...] = jnp.zeros_like(dka)
    dva[...] = jnp.zeros_like(dva)
    for q_at, k_at, diagonal in pieces(own, meta, block):
        kt = kv_ref[pl.ds(k_at, block), 0:128]
        vt = kv_ref[pl.ds(k_at, block), 128:256]
        zero = jnp.zeros((block, HD), BF16)
        for hh in range(2):
            kh = kt[:, HD * hh : HD * hh + HD]
            vh = vt[:, HD * hh : HD * hh + HD]
            kx = (jnp.concatenate([kh, zero], axis=1), jnp.concatenate([zero, kh], axis=1))
            vx = (jnp.concatenate([vh, zero], axis=1), jnp.concatenate([zero, vh], axis=1))
            c = 128 * hh
            qt = q_ref[pl.ds(q_at, block), c : c + 128]
            dt = do_ref[pl.ds(q_at, block), c : c + 128]
            dvs, dks, dqs = [], [], None
            for r in range(2):
                row = 2 * hh + r
                lse = lse_ref[0, row : row + 1, pl.ds(q_at, block)]
                dlt = dlt_ref[0, row : row + 1, pl.ds(q_at, block)]
                p = jnp.exp2(mm(kx[r], qt, NT) * SCALE2 - lse)
                if diagonal:
                    key = lax.broadcasted_iota(jnp.int32, p.shape, 0)
                    query = lax.broadcasted_iota(jnp.int32, p.shape, 1)
                    p = jnp.where(key <= query, p, 0.0)
                ds = (p * (mm(vx[r], dt, NT) - dlt)).astype(BF16)
                dvs.append(mm(p.astype(BF16), dt))
                dks.append(mm(ds, qt))
                term = mm(ds, kx[r], TN)
                dqs = term if dqs is None else dqs + term
            left = half((block, 128), 0)
            dva[pl.ds(k_at, block), c : c + 128] += jnp.where(left, dvs[0], dvs[1])
            dka[pl.ds(k_at, block), c : c + 128] += jnp.where(left, dks[0], dks[1])
            dq[pl.ds(q_at, block), c : c + 128] += dqs
    for at, ref, scale in ((0, dka, 0.125), (128, dva, 1.0)):
        a = ref[...]
        a = jnp.concatenate([a[:, 0:64] + a[:, 64:128], a[:, 128:192] + a[:, 192:256]], axis=1)
        dkv_ref[:, at : at + 128] = (a * scale).astype(dkv_ref.dtype)


def attend_back(meta, q, do, kv, lse, dlt, dq, own, block):
    rows = q.shape[0]
    pairs = kv.shape[1] // 256
    first = dq is None
    slim = pl.BlockSpec((rows, 256), lambda g, m: (0, g))
    line = pl.BlockSpec((1, 8, rows), lambda g, m: (g, 0, 0))
    in_specs = [slim, slim, slim, line, line]
    args = [meta, q, do, kv, lse, dlt]
    if not first:
        in_specs.append(slim)
        args.append(dq)
    work = 2 * block * block * pairs * 4
    return pl.pallas_call(
        functools.partial(attend_back_body, own, first, block),
        out_shape=(
            jax.ShapeDtypeStruct((rows, pairs * 256), F32),
            jax.ShapeDtypeStruct((rows, pairs * 256), F32 if own else BF16),
        ),
        grid_spec=pltpu.PrefetchScalarGridSpec(
            num_scalar_prefetch=1,
            grid=(pairs,),
            in_specs=in_specs,
            out_specs=(slim, slim),
            scratch_shapes=[pltpu.VMEM((rows, 256), F32), pltpu.VMEM((rows, 256), F32)],
        ),
        compiler_params=pltpu.CompilerParams(vmem_limit_bytes=40 << 20),
        cost_estimate=pl.CostEstimate(
            flops=work * 2048, bytes_accessed=12 << 20, transcendentals=work
        ),
        name="attend_back",
    )(*args)


def head_mean(u):
    a = lax.broadcasted_iota(jnp.int32, (128, 128), 0) // HD
    b = lax.broadcasted_iota(jnp.int32, (128, 128), 1) // HD
    ones = jnp.where(a == b, 1.0, 0.0).astype(BF16)
    high = u.astype(BF16)
    low = (u - high.astype(F32)).astype(BF16)
    return (mm(high, ones) + mm(low, ones)) * (1.0 / HD)


def turn(u):
    lane = lax.broadcasted_iota(jnp.int32, u.shape, 1)
    return jnp.where(lane % HD < HD // 2, pltpu.roll(u, 96, 1), pltpu.roll(u, 32, 1))


def rope_body(q_ref, k_ref, v_ref, cos_ref, sin_ref, gain_ref, qo_ref, kv_ref):
    cos, sin = cos_ref[...], sin_ref[...]

    def one(u, gain):
        n = u * lax.rsqrt(head_mean(u * u) + EPSILON) * gain
        return (n * cos + turn(n) * sin).astype(BF16)

    for t in range(q_ref.shape[1] // 128):
        qo_ref[:, 128 * t : 128 * t + 128] = one(q_ref[:, 128 * t : 128 * t + 128], gain_ref[0:1])
    for t in range(k_ref.shape[1] // 128):
        kv_ref[:, 256 * t : 256 * t + 128] = one(k_ref[:, 128 * t : 128 * t + 128], gain_ref[1:2])
        kv_ref[:, 256 * t + 128 : 256 * t + 256] = v_ref[:, 128 * t : 128 * t + 128]


def rope(q_raw, k_raw, v, cos, sin, gains, step):
    rows, qw = q_raw.shape
    kw = k_raw.shape[1]
    spec = lambda w: pl.BlockSpec((step, w), lambda i: (i, 0))
    return pl.pallas_call(
        rope_body,
        out_shape=(
            jax.ShapeDtypeStruct((rows, qw), BF16),
            jax.ShapeDtypeStruct((rows, 2 * kw), BF16),
        ),
        grid=(rows // step,),
        in_specs=[spec(qw), spec(kw), spec(kw), spec(128), spec(128)]
        + [pl.BlockSpec((8, 128), lambda i: (0, 0))],
        out_specs=(spec(qw), spec(2 * kw)),
        cost_estimate=pl.CostEstimate(
            flops=rows * qw * 800, bytes_accessed=rows * qw * 12, transcendentals=rows * qw
        ),
        name="rope",
    )(q_raw, k_raw, v, cos, sin, gains)


def rope_back_body(terms, dq_ref, q_ref, k_ref, cos_ref, sin_ref, gain_ref, *rest):
    dkv_refs, (out_ref, gg_ref) = rest[:terms], rest[terms:]
    cos, sin = cos_ref[...], sin_ref[...]

    @pl.when(pl.program_id(0) == 0)
    def _():
        gg_ref[...] = jnp.zeros_like(gg_ref)

    def one(d, u, row):
        gain = gain_ref[row : row + 1]
        dn = d * cos + turn(d * sin)
        r = lax.rsqrt(head_mean(u * u) + EPSILON)
        gd = gain * dn
        gg_ref[row : row + 1] += jnp.sum(dn * u * r, axis=0, keepdims=True)
        return (r * gd - u * (r * r * r) * head_mean(u * gd)).astype(BF16)

    qw, kw = q_ref.shape[1], k_ref.shape[1]
    for t in range(qw // 128):
        c = slice(128 * t, 128 * t + 128)
        out_ref[:, c] = one(dq_ref[:, c] * 0.125, q_ref[:, c], 0)
    for t in range(kw // 128):
        dk = sum(ref[:, 256 * t : 256 * t + 128].astype(F32) for ref in dkv_refs)
        dv = sum(ref[:, 256 * t + 128 : 256 * t + 256].astype(F32) for ref in dkv_refs)
        out_ref[:, qw + 128 * t : qw + 128 * t + 128] = one(dk, k_ref[:, 128 * t : 128 * t + 128], 1)
        out_ref[:, qw + kw + 128 * t : qw + kw + 128 * t + 128] = dv.astype(BF16)


def rope_back(dq, q_raw, k_raw, cos, sin, gains, dkvs, step):
    rows, qw = q_raw.shape
    kw = k_raw.shape[1]
    spec = lambda w: pl.BlockSpec((step, w), lambda i: (i, 0))
    fixed = pl.BlockSpec((8, 128), lambda i: (0, 0))
    return pl.pallas_call(
        functools.partial(rope_back_body, len(dkvs)),
        out_shape=(
            jax.ShapeDtypeStruct((rows, qw + 2 * kw), BF16),
            jax.ShapeDtypeStruct((8, 128), F32),
        ),
        grid=(rows // step,),
        in_specs=[spec(qw), spec(qw), spec(kw), spec(128), spec(128), fixed]
        + [spec(2 * kw)] * len(dkvs),
        out_specs=(spec(qw + 2 * kw), fixed),
        cost_estimate=pl.CostEstimate(
            flops=rows * qw * 1600, bytes_accessed=rows * qw * 20, transcendentals=rows * qw
        ),
        name="rope_back",
    )(dq, q_raw, k_raw, cos, sin, gains, *dkvs)


def delta_body(do_ref, mix_ref, out_ref):
    lane = lax.broadcasted_iota(jnp.int32, (8, 128), 1) // HD
    sub = lax.broadcasted_iota(jnp.int32, (8, 128), 0)
    total = jnp.zeros(out_ref.shape[1:], F32)
    for hh in range(2):
        x = do_ref[:, 128 * hh : 128 * hh + 128].astype(F32) * mix_ref[:, 128 * hh : 128 * hh + 128]
        pick = jnp.where(sub == 2 * hh + lane, 1.0, 0.0)
        total += lax.dot_general(
            pick, x, NT, precision=lax.Precision.HIGHEST, preferred_element_type=F32
        )
    out_ref[0] = total


def delta_rows(do, mix):
    rows, width = do.shape
    pairs = width // 256
    slim = pl.BlockSpec((rows, 256), lambda g: (0, g))
    return pl.pallas_call(
        delta_body,
        out_shape=jax.ShapeDtypeStruct((pairs, 8, rows), F32),
        grid=(pairs,),
        in_specs=[slim, slim],
        out_specs=pl.BlockSpec((1, 8, rows), lambda g: (g, 0, 0)),
        cost_estimate=pl.CostEstimate(
            flops=rows * width * 96, bytes_accessed=rows * width * 6, transcendentals=0
        ),
        name="delta",
    )(do, mix)


def middle_body(step, n_ref, dy_ref, wg_ref, wu_ref, wd_ref, h_ref, dg_ref, du_ref):
    for at in range(0, n_ref.shape[0], step):
        rows = pl.ds(at, step)
        n = n_ref[rows, :]
        g = mm(n, wg_ref[...])
        u = mm(n, wu_ref[...])
        dh = mm(dy_ref[rows, :], wd_ref[...], NT)
        s = 1.0 / (1.0 + jnp.exp2(g * (-LOG2E)))
        act = g * s
        h_ref[rows, :] = (act * u).astype(BF16)
        du_ref[rows, :] = (dh * act).astype(BF16)
        dg_ref[rows, :] = (dh * u * s * (1.0 + g * (1.0 - s))).astype(BF16)


def middle(n, dy, wg, wu, wd):
    rows, width = n.shape
    hidden = wg.shape[1]
    tile = 256
    whole = pl.BlockSpec((rows, width), lambda j: (0, 0))
    cols = pl.BlockSpec((width, tile), lambda j: (0, j))
    outs = pl.BlockSpec((rows, tile), lambda j: (0, j))
    shape = jax.ShapeDtypeStruct((rows, hidden), BF16)
    return pl.pallas_call(
        functools.partial(middle_body, min(rows, 256)),
        out_shape=(shape, shape, shape),
        grid=(hidden // tile,),
        in_specs=[whole, whole, cols, cols, pl.BlockSpec((tile, width), lambda j: (j, 0))],
        out_specs=(outs, outs, outs),
        compiler_params=pltpu.CompilerParams(vmem_limit_bytes=40 << 20),
        cost_estimate=pl.CostEstimate(
            flops=6 * rows * width * hidden,
            bytes_accessed=6 * (rows * hidden + width * hidden),
            transcendentals=rows * hidden,
        ),
        name="middle",
    )(n, dy, wg, wu, wd)


def swap(x):
    n = lax.axis_size("tp")
    return lax.ppermute(x, "tp", [(i, i ^ 1) for i in range(n)])


def core_swap(x):
    n = lax.axis_size("fsdp")
    return lax.ppermute(x, "fsdp", [(i, i ^ 1) for i in range(n)])


def y_shift(x, s):
    n = lax.axis_size("fsdp")
    return lax.ppermute(x, "fsdp", [(i, (i + 2 * s) % n) for i in range(n)])


def gather_rows(x):
    n = lax.axis_size("fsdp")
    me = lax.axis_index("fsdp")
    y, c, ny = me // 2, me % 2, n // 2
    mine = jnp.zeros((ny,) + x.shape, x.dtype)
    mine = lax.dynamic_update_index_in_dim(mine, x, y, 0)
    for s in range(1, ny):
        mine = lax.dynamic_update_index_in_dim(mine, y_shift(x, s), (y - s) % ny, 0)
    other = core_swap(mine)
    lower = jnp.where(c == 0, mine, other)
    upper = jnp.where(c == 0, other, mine)
    return jnp.stack([lower, upper], axis=1).reshape((n * x.shape[0],) + x.shape[1:])


def scatter_rows(g):
    n = lax.axis_size("fsdp")
    me = lax.axis_index("fsdp")
    y, c, ny = me // 2, me % 2, n // 2
    parts = g.reshape((ny, 2, g.shape[0] // n) + g.shape[1:])
    keep = lax.dynamic_index_in_dim(parts, c, 1, keepdims=False)
    give = lax.dynamic_index_in_dim(parts, 1 - c, 1, keepdims=False)
    both = (keep.astype(F32) + core_swap(give).astype(F32)).astype(BF16)
    total = lax.dynamic_index_in_dim(both, y, 0, keepdims=False).astype(F32)
    for s in range(1, ny):
        send = lax.dynamic_index_in_dim(both, (y + s) % ny, 0, keepdims=False)
        total = total + y_shift(send, s).astype(F32)
    return total


def nearest(m, i, n):
    left, right = i, n - 1 - i
    near = min(left, right)
    if m == 0:
        return 0
    if m <= 2 * near:
        return (m + 1) // 2 if m % 2 else -(m // 2)
    return m - near if right > left else -(m - near)


def pick(index, choices):
    keys = list(choices)
    value = keys[0][1]
    for name, array in keys[1:]:
        here = functools.reduce(jnp.logical_or, [index == i for i in choices[(name, array)]])
        value = jnp.where(here, array, value)
    return value


def choose(index, table):
    value = table[0][0]
    for array, positions in table[1:]:
        here = functools.reduce(jnp.logical_or, [index == i for i in positions])
        value = jnp.where(here, array, value)
    return value


def line_shards(x, n):
    out = {0: x}
    for t in range(1, n):
        out[-t] = lax.ppermute(out[-(t - 1)], "ctx", [(i, i + 1) for i in range(t - 1, n - 1)])
        out[t] = lax.ppermute(out[t - 1], "ctx", [(i, i - 1) for i in range(1, n - t + 1)])
    return out


def tables(x, index, n):
    lane = jnp.arange(128)
    exponent = -((lane % (HD // 2)).astype(F32) * 2.0) / HD
    angle = x.astype(F32)[:, None] * (ROPE_BASE**exponent)[None, :]
    sign = jnp.where(lane % HD < HD // 2, -1.0, 1.0).astype(F32)
    return jnp.cos(angle), jnp.sin(angle) * sign[None, :]


def norm_rows(x, gain):
    r = lax.rsqrt(jnp.mean(x * x, axis=-1, keepdims=True) + EPSILON)
    return x * r * gain, r


def norm_back(x, r, gain, d):
    scaled = d * gain
    dx = r * scaled - x * (r * r * r) * jnp.mean(x * scaled, axis=-1, keepdims=True)
    return dx, d * x * r


def per_device(
    tokens, cotangent, block_order, positions,
    attn_gain, w_query, key_weight, value_weight, query_gain, key_gain,
    w_out, ffn_gain, w_gate, w_up, w_down,
):
    n_ctx = lax.axis_size("ctx")
    n_fsdp = lax.axis_size("fsdp")
    me = lax.axis_index("ctx")
    seqs, rows, width = tokens.shape
    x = tokens.reshape(seqs * rows, width)
    dy = cotangent.reshape(seqs * rows, width)
    block = rows // 2
    qw, kw = w_query.shape[1], key_weight.shape[1]
    gs, hs = attn_gain.shape[0], query_gain.shape[0]

    w_qkv = gather_rows(jnp.concatenate([w_query, key_weight, value_weight], axis=1))
    small = jnp.concatenate([attn_gain, ffn_gain, query_gain, key_gain])
    small = lax.all_gather(small, "fsdp", axis=0, tiled=False).astype(F32)
    gain_attn = small[:, :gs].reshape(-1)
    gain_ffn = small[:, gs : 2 * gs].reshape(-1)
    gain_q = small[:, 2 * gs : 2 * gs + hs].reshape(-1)
    gain_k = small[:, 2 * gs + hs :].reshape(-1)
    gains = jnp.stack([jnp.tile(gain_q, 2), jnp.tile(gain_k, 2)] + [jnp.zeros(128, F32)] * 6)
    w_out2 = jnp.concatenate([w_out, swap(w_out)], axis=0)
    w_out2, w_gate, w_up, w_down, w_qkv = lax.optimization_barrier(
        (w_out2, w_gate, w_up, w_down, w_qkv)
    )
    out_full = lax.all_gather(w_out2, "fsdp", axis=1, tiled=True)
    down_full = lax.all_gather(w_down, "fsdp", axis=1, tiled=True)
    gate_full = lax.all_gather(w_gate, "fsdp", axis=0, tiled=True)
    up_full = lax.all_gather(w_up, "fsdp", axis=0, tiled=True)

    xf = x.astype(F32)
    normed, inv_one = norm_rows(xf, gain_attn)
    normed_b = normed.astype(BF16)
    cos, sin = tables(positions.reshape(-1), me, n_ctx)
    k_raw = mm(normed_b, w_qkv[:, qw : qw + kw])
    v_b = mm(normed_b, w_qkv[:, qw + kw :]).astype(BF16)
    q_raw = mm(normed_b, w_qkv[:, :qw])
    q_b, kv_b = rope(q_raw, k_raw, v_b, cos, sin, gains, min(256, block))

    shards = line_shards(kv_b, n_ctx)
    first_of = block_order[0::2]
    second_of = block_order[1::2]
    low_at = jnp.where(first_of < second_of, 0, block).astype(jnp.int32)
    low_id = jnp.minimum(first_of, second_of)
    q_low, q_id = low_at[me], low_id[me]
    kvs, metas = [], []
    for m in range(n_ctx):
        table = {}
        for i in range(n_ctx):
            table.setdefault(nearest(m, i, n_ctx), []).append(i)
        kvs.append(choose(me, [(shards[d], where) for d, where in table.items()]))
        far = jnp.array([i + nearest(m, i, n_ctx) for i in range(n_ctx)], jnp.int32)[me]
        if m == 0:
            metas.append(jnp.stack([q_low, block - q_low, q_low, q_low]))
        else:
            k_low = low_at[far]
            before = low_id[far] < q_id
            metas.append(
                jnp.stack(
                    [
                        jnp.where(before, q_low, block - q_low),
                        k_low,
                        block - q_low,
                        jnp.where(before, k_low, block - k_low),
                    ]
                )
            )
    acc = None
    for m in range(n_ctx):
        acc = attend(metas[m], q_b, kvs[m], acc, m == 0, m == n_ctx - 1, block)
    mixed_b, mix, lse = acc

    half_in = mixed_b.shape[1]
    attn_out = mm(mixed_b, out_full[:half_in]) + mm(swap(mixed_b), out_full[half_in:])
    resid = xf + attn_out
    normed_two, inv_two = norm_rows(resid, gain_ffn)
    two_b = normed_two.astype(BF16)

    hidden, dgate, dup = middle(two_b, dy, gate_full, up_full, down_full)
    d_two_part = (mm(dgate, gate_full, NT) + mm(dup, up_full, NT)).astype(BF16)
    d_two_other = swap(d_two_part)
    gate_g = mm(two_b, dgate, TN).astype(BF16)
    up_g = mm(two_b, dup, TN).astype(BF16)
    down_g = mm(dy, hidden, TN).astype(BF16)
    down_part = mm(hidden, down_full).astype(BF16)
    gate_g, up_g, down_g, down_part, d_two_other = lax.optimization_barrier(
        (gate_g, up_g, down_g, down_part, d_two_other)
    )
    output = (resid + (down_part.astype(F32) + swap(down_part).astype(F32))).astype(BF16)
    d_two = d_two_part.astype(F32) + d_two_other.astype(F32)
    d_norm, ffn_term = norm_back(resid, inv_two, gain_ffn, d_two)
    ffn_gain_g = jnp.sum(ffn_term, axis=0)
    d_resid = dy.astype(F32) + d_norm
    d_resid_b = d_resid.astype(BF16)

    do = mm(d_resid_b, out_full[:half_in], NT).astype(BF16)
    dlt = delta_rows(do, mix)
    grads = [None] * n_ctx
    dq = None
    for m in reversed(range(n_ctx)):
        dq, grads[m] = attend_back(metas[m], q_b, do, kvs[m], lse, dlt, dq, m == 0, block)
    home = [grads[0]]
    for side in (1, -1):
        got = None
        for t in range(n_ctx - 1):
            away = n_ctx - 1 - t
            table = {}
            for i in range(n_ctx):
                for m in range(1, n_ctx):
                    if nearest(m, i, n_ctx) == side * away:
                        table.setdefault(m, []).append(i)
            send = choose(me, [(grads[m], where) for m, where in table.items()])
            if got is not None:
                send = (send.astype(F32) + got.astype(F32)).astype(BF16)
            senders = sorted(i for where in table.values() for i in where)
            got = lax.ppermute(send, "ctx", [(i, i + side) for i in senders])
        if got is not None:
            home.append(got)
    out_g = mm(d_resid_b, mixed_b, TN).astype(BF16)

    d_qkv, head_gain = rope_back(dq, q_raw, k_raw, cos, sin, gains, home, min(256, block))
    normed_part = mm(d_qkv, w_qkv, NT).astype(BF16)
    normed_other = swap(normed_part)
    qkv_g = mm(normed_b, d_qkv, TN).astype(BF16)
    head_gain = head_gain[:2, :HD] + head_gain[:2, HD:]
    head_gain = lax.psum(head_gain, "tp")
    d_normed = normed_part.astype(F32) + normed_other.astype(F32)
    d_input, attn_term = norm_back(xf, inv_one, gain_attn, d_normed)
    input_grad = d_resid + d_input
    attn_gain_g = jnp.sum(attn_term, axis=0)

    def total(g):
        return lax.psum(scatter_rows(g).astype(BF16), "ctx").astype(F32)

    down_s, gate_s, up_s = total(down_g), total(gate_g), total(up_g)
    out_s, qkv_s = total(out_g), total(qkv_g)
    small_g = jnp.concatenate(
        [
            attn_gain_g.reshape(n_fsdp, gs),
            ffn_gain_g.reshape(n_fsdp, gs),
            head_gain[0].reshape(n_fsdp, hs),
            head_gain[1].reshape(n_fsdp, hs),
        ],
        axis=1,
    )
    small_g = lax.psum(small_g, ("fsdp", "ctx"))
    small_g = lax.dynamic_index_in_dim(small_g, lax.axis_index("fsdp"), 0, keepdims=False)
    return (
        output.reshape(tokens.shape),
        input_grad.reshape(tokens.shape),
        small_g[:gs],
        qkv_s[:, :qw],
        qkv_s[:, qw : qw + kw],
        qkv_s[:, qw + kw :],
        small_g[2 * gs : 2 * gs + hs],
        small_g[2 * gs + hs :],
        out_s.T,
        small_g[gs : 2 * gs],
        gate_s,
        up_s,
        down_s.T,
    )


def solution(mesh):
    rows = P("fsdp", "ctx", None)
    ins = P("fsdp", "tp")
    outs = P("tp", "fsdp")
    one = P("fsdp")
    return jax.shard_map(
        per_device,
        mesh=mesh,
        in_specs=(
            rows, rows, P(), P("fsdp", "ctx"), one, ins, ins, ins, one, one, outs, one, ins, ins, outs,
        ),
        out_specs=(rows, rows, one, ins, ins, ins, one, one, outs, one, ins, ins, outs),
        check_vma=False,
    )
```

time: 1640 us -> 737 us (0.45)
  waiting for transfers between devices: 795 us -> 210 us
  matrix products: 493 us -> 67 us
  Pallas kernels: 0 us -> 133 us
  other arithmetic: 143 us -> 58.4 us
  blocking collectives: 58.6 us -> 118 us
  local copies, waits for them, and re-layouts: 114 us -> 64.8 us
  starting transfers between devices: 0.99 us -> 47.1 us
    dot_general x77 -> x15, matrix products: 493 us -> 67 us  [mm(): return lax.dot_general(a, b, dims, preferred_element_type=F32)]
    psum x4 -> x1, waiting for transfers between devices: 355 us -> 35.4 us  [total(): return lax.psum(scatter_rows(g).astype(BF16), 'ctx').astype(F32)]
    reduce_scatter x9 -> x0, waiting for transfers between devices: 280 us -> none  [the longest x1 50.4 us: per_device(): lax.psum_scatter(up_w_grad.astype(jnp.bfloat16), 'fsdp', scatter_dimensio...]
    ppermute x0 -> x29, waiting for transfers between devices: none -> 173 us  [the longest x5 71.1 us: swap(): return lax.ppermute(x, 'tp', [(i, i ^ 1) for i in range(n)])]
    all_gather x7 -> x4, waiting for transfers between devices: 156 us -> 0.01 us  [the longest x1 0.01 us: per_device(): out_full = lax.all_gather(w_out2, 'fsdp', axis=1, tiled=True)]
    pallas_call x0 -> x12, Pallas kernels: none -> 133 us  [the longest x4 63.3 us: attend_back(): pl.pallas_call(functools.partial(attend_back_body, own, first, block), ou...]
    psum x2, blocking collectives: 17 us -> 111 us  [the longest x1 65.8 us: per_device(): small_g = lax.psum(small_g, ('fsdp', 'ctx'))]
    reduce_sum x21 -> x3, other arithmetic: 87.2 us -> 5.92 us  [the longest x1 3.93 us: per_device(): attn_gain_g = jnp.sum(attn_term, axis=0)]
  transfers between devices with their start and end apart: 20 -> 34, of which waited for: 17 -> 12; matrix products, arithmetic and copies ran while one was open for 20% -> 17% of each run, Pallas kernels for 0% -> 15%
where the time goes in v1:
time: 737 us; the launch traced here: 730 us
  waiting for transfers between devices  210 us (28%)
  Pallas kernels  133 us (18%)
  blocking collectives  118 us (16%)
  matrix products  67 us (9%)
  local copies, waits for them, and re-layouts  64.8 us (9%)
  other arithmetic  58.4 us (8%)
  starting transfers between devices  47.1 us (6%)
  between operations  32.3 us (4%)
    ppermute x5, waiting for transfers between devices, swap(): return lax.ppermute(x, 'tp', [(i, i ^ 1) for i in range(n)])  71.1 us
    dot_general x15, matrix products, mm(): return lax.dot_general(a, b, dims, preferred_element_type=F32)  67 us
    psum x1, blocking collectives, per_device(): small_g = lax.psum(small_g, ('fsdp', 'ctx'))  65.8 us
    pallas_call x4, Pallas kernels, attend_back(): pl.pallas_call(functools.partial(attend_back_body, own, first, block), ou...  63.3 us
    psum x1, blocking collectives, per_device(): head_gain = lax.psum(head_gain, 'tp')  45.4 us
    ppermute x6, waiting for transfers between devices, y_shift(): return lax.ppermute(x, 'fsdp', [(i, (i + 2 * s) % n) for i in range(n)])  42.5 us
    ppermute x3, waiting for transfers between devices, line_shards(): lax.ppermute(out[t - 1], 'ctx', [(i, i - 1) for i in range(1, n - t + 1)])  42.3 us
    psum x1, waiting for transfers between devices, total(): return lax.psum(scatter_rows(g).astype(BF16), 'ctx').astype(F32)  35.4 us
  transfers between devices with their start and end apart: 34, of which 12 were waited for; matrix products, arithmetic and copies ran while one was open for 17% of the time, Pallas kernels for 15%

profile of v1, /device:TPU:0, one launch (start us, length us, event | category | flops | bytes accessed | tf_op | source)
XLA Modules:
  0.0 729.9 jit_solution(10871562051986841445)
XLA Ops:
  13.3 11.7 %collective-permute-done.1 = bf16[256,1024]{1,0:T(8,128)(2,1)S(1)} collective-permute-done((bf16[256,1024]{1,0:T(8,128)(2,1)S(1)}, bf16[256,1024]{1,0:T(8,128)(2,1)S(1)}, u32[]{:S(2)}, u32[]{:S(2)}) %collective-permute-start.1) | collective-permute-done | bytes 524320 | tf_op jit(solution)/shard_map/ppermute | solution.py:381
  69.4 20.1 %collective-permute-done.6 = bf16[1024,512]{1,0:T(8,128)(2,1)S(1)} collective-permute-done((bf16[1024,512]{1,0:T(8,128)(2,1)}, bf16[1024,512]{1,0:T(8,128)(2,1)S(1)}, u32[]{:S(2)}, u32[]{:S(2)}) %collective-permute-start.6) | collective-permute-done | bytes 1048608 | tf_op jit(solution)/shard_map/ppermute | solution.py:444
  92.5 22.2 %collective-permute-done.7 = bf16[1024,512]{1,0:T(8,128)(2,1)S(1)} collective-permute-done((bf16[1024,512]{1,0:T(8,128)(2,1)S(1)}, bf16[1024,512]{1,0:T(8,128)(2,1)S(1)}, u32[]{:S(2)}, u32[]{:S(2)}) %collective-permute-start.7) | collective-permute-done | bytes 1048608 | tf_op jit(solution)/shard_map/ppermute | solution.py:444
  142.4 8.5 %attend.4.rest_0_ = f32[1024,1024]{1,0:T(8,128)S(1)} custom-call(s32[4]{0:T(128)S(1)} %get-tuple-element.128.meta, bf16[1024,512]{1,0:T(8,128)(2,1)S(1)} %copy-done.14, bf16[1024,512]{1,0:T(8,128)(2,1)S(1)} %copy-done.17), custom_call_target="tpu_custom_call" | custom-call | flops 4294967296 | bytes 12582912 | tf_op jit(solution)/shard_map/attend/pallas_call | solution.py:108
  165.9 10.5 %attend.7 = (bf16[1024,512]{1,0:T(8,128)(2,1)S(1)}, f32[1024,512]{1,0:T(8,128)S(1)}, f32[2,8,1024]{2,1,0:T(8,128)S(1)}) custom-call(s32[4]{0:T(128)S(1)} %get-tuple-element.125.meta, bf16[1024,512]{1,0:T(8,128)(2,1)S(1)} %copy-done.14, bf16[1024,512]{1,0:T(8,128)(2,1)S(1)} %get-tuple-element.87.kv_ref, f32[1024,1024]{1,0:T(8,128)S(1)} %attend.6.rest_0_), custom_call_target="tpu_custom_call" | custom-call | flops 4294967296 | bytes 12582912 | tf_op jit(solution)/shard_map/attend/pallas_call | solution.py:108
  179.6 21.2 %collective-permute-done.9 = bf16[1024,512]{1,0:T(8,128)(2,1)S(1)} collective-permute-done((bf16[1024,512]{1,0:T(8,128)(2,1)S(1)}, bf16[1024,512]{1,0:T(8,128)(2,1)S(1)}, u32[]{:S(2)}, u32[]{:S(2)}) %collective-permute-start.9) | collective-permute-done | bytes 1048608 | tf_op jit(solution)/shard_map/ppermute | solution.py:371
  210.4 19.9 %middle.1 = (bf16[1024,2304]{1,0:T(8,128)(2,1)S(1)}, bf16[1024,2304]{1,0:T(8,128)(2,1)S(1)}, bf16[1024,2304]{1,0:T(8,128)(2,1)}) custom-call(bf16[1024,1024]{1,0:T(8,128)(2,1)S(1)} %copy-done.4, bf16[1024,1024]{1,0:T(8,128)(2,1)S(1)} %bitcast.149, bf16[1024,2304]{1,0:T(8,128)(2,1)} %all-gather.8.cloned.1.call-done.wg_ref, ...), custom_call_target="tpu_custom_call" | custom-call | flops 14495514624 | bytes 28311552 | tf_op jit(solution)/shard_map/middle/pallas_call | solution.py:353
  230.3 7.9 %convolution_convert_fusion.1 = bf16[1024,2304]{1,0:T(8,128)(2,1)S(1)} fusion(bf16[1024,1024]{1,0:T(8,128)(2,1)S(1)} %copy-done.4, bf16[1024,2304]{1,0:T(8,128)(2,1)} %get-tuple-element.50), kind=kOutput, calls=%fused_computation.7 | convolution fusion | flops 4834197504 | bytes 11534336 | tf_op jit(solution)/shard_map/dot_general | solution.py:22
  250.5 9.1 %add_convert_fusion.1 = bf16[1024,1024]{1,0:T(8,128)(2,1)S(1)} fusion(f32[1024,1024]{1,0:T(8,128)} %fusion.53, bf16[1024,2304]{1,0:T(8,128)(2,1)} %get-tuple-element.50, bf16[1024,2304]{1,0:T(8,128)(2,1)} %all-gather.10.cloned.1.call-done.wu_ref), kind=kOutput, calls=%fused_computation.32 | convolution fusion | flops 4833935360 | bytes 15728640 | tf_op jit(solution)/shard_map/dot_general | solution.py:22
  274.5 30.8 %collective-permute-done.10 = bf16[1024,1024]{1,0:T(8,128)(2,1)S(1)} collective-permute-done((bf16[1024,1024]{1,0:T(8,128)(2,1)S(1)}, bf16[1024,1024]{1,0:T(8,128)(2,1)S(1)}, u32[]{:S(2)}, u32[]{:S(2)}) %collective-permute-start.10) | collective-permute-done | bytes 2097184 | tf_op jit(solution)/shard_map/ppermute | solution.py:371
  310.7 8.8 %reshape.171 = bf16[2,2,256,2304]{2,1,0,3:T(2,128)(2,1)} reshape(bf16[1024,2304]{0,1:T(8,128)(2,1)} %fusion) | data formatting | bytes 9437184 | tf_op jit(solution)/shard_map/reshape | solution.py:402
  319.5 12.4 %constant_dynamic-slice_fusion.2 = (bf16[2,1,256,2304]{2,1,0,3:T(2,128)(2,1)}, bf16[2,1,256,2304]{2,1,0,3:T(2,128)(2,1)S(1)}) fusion(bf16[2,2,256,2304]{2,1,0,3:T(2,128)(2,1)} %reshape.171, s32[]{:T(128)S(6)} %select_n.246, s32[]{:T(128)S(6)} %select_n.247), kind=kLoop, calls=%fused_computation.105 | loop fusion | bytes 9437192 | tf_op jit(solution)/shard_map/jit(dynamic_index_in_dim)/dynamic_slice | solution.py:403
  337.1 12.2 %collective-permute-done.11 = bf16[1024,1024]{1,0:T(8,128)(2,1)} collective-permute-done((bf16[1024,1024]{1,0:T(8,128)(2,1)}, bf16[1024,1024]{1,0:T(8,128)(2,1)}, u32[]{:S(2)}, u32[]{:S(2)}) %collective-permute-start.11) | collective-permute-done | bytes 2097184 | tf_op jit(solution)/shard_map/ppermute | solution.py:371
  365.6 14.9 %attend_back.4 = (f32[1024,512]{1,0:T(8,128)S(1)}, bf16[1024,512]{1,0:T(8,128)(2,1)}) custom-call(s32[4]{0:T(128)S(1)} %get-tuple-element.125.meta, bf16[1024,512]{1,0:T(8,128)(2,1)S(1)} %copy-done.15, bf16[1024,512]{1,0:T(8,128)(2,1)S(1)} %copy-done.11, bf16[1024,512]{1,0:T(8,128)(2,1)S(1)} %copy-done.8, f32[2,8,1024]{2,1,0:T(8,128)S(1)} %get-tuple-element.54.lse_ref, ...), custom_call_target="tpu_custom_call" | custom-call | flops 8589934592 | bytes 12582912 | tf_op jit(solution)/shard_map/attend_back/pallas_call | solution.py:182
  396.2 14.4 %attend_back.5 = (f32[1024,512]{1,0:T(8,128)S(1)}, bf16[1024,512]{1,0:T(8,128)(2,1)S(1)}) custom-call(s32[4]{0:T(128)S(1)} %get-tuple-element.126.meta, bf16[1024,512]{1,0:T(8,128)(2,1)S(1)} %copy-done.16, bf16[1024,512]{1,0:T(8,128)(2,1)S(1)} %copy-done.11, bf16[1024,512]{1,0:T(8,128)(2,1)S(1)} %copy-done.6, f32[2,8,1024]{2,1,0:T(8,128)S(1)} %get-tuple-element.54.lse_ref, ...), custom_call_target="tpu_custom_call" | custom-call | flops 8589934592 | bytes 12582912 | tf_op jit(solution)/shard_map/attend_back/pallas_call | solution.py:182
  410.7 14.1 %attend_back.6 = (f32[1024,512]{1,0:T(8,128)S(1)}, bf16[1024,512]{1,0:T(8,128)(2,1)S(1)}) custom-call(s32[4]{0:T(128)S(1)} %get-tuple-element.127.meta, bf16[1024,512]{1,0:T(8,128)(2,1)S(1)} %copy-done.16, bf16[1024,512]{1,0:T(8,128)(2,1)S(1)} %copy-done.11, bf16[1024,512]{1,0:T(8,128)(2,1)S(1)} %get-tuple-element.94.kv_ref, ...), custom_call_target="tpu_custom_call" | custom-call | flops 8589934592 | bytes 12582912 | tf_op jit(solution)/shard_map/attend_back/pallas_call | solution.py:182
  424.9 19.8 %attend_back.7 = (f32[1024,512]{1,0:T(8,128)S(1)}, f32[1024,512]{1,0:T(8,128)S(1)}) custom-call(s32[4]{0:T(128)S(1)} %get-tuple-element.128.meta, bf16[1024,512]{1,0:T(8,128)(2,1)S(1)} %copy-done.16, bf16[1024,512]{1,0:T(8,128)(2,1)S(1)} %copy-done.11, bf16[1024,512]{1,0:T(8,128)(2,1)S(1)} %copy-done.18, f32[2,8,1024]{2,1,0:T(8,128)S(1)} %get-tuple-element.54.lse_ref, ...), custom_call_target="tpu_custom_call" | custom-call | flops 8589934592 | bytes 12582912 | tf_op jit(solution)/shard_map/attend_back/pallas_call | solution.py:182
  461.7 17.0 %collective-permute-done.13 = bf16[1024,512]{1,0:T(8,128)(2,1)S(1)} collective-permute-done((bf16[1024,512]{1,0:T(8,128)(2,1)S(1)}, bf16[1024,512]{1,0:T(8,128)(2,1)S(1)}, u32[]{:S(2)}, u32[]{:S(2)}) %collective-permute-start.13) | collective-permute-done | bytes 1048608 | tf_op jit(solution)/shard_map/ppermute | solution.py:584
  490.6 18.0 %collective-permute-done.22 = bf16[256,512]{0,1:T(8,128)(2,1)S(1)} collective-permute-done((bf16[256,512]{0,1:T(8,128)(2,1)S(1)}, bf16[256,512]{0,1:T(8,128)(2,1)S(1)}, u32[]{:S(2)}, u32[]{:S(2)}) %collective-permute-start.22) | collective-permute-done | bytes 262176 | tf_op jit(solution)/shard_map/ppermute | solution.py:381
  512.5 8.0 %rope_back.1 = (bf16[1024,1024]{1,0:T(8,128)(2,1)}, f32[8,128]{1,0:T(8,128)}) custom-call(f32[1024,512]{1,0:T(8,128)} %copy-done.1, f32[1024,512]{1,0:T(8,128)} %fusion.28.q_ref, f32[1024,256]{1,0:T(8,128)} %fusion.35.k_ref, f32[1024,128]{1,0:T(8,128)} %get-tuple-element.106.cos_ref, f32[1024,128]{1,0:T(8,128)} %get-tuple-element.105.sin_ref, ...), custom_call_target="tpu_custom_call" | custom-call | flops 838860800 | bytes 10485760 | tf_op jit(solution)/shard_map/rope_back/pallas_call | solution.py:284
  539.6 7.0 collective-permute-done.20
  554.7 45.4 %psum.49 = f32[2,64]{1,0:T(2,128)S(1)} all-reduce(f32[2,64]{1,0:T(2,128)S(1)} %slice_add_fusion), channel_id=1, replica_groups=mesh['fsdp'=4,'ctx'=4,'tp'=2] {'tp'}, use_global_device_ids=true, to_apply=%region_6.7 | all-reduce | flops 128 | bytes 1024 | tf_op jit(solution)/shard_map/psum | solution.py:594
  604.3 65.8 %psum.50 = f32[4,544]{1,0:T(4,128)S(1)} all-reduce(f32[4,544]{1,0:T(4,128)S(1)} %pad_maximum_fusion.2), channel_id=1, replica_groups=mesh['fsdp'=4,'ctx'=4,'tp'=2] {'fsdp','ctx'}, use_global_device_ids=true, to_apply=%region_7.8 | all-reduce | flops 2176 | bytes 17408 | tf_op jit(solution)/shard_map/psum | solution.py:614
  677.0 35.4 %all-reduce.4.cloned.1.call-done = (bf16[256,1024]{1,0:T(8,128)(2,1)}, bf16[512,256]{1,0:T(8,128)(2,1)}, bf16[256,2304]{1,0:T(8,128)(2,1)}, bf16[256,2304]{1,0:T(8,128)(2,1)}, bf16[2304,256]{1,0:T(8,128)(2,1)}) async-done(((bf16[256,1024]{1,0:T(8,128)(2,1)}, bf16[512,256]{1,0:T(8,128)(2,1)}, bf16[256,2304]{1,0:T(8,128)(2,1)}, bf16[256,2304]{1,0:T(8,128)(2,1)}, bf16[2304,256]{1,0:T(8,128)(2,1)}), ...) | async-done | bytes 4325392 | tf_op jit(solution)/shard_map/psum | solution.py:601
  (334 shorter events, 242.3 us)
Async XLA Ops:
  7.2 172.4 %all-gather.6.cloned.1.call-start = ((), (), s32[]{:S(2)}) async-start(), calls=%async_computation | async-start | bytes 2621440 | tf_op jit(solution)/shard_map/all_gather | solution.py:494
  36.4 172.0 %all-gather.8.cloned.1.call-start = ((), (), s32[]{:S(2)}) async-start(), calls=%async_computation.1 | async-start | bytes 5898240 | tf_op jit(solution)/shard_map/all_gather | solution.py:496
  37.2 171.3 %all-gather.10.cloned.1.call-start = ((), (), s32[]{:S(2)}) async-start(), calls=%async_computation.2 | async-start | bytes 5898240 | tf_op jit(solution)/shard_map/all_gather | solution.py:497
  37.9 170.5 %all-gather.12.cloned.1.call-start = ((), (), s32[]{:S(2)}) async-start(), calls=%async_computation.3 | async-start | bytes 5898240 | tf_op jit(solution)/shard_map/all_gather | solution.py:495
  63.4 26.1 %collective-permute-start.6 = (bf16[1024,512]{1,0:T(8,128)(2,1)}, bf16[1024,512]{1,0:T(8,128)(2,1)S(1)}, u32[]{:S(2)}, u32[]{:S(2)}) collective-permute-start(bf16[1024,512]{1,0:T(8,128)(2,1)} %get-tuple-element.43.kv_ref), channel_id=1, source_target_pairs={{2,0},{4,2},{6,4},{3,1},{5,3},{7,5},{10,8},{12,10},{14,12},{11,9},... | collective-permute-start | bytes 3145736 | tf_op jit(solution)/shard_map/ppermute | solution.py:444
  64.7 26.1 %collective-permute-start.3 = (bf16[1024,512]{1,0:T(8,128)(2,1)}, bf16[1024,512]{1,0:T(8,128)(2,1)S(1)}, u32[]{:S(2)}, u32[]{:S(2)}) collective-permute-start(bf16[1024,512]{1,0:T(8,128)(2,1)} %get-tuple-element.43.kv_ref), channel_id=1, source_target_pairs={{0,2},{2,4},{4,6},{1,3},{3,5},{5,7},{8,10},{10,12},{12,14},{9,11},... | collective-permute-start | bytes 3145736 | tf_op jit(solution)/shard_map/ppermute | solution.py:443
  69.4 643.0 %all-reduce.4.cloned.1.call-start = ((), (), s32[]{:S(2)}) async-start(), calls=%async_computation.4 | async-start | bytes 8650752 | tf_op jit(solution)/shard_map/psum | solution.py:601
  89.5 25.1 %collective-permute-start.7 = (bf16[1024,512]{1,0:T(8,128)(2,1)S(1)}, bf16[1024,512]{1,0:T(8,128)(2,1)S(1)}, u32[]{:S(2)}, u32[]{:S(2)}) collective-permute-start(bf16[1024,512]{1,0:T(8,128)(2,1)S(1)} %collective-permute-done.6), channel_id=1, source_target_pairs={{2,0},{4,2},{3,1},{5,3},{10,8},{12,10},{11,9},{13,11},{18,16},{20,... | collective-permute-start | bytes 3145736 | tf_op jit(solution)/shard_map/ppermute | solution.py:444
  114.6 36.4 %collective-permute-start.8 = (bf16[1024,512]{1,0:T(8,128)(2,1)S(1)}, bf16[1024,512]{1,0:T(8,128)(2,1)}, u32[]{:S(2)}, u32[]{:S(2)}) collective-permute-start(bf16[1024,512]{1,0:T(8,128)(2,1)S(1)} %collective-permute-done.7), channel_id=1, source_target_pairs={{2,0},{3,1},{10,8},{11,9},{18,16},{19,17},{26,24},{27,25}} | collective-permute-start | bytes 3145736 | tf_op jit(solution)/shard_map/ppermute | solution.py:444
  115.9 35.1 %collective-permute-start.5 = (bf16[1024,512]{1,0:T(8,128)(2,1)}, bf16[1024,512]{1,0:T(8,128)(2,1)}, u32[]{:S(2)}, u32[]{:S(2)}) collective-permute-start(bf16[1024,512]{1,0:T(8,128)(2,1)} %collective-permute-done.4), channel_id=1, source_target_pairs={{4,6},{5,7},{12,14},{13,15},{20,22},{21,23},{28,30},{29,31}} | collective-permute-start | bytes 3145736 | tf_op jit(solution)/shard_map/ppermute | solution.py:443
  259.7 45.6 %collective-permute-start.10 = (bf16[1024,1024]{1,0:T(8,128)(2,1)S(1)}, bf16[1024,1024]{1,0:T(8,128)(2,1)S(1)}, u32[]{:S(2)}, u32[]{:S(2)}) collective-permute-start(bf16[1024,1024]{1,0:T(8,128)(2,1)S(1)} %add_convert_fusion.1), channel_id=1, source_target_pairs={{0,1},{1,0},{2,3},{3,2},{4,5},{5,4},{6,7},{7,6},{8,9},{9,8},{10,11... | collective-permute-start | bytes 6291464 | tf_op jit(solution)/shard_map/ppermute | solution.py:371
  305.3 44.0 %collective-permute-start.11 = (bf16[1024,1024]{1,0:T(8,128)(2,1)}, bf16[1024,1024]{1,0:T(8,128)(2,1)}, u32[]{:S(2)}, u32[]{:S(2)}) collective-permute-start(bf16[1024,1024]{1,0:T(8,128)(2,1)} %convolution_convert_fusion.5), channel_id=1, source_target_pairs={{0,1},{1,0},{2,3},{3,2},{4,5},{5,4},{6,7},{7,6},{8,9},{9,8},{10,11... | collective-permute-start | bytes 6291464 | tf_op jit(solution)/shard_map/ppermute | solution.py:371
  308.6 136.2 %collective-permute-start.23 = (bf16[2,256,2304]{2,1,0:T(8,128)(2,1)}, bf16[2,256,2304]{2,1,0:T(8,128)(2,1)}, u32[]{:S(2)}, u32[]{:S(2)}) collective-permute-start(bf16[2,256,2304]{2,1,0:T(8,128)(2,1)} %dynamic-slice_bitcast_fusion.1), channel_id=1, source_target_pairs={{0,8},{8,0},{16,24},{24,16},{1,9},{9,1},{17,25},{25,17},{2,10},{10... | collective-permute-start | bytes 7077896 | tf_op jit(solution)/shard_map/ppermute | solution.py:376
  310.2 145.5 %collective-permute-start.25 = (bf16[2,256,2304]{2,1,0:T(8,128)(2,1)}, bf16[2,256,2304]{2,1,0:T(8,128)(2,1)}, u32[]{:S(2)}, u32[]{:S(2)}) collective-permute-start(bf16[2,256,2304]{2,1,0:T(8,128)(2,1)} %dynamic-slice_bitcast_fusion), channel_id=1, source_target_pairs={{0,8},{8,0},{16,24},{24,16},{1,9},{9,1},{17,25},{25,17},{2,10},{10... | collective-permute-start | bytes 7077896 | tf_op jit(solution)/shard_map/ppermute | solution.py:376
  333.7 146.9 %collective-permute-start.27 = (bf16[2,256,2304]{1,2,0:T(8,128)(2,1)}, bf16[2,256,2304]{1,2,0:T(8,128)(2,1)}, u32[]{:S(2)}, u32[]{:S(2)}) collective-permute-start(bf16[2,256,2304]{1,2,0:T(8,128)(2,1)} %bitcast.148), channel_id=1, source_target_pairs={{0,8},{8,0},{16,24},{24,16},{1,9},{9,1},{17,25},{25,17},{2,10},{10... | collective-permute-start | bytes 7077896 | tf_op jit(solution)/shard_map/ppermute | solution.py:376
  381.8 66.8 %collective-permute-start.12 = (bf16[1024,512]{1,0:T(8,128)(2,1)}, bf16[1024,512]{1,0:T(8,128)(2,1)}, u32[]{:S(2)}, u32[]{:S(2)}) collective-permute-start(bf16[1024,512]{1,0:T(8,128)(2,1)} %get-tuple-element.62), channel_id=1, source_target_pairs={{0,2},{1,3},{8,10},{9,11},{16,18},{17,19},{24,26},{25,27}} | collective-permute-start | bytes 3145736 | tf_op jit(solution)/shard_map/ppermute | solution.py:584
  386.6 65.8 %collective-permute-start.15 = (bf16[1024,512]{1,0:T(8,128)(2,1)}, bf16[1024,512]{1,0:T(8,128)(2,1)}, u32[]{:S(2)}, u32[]{:S(2)}) collective-permute-start(bf16[1024,512]{1,0:T(8,128)(2,1)} %get-tuple-element.62), channel_id=1, source_target_pairs={{6,4},{7,5},{14,12},{15,13},{22,20},{23,21},{30,28},{31,29}} | collective-permute-start | bytes 3145736 | tf_op jit(solution)/shard_map/ppermute | solution.py:584
  444.8 43.4 %collective-permute-start.21 = (bf16[2,256,512]{1,2,0:T(8,128)(2,1)S(1)}, bf16[2,256,512]{1,2,0:T(8,128)(2,1)S(1)}, u32[]{:S(2)}, u32[]{:S(2)}) collective-permute-start(bf16[2,256,512]{1,2,0:T(8,128)(2,1)S(1)} %bitcast.167), channel_id=1, source_target_pairs={{0,8},{8,0},{16,24},{24,16},{1,9},{9,1},{17,25},{25,17},{2,10},{10... | collective-permute-start | bytes 1572872 | tf_op jit(solution)/shard_map/ppermute | solution.py:376
  448.7 76.3 %collective-permute-start.24 = (bf16[256,2304]{1,0:T(8,128)(2,1)S(1)}, bf16[256,2304]{1,0:T(8,128)(2,1)}, u32[]{:S(2)}, u32[]{:S(2)}) collective-permute-start(bf16[256,2304]{1,0:T(8,128)(2,1)S(1)} %dynamic-slice_bitcast_fusion.4), channel_id=1, source_target_pairs={{0,16},{8,24},{16,0},{24,8},{1,17},{9,25},{17,1},{25,9},{2,18},{10... | collective-permute-start | bytes 3538952 | tf_op jit(solution)/shard_map/ppermute | solution.py:381
  460.9 66.8 %collective-permute-start.26 = (bf16[256,2304]{1,0:T(8,128)(2,1)}, bf16[256,2304]{1,0:T(8,128)(2,1)}, u32[]{:S(2)}, u32[]{:S(2)}) collective-permute-start(bf16[256,2304]{1,0:T(8,128)(2,1)} %dynamic-slice_bitcast_fusion.3), channel_id=1, source_target_pairs={{0,16},{8,24},{16,0},{24,8},{1,17},{9,25},{17,1},{25,9},{2,18},{10... | collective-permute-start | bytes 3538952 | tf_op jit(solution)/shard_map/ppermute | solution.py:381
  479.3 31.8 %collective-permute-start.17 = (bf16[1024,512]{1,0:T(8,128)(2,1)S(1)}, bf16[1024,512]{1,0:T(8,128)(2,1)S(1)}, u32[]{:S(2)}, u32[]{:S(2)}) collective-permute-start(bf16[1024,512]{1,0:T(8,128)(2,1)S(1)} %get-tuple-element.92), channel_id=1, source_target_pairs={{2,0},{4,2},{6,4},{3,1},{5,3},{7,5},{10,8},{12,10},{14,12},{11,9},... | collective-permute-start | bytes 3145736 | tf_op jit(solution)/shard_map/ppermute | solution.py:584
  480.6 30.5 %collective-permute-start.14 = (bf16[1024,512]{1,0:T(8,128)(2,1)S(1)}, bf16[1024,512]{1,0:T(8,128)(2,1)S(1)}, u32[]{:S(2)}, u32[]{:S(2)}) collective-permute-start(bf16[1024,512]{1,0:T(8,128)(2,1)S(1)} %get-tuple-element.93), channel_id=1, source_target_pairs={{0,2},{2,4},{4,6},{1,3},{3,5},{5,7},{8,10},{10,12},{12,14},{9,11},... | collective-permute-start | bytes 3145736 | tf_op jit(solution)/shard_map/ppermute | solution.py:584
  508.6 28.3 %collective-permute-start.28 = (bf16[256,2304]{0,1:T(8,128)(2,1)}, bf16[256,2304]{0,1:T(8,128)(2,1)}, u32[]{:S(2)}, u32[]{:S(2)}) collective-permute-start(bf16[256,2304]{0,1:T(8,128)(2,1)} %dynamic-slice_bitcast_fusion.2), channel_id=1, source_target_pairs={{0,16},{8,24},{16,0},{24,8},{1,17},{9,25},{17,1},{25,9},{2,18},{10... | collective-permute-start | bytes 3538952 | tf_op jit(solution)/shard_map/ppermute | solution.py:381
  553.5 46.8 %collective-permute-start.18 = (bf16[1024,1024]{1,0:T(8,128)(2,1)}, bf16[1024,1024]{1,0:T(8,128)(2,1)}, u32[]{:S(2)}, u32[]{:S(2)}) collective-permute-start(bf16[1024,1024]{1,0:T(8,128)(2,1)} %convolution_convert_fusion.4), channel_id=1, source_target_pairs={{0,1},{1,0},{2,3},{3,2},{4,5},{5,4},{6,7},{7,6},{8,9},{9,8},{10,11... | collective-permute-start | bytes 6291464 | tf_op jit(solution)/shard_map/ppermute | solution.py:371
  (88 other events, 1255.6 us)
Sparse Core Ops, SparseCore 0:
  36.6 24.3 all-gather.5
  62.5 37.4 all-gather.7
  101.5 37.4 all-gather.9
  140.4 38.0 all-gather.11
  547.7 164.6 all-reduce.3

commit v2 on v1

v2 whole, which is shorter than its diff:
```python
import functools

import jax
import jax.numpy as jnp
from jax import lax
from jax.experimental import pallas as pl
from jax.experimental.pallas import tpu as pltpu
from jax.sharding import PartitionSpec as P

HD = 64
EPSILON = 1e-05
ROPE_BASE = 1000000.0
LOG2E = 1.4426950408889634
SCALE2 = 0.125 * LOG2E
NT = (((1,), (1,)), ((), ()))
NN = (((1,), (0,)), ((), ()))
TN = (((0,), (0,)), ((), ()))
F32, BF16 = jnp.float32, jnp.bfloat16


def mm(a, b, dims=NN):
    return lax.dot_general(a, b, dims, preferred_element_type=F32)


def cost(flops, bytes_accessed):
    return pl.CostEstimate(
        flops=flops // 64, bytes_accessed=bytes_accessed // 64, transcendentals=0
    )


def half(shape, which):
    lane = lax.broadcasted_iota(jnp.int32, shape, len(shape) - 1)
    return (lane < HD) if which == 0 else (lane >= HD)


def pieces(m, n_ctx, block, where, order):
    me = where[0]

    def low(shard):
        first, second = order[2 * shard], order[2 * shard + 1]
        return jnp.minimum(first, second), jnp.where(first < second, 0, block)

    q_id, q_low = low(me)
    q_high = block - q_low
    if m == 0:
        q_low, q_high = pl.multiple_of(q_low, block), pl.multiple_of(q_high, block)
        return [(q_low, q_low, True), (q_high, q_low, False), (q_high, q_high, True)]
    left, right = me, n_ctx - 1 - me
    beyond = m - jnp.minimum(left, right)
    inner = (m + 1) // 2 if m % 2 else -(m // 2)
    outer = jnp.where(right > left, beyond, -beyond)
    far = me + jnp.where(m <= 2 * jnp.minimum(left, right), inner, outer)
    k_id, k_low = low(far)
    before = k_id < q_id
    q_first = pl.multiple_of(jnp.where(before, q_low, q_high), block)
    k_second = pl.multiple_of(jnp.where(before, k_low, block - k_low), block)
    return [
        (q_first, pl.multiple_of(k_low, block), False),
        (pl.multiple_of(q_high, block), k_second, False),
    ]


def attend_body(m, n_ctx, first, last, block, where, order, q_ref, kv_ref, *rest):
    rest = list(rest)
    given = None if first else rest.pop(0)
    if last:
        mixb_ref, mix_ref, lse_ref, acc = rest
    else:
        (acc,) = rest
    acc[...] = jnp.zeros_like(acc) if first else given[...]
    for q_at, k_at, diagonal in pieces(m, n_ctx, block, where, order):
        kt = kv_ref[pl.ds(k_at, block), 0:128]
        vt = kv_ref[pl.ds(k_at, block), 128:256]
        one = jnp.ones((block, HD), BF16)
        for hh in range(2):
            kh = kt[:, HD * hh : HD * hh + HD]
            vh = vt[:, HD * hh : HD * hh + HD]
            kd = jnp.concatenate([kh, kh], axis=1)
            vx = (jnp.concatenate([vh, one], axis=1), jnp.concatenate([one, vh], axis=1))
            qt = q_ref[pl.ds(q_at, block), 128 * hh : 128 * hh + 128]
            for r in range(2):
                qr = jnp.where(half((block, 128), r), qt, jnp.zeros_like(qt))
                p = jnp.exp2(mm(qr, kd, NT) * SCALE2)
                if diagonal:
                    row = lax.broadcasted_iota(jnp.int32, p.shape, 0)
                    col = lax.broadcasted_iota(jnp.int32, p.shape, 1)
                    p = jnp.where(col <= row, p, 0.0)
                c = 256 * hh + 128 * r
                acc[pl.ds(q_at, block), c : c + 128] += mm(p.astype(BF16), vx[r])
    if last:
        rows = acc.shape[0]
        lane = lax.broadcasted_iota(jnp.int32, (8, 128), 1)
        sub = lax.broadcasted_iota(jnp.int32, (8, 128), 0)
        total = jnp.zeros((8, rows), F32)
        for hh in range(2):
            out = []
            for r in range(2):
                a = acc[:, 256 * hh + 128 * r : 256 * hh + 128 * r + 128]
                out.append(a / pltpu.roll(a, HD, 1))
                pick = jnp.where((lane == (HD if r == 0 else 0)) & (sub == 2 * hh + r), 1.0, 0.0)
                total += lax.dot_general(
                    pick, a, NT, precision=lax.Precision.HIGHEST, preferred_element_type=F32
                )
            mix = jnp.where(half((rows, 128), 0), out[0], out[1])
            mix_ref[:, 128 * hh : 128 * hh + 128] = mix
            mixb_ref[:, 128 * hh : 128 * hh + 128] = mix.astype(BF16)
        lse_ref[0] = jnp.log2(jnp.where(sub[:, 0:1] < 4, total, 1.0))


def attend(m, n_ctx, place, q, kv, acc, last, block, at=None):
    rows = q.shape[0]
    total = kv.shape[1] // 256
    base, pairs = (0, total) if at is None else (at, 1)
    first = acc is None
    args = [*place, q, kv]
    wide = pl.BlockSpec((rows, 512), lambda g, *_: (0, g))
    slim = pl.BlockSpec((rows, 256), lambda g, *_: (0, g))
    pair = pl.BlockSpec((rows, 256), lambda g, *_: (0, g + base))
    in_specs = [pair, pair]
    if not first:
        in_specs.append(pl.BlockSpec((rows, 512), lambda g, *_: (0, g + base)))
        args.append(acc)
    if last:
        out_shape = (
            jax.ShapeDtypeStruct((rows, pairs * 256), BF16),
            jax.ShapeDtypeStruct((rows, pairs * 256), F32),
            jax.ShapeDtypeStruct((pairs, 8, rows), F32),
        )
        out_specs = (slim, slim, pl.BlockSpec((1, 8, rows), lambda g, *_: (g, 0, 0)))
        scratch = [pltpu.VMEM((rows, 512), F32)]
    else:
        out_shape = jax.ShapeDtypeStruct((rows, pairs * 512), F32)
        out_specs = wide
        scratch = []
    work = 2 * block * block * pairs * 4
    return pl.pallas_call(
        functools.partial(attend_body, m, n_ctx, first, last, block),
        out_shape=out_shape,
        grid_spec=pltpu.PrefetchScalarGridSpec(
            num_scalar_prefetch=2,
            grid=(pairs,),
            in_specs=in_specs,
            out_specs=out_specs,
            scratch_shapes=scratch,
        ),
        compiler_params=pltpu.CompilerParams(vmem_limit_bytes=40 << 20),
        cost_estimate=cost(work * 1024, 12 << 20),
        name="attend",
    )(*args)


def attend_back_body(m, n_ctx, first, block, where, order, q_ref, do_ref, kv_ref, lse_ref, dlt_ref, *rest):
    rest = list(rest)
    given = None if first else rest.pop(0)
    dq, dkv_ref, dka, dva = rest
    dq[...] = jnp.zeros_like(dq) if first else given[...]
    dka[...] = jnp.zeros_like(dka)
    dva[...] = jnp.zeros_like(dva)
    for q_at, k_at, diagonal in pieces(m, n_ctx, block, where, order):
        kt = kv_ref[pl.ds(k_at, block), 0:128]
        vt = kv_ref[pl.ds(k_at, block), 128:256]
        zero = jnp.zeros((block, HD), BF16)
        for hh in range(2):
            kh = kt[:, HD * hh : HD * hh + HD]
            vh = vt[:, HD * hh : HD * hh + HD]
            kx = (jnp.concatenate([kh, zero], axis=1), jnp.concatenate([zero, kh], axis=1))
            vx = (jnp.concatenate([vh, zero], axis=1), jnp.concatenate([zero, vh], axis=1))
            c = 128 * hh
            qt = q_ref[pl.ds(q_at, block), c : c + 128]
            dt = do_ref[pl.ds(q_at, block), c : c + 128]
            dvs, dks, dqs = [], [], None
            for r in range(2):
                row = 2 * hh + r
                lse = lse_ref[0, row : row + 1, pl.ds(q_at, block)]
                dlt = dlt_ref[0, row : row + 1, pl.ds(q_at, block)]
                p = jnp.exp2(mm(kx[r], qt, NT) * SCALE2 - lse)
                if diagonal:
                    key = lax.broadcasted_iota(jnp.int32, p.shape, 0)
                    query = lax.broadcasted_iota(jnp.int32, p.shape, 1)
                    p = jnp.where(key <= query, p, 0.0)
                ds = (p * (mm(vx[r], dt, NT) - dlt)).astype(BF16)
                dvs.append(mm(p.astype(BF16), dt))
                dks.append(mm(ds, qt))
                term = mm(ds, kx[r], TN)
                dqs = term if dqs is None else dqs + term
            left = half((block, 128), 0)
            dva[pl.ds(k_at, block), c : c + 128] += jnp.where(left, dvs[0], dvs[1])
            dka[pl.ds(k_at, block), c : c + 128] += jnp.where(left, dks[0], dks[1])
            dq[pl.ds(q_at, block), c : c + 128] += dqs
    for at, ref, scale in ((0, dka, 0.125), (128, dva, 1.0)):
        a = ref[...]
        a = jnp.concatenate([a[:, 0:64] + a[:, 64:128], a[:, 128:192] + a[:, 192:256]], axis=1)
        dkv_ref[:, at : at + 128] = (a * scale).astype(dkv_ref.dtype)


def attend_back(m, n_ctx, place, q, do, kv, lse, dlt, dq, block):
    rows = q.shape[0]
    pairs = kv.shape[1] // 256
    first = dq is None
    slim = pl.BlockSpec((rows, 256), lambda g, *_: (0, g))
    line = pl.BlockSpec((1, 8, rows), lambda g, *_: (g, 0, 0))
    in_specs = [slim, slim, slim, line, line]
    args = [*place, q, do, kv, lse, dlt]
    if not first:
        in_specs.append(slim)
        args.append(dq)
    work = 2 * block * block * pairs * 4
    return pl.pallas_call(
        functools.partial(attend_back_body, m, n_ctx, first, block),
        out_shape=(
            jax.ShapeDtypeStruct((rows, pairs * 256), F32),
            jax.ShapeDtypeStruct((rows, pairs * 256), F32 if m == 0 else BF16),
        ),
        grid_spec=pltpu.PrefetchScalarGridSpec(
            num_scalar_prefetch=2,
            grid=(pairs,),
            in_specs=in_specs,
            out_specs=(slim, slim),
            scratch_shapes=[pltpu.VMEM((rows, 256), F32), pltpu.VMEM((rows, 256), F32)],
        ),
        compiler_params=pltpu.CompilerParams(vmem_limit_bytes=40 << 20),
        cost_estimate=cost(work * 2048, 12 << 20),
        name="attend_back",
    )(*args)


def head_mean(u):
    a = lax.broadcasted_iota(jnp.int32, (128, 128), 0) // HD
    b = lax.broadcasted_iota(jnp.int32, (128, 128), 1) // HD
    ones = jnp.where(a == b, 1.0, 0.0).astype(BF16)
    high = u.astype(BF16)
    low = (u - high.astype(F32)).astype(BF16)
    return (mm(high, ones) + mm(low, ones)) * (1.0 / HD)


def turn(u):
    lane = lax.broadcasted_iota(jnp.int32, u.shape, 1)
    return jnp.where(lane % HD < HD // 2, pltpu.roll(u, 96, 1), pltpu.roll(u, 32, 1))


def rotated(u, gain, cos, sin):
    n = u * lax.rsqrt(head_mean(u * u) + EPSILON) * gain
    return (n * cos + turn(n) * sin).astype(BF16)


def row_scale(x):
    return lax.rsqrt(jnp.mean(x * x, axis=-1, keepdims=True) + EPSILON)


def blocks_product(n, w_ref):
    count = w_ref.shape[0]
    size = w_ref.shape[1] - 16
    return sum(mm(n[:, f * size : f * size + size], w_ref[f, 0:size, :]) for f in range(count))


def key_body(x_ref, g_ref, w_ref, cos_ref, sin_ref, gain_ref, n_ref, k_ref, kv_ref):
    x = x_ref[...].astype(F32)
    n = (x * row_scale(x) * g_ref[0:1]).astype(BF16)
    n_ref[...] = n
    both = blocks_product(n, w_ref)
    width = k_ref.shape[1]
    k_ref[...] = both[:, :width]
    for t in range(width // 128):
        c = 128 * t
        kv_ref[:, 2 * c : 2 * c + 128] = rotated(
            both[:, c : c + 128], gain_ref[1:2], cos_ref[...], sin_ref[...]
        )
        kv_ref[:, 2 * c + 128 : 2 * c + 256] = both[:, width + c : width + c + 128].astype(BF16)


def query_body(n_ref, w_ref, cos_ref, sin_ref, gain_ref, u_ref, q_ref):
    u = blocks_product(n_ref[...], w_ref)
    u_ref[...] = u
    for t in range(u.shape[1] // 128):
        c = slice(128 * t, 128 * t + 128)
        q_ref[:, c] = rotated(u[:, c], gain_ref[0:1], cos_ref[...], sin_ref[...])


def row_call(body, name, step, rows, ins, outs, flops, scratch=(), aliases=None, first=0, count=None):
    spec = lambda w: pl.BlockSpec((step, w), lambda i: (i + first, 0))
    in_specs = []
    for array, kind in ins:
        if kind == "rows":
            in_specs.append(spec(array.shape[1]))
        elif kind == "part":
            in_specs.append(pl.BlockSpec((step, array.shape[1]), lambda i: (i, 0)))
        elif kind == "whole":
            in_specs.append(pl.BlockSpec(array.shape, lambda i, n=array.ndim: (0,) * n))
        else:
            in_specs.append(kind)
    return pl.pallas_call(
        body,
        out_shape=tuple(o[0] for o in outs),
        grid=(rows // step if count is None else count,),
        in_specs=in_specs,
        out_specs=tuple(spec(o[0].shape[1]) if o[1] is None else o[1] for o in outs),
        scratch_shapes=list(scratch),
        input_output_aliases=aliases or {},
        compiler_params=pltpu.CompilerParams(vmem_limit_bytes=40 << 20),
        cost_estimate=cost(flops, 1 << 20),
        name=name,
    )(*(array for array, _ in ins))


def project_keys(x, gain, packed, cos, sin, gains, kw, step):
    rows, width = x.shape
    f, r, cols = packed.shape
    shape = lambda w, t: (jax.ShapeDtypeStruct((rows, w), t), None)
    part = pl.BlockSpec((f, r, 2 * kw), lambda i: (0, 0, cols // (2 * kw) - 1))
    return row_call(
        key_body, "project_keys", step, rows,
        [(x, "rows"), (gain, "whole"), (packed, part), (cos, "rows"), (sin, "rows"), (gains, "whole")],
        [shape(width, BF16), shape(kw, F32), shape(2 * kw, BF16)],
        rows * width * kw * 4,
    )


def project_queries(n, packed, cos, sin, gains, qw, step):
    rows, width = n.shape
    f, r, _ = packed.shape
    shape = lambda w, t: (jax.ShapeDtypeStruct((rows, w), t), None)
    part = pl.BlockSpec((f, r, qw), lambda i: (0, 0, 0))
    return row_call(
        query_body, "project_queries", step, rows,
        [(n, "rows"), (packed, part), (cos, "rows"), (sin, "rows"), (gains, "whole")],
        [shape(qw, F32), shape(qw, BF16)],
        rows * width * qw * 2,
    )


def pair_product(own, other, w_ref, at):
    size = own.shape[1]
    base = w_ref.shape[1] // 2
    return jnp.concatenate(
        [
            mm(own, w_ref[f, at * size : at * size + size, :])
            + mm(other, w_ref[f, base + at * size : base + at * size + size, :])
            for f in range(w_ref.shape[0])
        ],
        axis=1,
    )


def join_body(at, own_ref, other_ref, w_ref, *refs):
    term = pair_product(own_ref[...], other_ref[...], w_ref, at)
    refs[-1][...] = term if len(refs) == 1 else refs[0][...] + term


def join_last_body(at, own_ref, other_ref, w_ref, x_ref, g_ref, *refs):
    r_ref, n_ref = refs[-2:]
    term = pair_product(own_ref[...], other_ref[...], w_ref, at)
    if len(refs) == 3:
        term = refs[0][...] + term
    r = x_ref[...].astype(F32) + term
    r_ref[...] = r
    n_ref[...] = (r * row_scale(r) * g_ref[0:1]).astype(BF16)


def join(x, gain, w, own, others, step):
    rows, width = x.shape
    shape = lambda w, t: (jax.ShapeDtypeStruct((rows, w), t), None)
    flops = rows * width * width
    so_far = []
    for at, (mine, other) in enumerate(zip(own, others)):
        ins = [(mine, "rows"), (other, "rows"), (w, "whole")]
        held = [(v, "rows") for v in so_far]
        if at < len(own) - 1:
            so_far = row_call(
                functools.partial(join_body, at), "join", step, rows, ins + held, [shape(width, F32)], flops
            )
    return row_call(
        functools.partial(join_last_body, at), "join_last", step, rows,
        ins + [(x, "rows"), (gain, "whole")] + held,
        [shape(width, F32), shape(width, BF16)],
        flops,
    )


def into_body(pairs, aliased, a_ref, b_ref, r_ref, dy_ref, g_ref, w_ref, mix_ref, *refs):
    d_ref, db_ref, do_ref, dlt_ref, gg_ref = refs[aliased:]
    gain = g_ref[0:1]
    r = r_ref[...]
    scale = row_scale(r)
    d = a_ref[...].astype(F32) + b_ref[...].astype(F32)
    scaled = d * gain
    back = scale * scaled - r * (scale * scale * scale) * jnp.mean(r * scaled, axis=-1, keepdims=True)

    @pl.when(pl.program_id(0) == 0)
    def _():
        gg_ref[...] = jnp.zeros_like(gg_ref)

    gg_ref[0:1] += jnp.sum(d * r * scale, axis=0, keepdims=True)
    out = dy_ref[...].astype(F32) + back
    d_ref[...] = out
    out = out.astype(BF16)
    db_ref[...] = out
    size = w_ref.shape[2]
    do = sum(mm(out[:, f * size : f * size + size], w_ref[f], NT) for f in range(w_ref.shape[0]))
    do = do.astype(BF16)
    do_ref[...] = do
    lane = lax.broadcasted_iota(jnp.int32, (8, 128), 1) // HD
    sub = lax.broadcasted_iota(jnp.int32, (8, 128), 0)
    for p in range(pairs):
        total = jnp.zeros((8, r.shape[0]), F32)
        for hh in range(2):
            c = slice(256 * p + 128 * hh, 256 * p + 128 * hh + 128)
            x = do[:, c].astype(F32) * mix_ref[:, c]
            total += lax.dot_general(
                jnp.where(sub == 2 * hh + lane, 1.0, 0.0), x, NT,
                precision=lax.Precision.HIGHEST, preferred_element_type=F32,
            )
        dlt_ref[p] = total


def into_attention(a, b, resid, dy, gain, w, mix, given, first, step):
    rows, width = resid.shape
    wide = w.shape[1] // 2
    pairs = wide // 256
    own_w = pl.BlockSpec((w.shape[0], wide, w.shape[2]), lambda i: (0, 0, 0))
    shape = lambda w, t: (jax.ShapeDtypeStruct((rows, w), t), None)
    hbm = pl.BlockSpec(memory_space=pl.ANY)
    base = [(a, "part"), (b, "part"), (resid, "rows"), (dy, "rows"), (gain, "whole"), (w, own_w), (mix, "rows")]
    given = list(given or ())
    return row_call(
        functools.partial(into_body, pairs, len(given)), "into_attention", step, rows,
        base + [(g, hbm) for g in given],
        [
            shape(width, F32), shape(width, BF16), shape(wide, BF16),
            (jax.ShapeDtypeStruct((pairs, 8, rows), F32), pl.BlockSpec((pairs, 8, step), lambda i: (0, 0, i + first))),
            (jax.ShapeDtypeStruct((8, width), F32), pl.BlockSpec((8, width), lambda i: (0, 0))),
        ],
        rows * width * wide,
        aliases={len(base) + k: k for k in range(len(given))},
        first=first, count=a.shape[0] // step,
    )


def leave_body(a_ref, b_ref, x_ref, g_ref, d_ref, out_ref):
    x = x_ref[...].astype(F32)
    scale = row_scale(x)
    scaled = (a_ref[...].astype(F32) + b_ref[...].astype(F32)) * g_ref[0:1]
    back = scale * scaled - x * (scale * scale * scale) * jnp.mean(x * scaled, axis=-1, keepdims=True)
    out_ref[...] = d_ref[...] + back


def leave(a, b, x, gain, d, step):
    rows, width = x.shape
    return row_call(
        leave_body, "leave", step, rows,
        [(a, "rows"), (b, "rows"), (x, "rows"), (gain, "whole"), (d, "rows")],
        [(jax.ShapeDtypeStruct((rows, width), F32), None)],
        rows * width * 16,
    )[0]


def rope_back_body(terms, dq_ref, q_ref, k_ref, cos_ref, sin_ref, gain_ref, *rest):
    dkv_refs, (out_ref, gg_ref) = rest[:terms], rest[terms:]
    cos, sin = cos_ref[...], sin_ref[...]

    @pl.when(pl.program_id(0) == 0)
    def _():
        gg_ref[...] = jnp.zeros_like(gg_ref)

    def one(d, u, row):
        gain = gain_ref[row : row + 1]
        dn = d * cos + turn(d * sin)
        r = lax.rsqrt(head_mean(u * u) + EPSILON)
        gd = gain * dn
        gg_ref[row : row + 1] += jnp.sum(dn * u * r, axis=0, keepdims=True)
        return (r * gd - u * (r * r * r) * head_mean(u * gd)).astype(BF16)

    qw, kw = q_ref.shape[1], k_ref.shape[1]
    for t in range(qw // 128):
        c = slice(128 * t, 128 * t + 128)
        out_ref[:, c] = one(dq_ref[:, c] * 0.125, q_ref[:, c], 0)
    for t in range(kw // 128):
        dk = sum(ref[:, 256 * t : 256 * t + 128].astype(F32) for ref in dkv_refs)
        dv = sum(ref[:, 256 * t + 128 : 256 * t + 256].astype(F32) for ref in dkv_refs)
        out_ref[:, qw + 128 * t : qw + 128 * t + 128] = one(dk, k_ref[:, 128 * t : 128 * t + 128], 1)
        out_ref[:, qw + kw + 128 * t : qw + kw + 128 * t + 128] = dv.astype(BF16)


def rope_back(dq, q_raw, k_raw, cos, sin, gains, dkvs, step):
    rows, qw = q_raw.shape
    kw = k_raw.shape[1]
    spec = lambda w: pl.BlockSpec((step, w), lambda i: (i, 0))
    fixed = pl.BlockSpec((8, 128), lambda i: (0, 0))
    return pl.pallas_call(
        functools.partial(rope_back_body, len(dkvs)),
        out_shape=(
            jax.ShapeDtypeStruct((rows, qw + 2 * kw), BF16),
            jax.ShapeDtypeStruct((8, 128), F32),
        ),
        grid=(rows // step,),
        in_specs=[spec(qw), spec(qw), spec(kw), spec(128), spec(128), fixed]
        + [spec(2 * kw)] * len(dkvs),
        out_specs=(spec(qw + 2 * kw), fixed),
        cost_estimate=cost(rows * qw * 1600, rows * qw * 20),
        name="rope_back",
    )(dq, q_raw, k_raw, cos, sin, gains, *dkvs)


def middle_body(step, aliased, n_ref, dy_ref, wg_ref, wu_ref, wd_ref, *refs):
    h_ref, dg_ref, du_ref, dn_ref, acc = refs[aliased:]

    @pl.when(pl.program_id(0) == 0)
    def _():
        acc[...] = jnp.zeros_like(acc)

    for at in range(0, n_ref.shape[0], step):
        rows = pl.ds(at, step)
        n = n_ref[rows, :]
        g = mm(n, wg_ref[...])
        u = mm(n, wu_ref[...])
        dh = mm(dy_ref[rows, :], wd_ref[...], NT)
        s = 1.0 / (1.0 + jnp.exp2(g * (-LOG2E)))
        act = g * s
        h_ref[rows, :] = (act * u).astype(BF16)
        du_ref[rows, :] = (dh * act).astype(BF16)
        dg_ref[rows, :] = (dh * u * s * (1.0 + g * (1.0 - s))).astype(BF16)
    acc[...] += mm(dg_ref[...], wg_ref[...], NT) + mm(du_ref[...], wu_ref[...], NT)

    @pl.when(pl.program_id(0) == pl.num_programs(0) - 1)
    def _():
        dn_ref[...] = acc[...].astype(BF16)


def middle(n, dy, both, wd, given, at, parts):
    total, width = n.shape
    rows = total // parts
    hidden = both.shape[1] // 2
    tile = 256
    whole = pl.BlockSpec((rows, width), lambda j: (at, 0))
    cols = pl.BlockSpec((width, tile), lambda j: (0, j))
    more = pl.BlockSpec((width, tile), lambda j: (0, j + hidden // tile))
    outs = pl.BlockSpec((rows, tile), lambda j: (at, j))
    shape = jax.ShapeDtypeStruct((total, hidden), BF16)
    given = list(given or ())
    return pl.pallas_call(
        functools.partial(middle_body, min(rows, 256), len(given)),
        out_shape=(shape, shape, shape, jax.ShapeDtypeStruct((rows, width), BF16)),
        grid=(hidden // tile,),
        in_specs=[whole, whole, cols, more, pl.BlockSpec((tile, width), lambda j: (j, 0))]
        + [pl.BlockSpec(memory_space=pl.ANY)] * len(given),
        out_specs=(outs, outs, outs, pl.BlockSpec((rows, width), lambda j: (0, 0))),
        scratch_shapes=[pltpu.VMEM((rows, width), F32)],
        input_output_aliases={5 + k: k for k in range(len(given))},
        compiler_params=pltpu.CompilerParams(vmem_limit_bytes=40 << 20),
        cost_estimate=cost(10 * rows * width * hidden, 6 * (rows * hidden + width * hidden)),
        name="middle",
    )(n, dy, both, both, wd, *given)


def down_body(h_ref, w_ref, out_ref):
    out_ref[...] = mm(h_ref[...], w_ref[...]).astype(BF16)


def down(h, w):
    rows, hidden = h.shape
    width = w.shape[1]
    tile = min(rows, 256)
    return pl.pallas_call(
        down_body,
        out_shape=jax.ShapeDtypeStruct((rows, width), BF16),
        grid=(rows // tile,),
        in_specs=[
            pl.BlockSpec((tile, hidden), lambda j: (j, 0)),
            pl.BlockSpec((hidden, width), lambda j: (0, 0)),
        ],
        out_specs=pl.BlockSpec((tile, width), lambda j: (j, 0)),
        compiler_params=pltpu.CompilerParams(vmem_limit_bytes=40 << 20),
        cost_estimate=cost(2 * rows * width * hidden, 2 * (rows * hidden + width * hidden)),
        name="down",
    )(h, w)


def grad_body(at_ref, a_ref, z_ref, b_ref, keep_ref, give_ref):
    keep_ref[0] = mm(a_ref[...], b_ref[...], TN).astype(BF16)
    give_ref[0] = mm(z_ref[...], b_ref[...], TN).astype(BF16)


def weight_grad(a, b, parts, core):
    rows, width = a.shape
    cols = b.shape[1]
    block = width // parts
    tile = next(t for t in (2304, 1024, 512, 256, 128) if cols % t == 0)
    shape = jax.ShapeDtypeStruct((parts // 2, block, cols), BF16)
    out = pl.BlockSpec((1, block, tile), lambda j, i, c: (i, 0, j))
    return pl.pallas_call(
        grad_body,
        out_shape=(shape, shape),
        grid_spec=pltpu.PrefetchScalarGridSpec(
            num_scalar_prefetch=1,
            grid=(cols // tile, parts // 2),
            in_specs=[
                pl.BlockSpec((rows, block), lambda j, i, c: (0, 2 * i + c[0])),
                pl.BlockSpec((rows, block), lambda j, i, c: (0, 2 * i + 1 - c[0])),
                pl.BlockSpec((rows, tile), lambda j, i, c: (0, j)),
            ],
            out_specs=(out, out),
        ),
        compiler_params=pltpu.CompilerParams(vmem_limit_bytes=40 << 20),
        cost_estimate=cost(2 * rows * width * cols, 2 * (rows * width + rows * cols + width * cols)),
        name="weight_grad",
    )(core.reshape(1), a, a, b)


def swap(x):
    n = lax.axis_size("tp")
    return lax.ppermute(x, "tp", [(i, i ^ 1) for i in range(n)])


def core_swap(x):
    n = lax.axis_size("fsdp")
    return lax.ppermute(x, "fsdp", [(i, i ^ 1) for i in range(n)])


def y_shift(x, s):
    n = lax.axis_size("fsdp")
    return lax.ppermute(x, "fsdp", [(i, (i + 2 * s) % n) for i in range(n)])


def gather_y(x):
    n = lax.axis_size("fsdp")
    y, ny = lax.axis_index("fsdp") // 2, n // 2
    mine = jnp.zeros((ny,) + x.shape, x.dtype)
    mine = lax.dynamic_update_index_in_dim(mine, x, y, 0)
    for s in range(1, ny):
        mine = lax.dynamic_update_index_in_dim(mine, y_shift(x, s), (y - s) % ny, 0)
    return mine


def gather_core(mine):
    c = lax.axis_index("fsdp") % 2
    other = core_swap(mine)
    lower = jnp.where(c == 0, mine, other)
    upper = jnp.where(c == 0, other, mine)
    return jnp.stack([lower, upper], axis=1)


def core_sums(keep, give):
    ny = keep.shape[0]
    y = lax.axis_index("fsdp") // 2
    got = core_swap(give)
    sends = [both_block(keep, got, (y + s) % ny).astype(BF16) for s in range(1, ny)]
    return keep, got, sends


def both_block(keep, got, n):
    a = lax.dynamic_index_in_dim(keep, n, 0, keepdims=False).astype(F32)
    return a + lax.dynamic_index_in_dim(got, n, 0, keepdims=False).astype(F32)


def y_sums(keep, got, sends, *after):
    parts = [y_shift(send, s + 1) for s, send in enumerate(sends)]
    keep, got, *rest = lax.optimization_barrier((keep, got, *parts, *after))
    total = both_block(keep, got, lax.axis_index("fsdp") // 2)
    for part in rest[: len(parts)]:
        total = total + part.astype(F32)
    return total.astype(BF16)


def nearest(m, i, n):
    left, right = i, n - 1 - i
    near = min(left, right)
    if m == 0:
        return 0
    if m <= 2 * near:
        return (m + 1) // 2 if m % 2 else -(m // 2)
    return m - near if right > left else -(m - near)


def choose(index, table):
    value = table[0][0]
    for array, positions in table[1:]:
        here = functools.reduce(jnp.logical_or, [index == i for i in positions])
        value = jnp.where(here, array, value)
    return value


def tie(x, *others):
    return lax.optimization_barrier((x,) + others)[0]


def tables(x):
    lane = jnp.arange(128)
    exponent = -((lane % (HD // 2)).astype(F32) * 2.0) / HD
    angle = x.astype(F32)[:, None] * (ROPE_BASE**exponent)[None, :]
    sign = jnp.where(lane % HD < HD // 2, -1.0, 1.0).astype(F32)
    return jnp.cos(angle), jnp.sin(angle) * sign[None, :]


def per_device(
    tokens, cotangent, block_order, positions,
    attn_gain, w_query, key_weight, value_weight, query_gain, key_gain,
    w_out, ffn_gain, w_gate, w_up, w_down,
):
    n_ctx = lax.axis_size("ctx")
    n_fsdp = lax.axis_size("fsdp")
    me = lax.axis_index("ctx")
    seqs, rows, width = tokens.shape
    x = tokens.reshape(seqs * rows, width)
    dy = cotangent.reshape(seqs * rows, width)
    block = rows // 2
    qw, kw = w_query.shape[1], key_weight.shape[1]
    gs, hs = attn_gain.shape[0], query_gain.shape[0]

    qkv_w = qw + 2 * kw
    small = jnp.concatenate([attn_gain, ffn_gain, query_gain, key_gain])
    small = jnp.pad(small.reshape(1, -1), ((0, 15), (0, qkv_w - 2 * (gs + hs))))
    packed = jnp.concatenate(
        [jnp.concatenate([w_query, key_weight, value_weight], axis=1), small], axis=0
    )
    mine = gather_y(packed)
    out_i = tie(w_out, packed)
    out_i = jnp.concatenate([out_i, swap(out_i)], axis=0)
    cos, sin = tables(positions.reshape(-1))
    both_i = jnp.concatenate(lax.optimization_barrier((w_gate, w_up, packed))[:2], axis=1)
    mine, out_i, cos, sin, both_i = lax.optimization_barrier((mine, out_i, cos, sin, both_i))
    both_full = lax.all_gather(both_i, "fsdp", axis=0, tiled=True)
    packed = gather_core(mine).reshape(n_fsdp, gs + 16, qkv_w)
    small = packed[:, gs].astype(F32)
    row = lambda v: jnp.broadcast_to(v.reshape(1, -1), (8, v.size))
    gain_attn = row(small[:, :gs])
    gain_ffn = row(small[:, gs : 2 * gs])
    gain_q = small[:, 2 * gs : 2 * gs + hs].reshape(-1)
    gain_k = small[:, 2 * gs + hs : 2 * (gs + hs)].reshape(-1)
    gains = jnp.stack([jnp.tile(gain_q, 2), jnp.tile(gain_k, 2)] + [jnp.zeros(128, F32)] * 6)

    step = min(256, block)
    normed_b, k_raw, kv_b = project_keys(x, gain_attn, packed, cos, sin, gains, kw, step)
    q_raw, q_b = project_queries(tie(normed_b, kv_b), packed, cos, sin, gains, qw, step)
    place = (me.astype(jnp.int32).reshape(1), block_order)
    shards = {0: kv_b}

    def shard(m):
        table = {}
        for i in range(n_ctx):
            table.setdefault(nearest(m, i, n_ctx), []).append(i)
        return choose(me, [(shards[d], where) for d, where in table.items()])

    kvs = []
    acc = None
    for t in range(1, n_ctx):
        right = [(i, i + 1) for i in range(t - 1, n_ctx - 1)]
        left = [(i, i - 1) for i in range(1, n_ctx - t + 1)]
        shards[-t] = lax.ppermute(shards[-(t - 1)], "ctx", right)
        shards[t] = lax.ppermute(shards[t - 1], "ctx", left)
        if t == 1:
            shards[-t], shards[t], q_b = lax.optimization_barrier((shards[-t], shards[t], q_b))
            out_w = lax.all_gather(tie(out_i, kv_b), "fsdp", axis=0, tiled=False)
            down_full = lax.all_gather(tie(w_down, q_b), "fsdp", axis=1, tiled=True)
            continue
        while len(kvs) < t:
            kvs.append(shard(len(kvs)))
            acc = attend(len(kvs) - 1, n_ctx, place, q_b, kvs[-1], acc, False, block)
        shards[-t], shards[t], acc = lax.optimization_barrier((shards[-t], shards[t], acc))
        if t == 2:
            acc = tie(acc, both_full)
    while len(kvs) < n_ctx - 1:
        kvs.append(shard(len(kvs)))
        acc = attend(len(kvs) - 1, n_ctx, place, q_b, kvs[-1], acc, False, block)
    m = n_ctx - 1
    kvs.append(shard(m))
    pairs = kw // 128
    mixes, others = [], []
    last_q = q_b
    for p in range(pairs):
        mixes.append(attend(m, n_ctx, place, last_q, kvs[m], acc, True, block, p))
        last_q = tie(q_b, mixes[-1][0])
        others.append(swap(mixes[-1][0]))
    mixed_b = jnp.concatenate([piece[0] for piece in mixes], axis=1)
    mix = jnp.concatenate([piece[1] for piece in mixes], axis=1)
    lse = jnp.concatenate([piece[2] for piece in mixes], axis=0)

    own = [piece[0] for piece in mixes]
    resid, two_b = join(x, gain_ffn, out_w, own, others, step)

    core = lax.axis_index("fsdp") % 2

    parts = 2
    given, d_parts, d_others = None, [], []
    two_t = two_b
    for at in range(parts):
        *given, d_part = middle(two_t, dy, both_full, down_full, given, at, parts)
        two_t = tie(two_b, d_part)
        d_parts.append(d_part)
        d_others.append(swap(d_part))
    hidden, dgate, dup = given
    down_w = weight_grad(dy, hidden, n_fsdp, core)
    two_t, hidden_t = lax.optimization_barrier((two_b, hidden, down_w, d_others[0]))[:2]
    gate_w = weight_grad(two_t, dgate, n_fsdp, core)
    up_w = weight_grad(two_t, dup, n_fsdp, core)
    down_part = down(hidden_t, down_full)
    d_others[-1], down_w, gate_w, up_w, down_part = lax.optimization_barrier(
        (d_others[-1], down_w, gate_w, up_w, down_part)
    )
    down_c, gate_c, up_c = core_sums(*down_w), core_sums(*gate_w), core_sums(*up_w)

    given, ffn_gain_g = None, 0.0
    per = rows * seqs // parts // step
    for at in range(parts):
        *given, g = into_attention(
            d_parts[at], d_others[at], resid, dy, gain_ffn, out_w, mix, given, at * per, step
        )
        ffn_gain_g = ffn_gain_g + g[0]
    d_resid, d_resid_b, do, dlt = given
    do = tie(do, *down_c[2], *gate_c[2])

    grads = [None] * n_ctx
    got = {}
    dq = None
    for m in reversed(range(n_ctx)):
        dq, grads[m] = attend_back(m, n_ctx, place, q_b, do, kvs[m], lse, dlt, dq, block)
        if m == 0:
            break
        sends = []
        for side in (1, -1):
            table = {}
            for i in range(n_ctx):
                for k in range(1, n_ctx):
                    if nearest(k, i, n_ctx) == side * m:
                        table.setdefault(k, []).append(i)
            send = choose(me, [(grads[k], where) for k, where in table.items()])
            if side in got:
                send = (send.astype(F32) + got[side].astype(F32)).astype(BF16)
            sends.append(send)
            senders = sorted(i for where in table.values() for i in where)
            got[side] = lax.ppermute(send, "ctx", [(i, i + side) for i in senders])
        if m == n_ctx - 1:
            down_other = swap(tie(down_part, dq))
            down_s = y_sums(*down_c)
            sends += [down_s] + up_c[2]
            down_s = lax.psum(down_s, "ctx")
        if m == max(n_ctx - 2, 1):
            gate_s = y_sums(*gate_c, dq)
            sends.append(gate_s)
            out_g = weight_grad(tie(d_resid_b, dq), mixed_b, n_fsdp, core)
        if m == 1:
            up_s = y_sums(*up_c, dq)
            sends += [up_s, *out_g]
            gate_s, up_s, down_s = lax.optimization_barrier((gate_s, up_s, down_s))
            gate_s, up_s = lax.psum((gate_s, up_s), "ctx")
        dq = tie(dq, *sends)
    dq, down_other = lax.optimization_barrier((dq, down_other))
    out_s = y_sums(*core_sums(*out_g))
    home = [grads[0]] + list(got.values())
    output = (tie(resid, dq) + (down_part.astype(F32) + down_other.astype(F32))).astype(BF16)

    d_qkv, head_gain = rope_back(dq, q_raw, k_raw, cos, sin, gains, home, step)
    qkv_c = core_sums(*weight_grad(normed_b, d_qkv, n_fsdp, core))
    w_qkv = packed[:, :gs].reshape(n_fsdp * gs, qkv_w)
    normed_part = mm(d_qkv, w_qkv, NT)

    head_gain = head_gain[:2, :HD] + head_gain[:2, HD:]
    xf = x.astype(F32)
    inv_one = lax.rsqrt(jnp.mean(xf * xf, axis=-1, keepdims=True) + EPSILON)
    attn_gain_g = jnp.sum(normed_part * (xf * inv_one), axis=0)
    small_g = jnp.concatenate(
        [
            attn_gain_g.reshape(n_fsdp, gs),
            0.5 * ffn_gain_g.reshape(n_fsdp, gs),
            head_gain[0].reshape(n_fsdp, hs),
            head_gain[1].reshape(n_fsdp, hs),
        ],
        axis=1,
    )
    small_g = (small_g + swap(small_g)).astype(BF16).reshape(n_fsdp // 2, 2, 1, -1)
    normed_part = tie(normed_part.astype(BF16), small_g)
    normed_other = swap(normed_part)
    small_s = y_sums(
        *core_sums(
            lax.dynamic_index_in_dim(small_g, core, 1, keepdims=False),
            lax.dynamic_index_in_dim(small_g, 1 - core, 1, keepdims=False),
        )
    )
    last = jnp.concatenate([y_sums(*qkv_c), out_s], axis=1)
    small_s = jnp.pad(small_s, ((0, 15), (0, last.shape[1] - small_s.shape[1])))
    last = jnp.concatenate([last, small_s], axis=0)
    last, gate_s, up_s = lax.optimization_barrier((last, gate_s, up_s))
    last = lax.psum(last, "ctx")
    input_grad = leave(normed_part, normed_other, x, gain_attn, d_resid, step)
    last = tie(last, input_grad)
    q_s, k_s, v_s = last[:gs, :qw], last[:gs, qw : qw + kw], last[:gs, qw + kw : qkv_w]
    out_s = last[:gs, qkv_w:]
    small_s = last[gs : gs + 1, : 2 * (gs + hs)]
    down_s, gate_s, up_s, out_s, q_s, k_s, v_s = (
        v.astype(F32) for v in (down_s, gate_s, up_s, out_s, q_s, k_s, v_s)
    )
    small_g = small_s[0].astype(F32)
    return (
        output.reshape(tokens.shape),
        input_grad.reshape(tokens.shape),
        small_g[:gs],
        q_s,
        k_s,
        v_s,
        small_g[2 * gs : 2 * gs + hs],
        small_g[2 * gs + hs :],
        out_s.T,
        small_g[gs : 2 * gs],
        gate_s,
        up_s,
        down_s.T,
    )


def solution(mesh):
    rows = P("fsdp", "ctx", None)
    ins = P("fsdp", "tp")
    outs = P("tp", "fsdp")
    one = P("fsdp")
    return jax.shard_map(
        per_device,
        mesh=mesh,
        in_specs=(
            rows, rows, P(), P("fsdp", "ctx"), one, ins, ins, ins, one, one, outs, one, ins, ins, outs,
        ),
        out_specs=(rows, rows, one, ins, ins, ins, one, one, outs, one, ins, ins, outs),
        check_vma=False,
    )
```

time: 737 us -> 570 us (0.77)
  blocking collectives: 118 us -> 0 us
  Pallas kernels: 133 us -> 198 us
  matrix products: 67 us -> 3.8 us
  waiting for transfers between devices: 210 us -> 151 us
  between operations: 32.3 us -> 15.2 us
  starting transfers between devices: 47.1 us -> 61.9 us
    psum x2 -> x0, blocking collectives: 111 us -> none  [the longest x1 65.8 us: per_device(): small_g = lax.psum(small_g, ('fsdp', 'ctx'))]
    pallas_call x11 -> x24, Pallas kernels: 125 us -> 190 us  [the longest x4 61.3 us: attend_back(): pl.pallas_call(functools.partial(attend_back_body, m, n_ctx, first, block...]
    dot_general x15 -> x1, matrix products: 67 us -> 3.8 us  [mm(): return lax.dot_general(a, b, dims, preferred_element_type=F32)]
    ppermute x5 -> x8, waiting for transfers between devices: 71.1 us -> 10.2 us  [swap(): return lax.ppermute(x, 'tp', [(i, i ^ 1) for i in range(n)])]
    psum x1 -> x3, waiting for transfers between devices: 35.4 us -> 79.4 us  [the longest x1 54.3 us: per_device(): gate_s, up_s = lax.psum((gate_s, up_s), 'ctx')]
    unnamed x165 -> x188, local copies, waits for them, and re-layouts: 23 us -> 59.7 us
    ppermute x6 -> x7, waiting for transfers between devices: 42.5 us -> 14 us  [y_shift(): return lax.ppermute(x, 'fsdp', [(i, (i + 2 * s) % n) for i in range(n)])]
    dynamic_slice x9 -> x1, local copies, waits for them, and re-layouts: 20.2 us -> 0.02 us  [per_device(): lax.dynamic_index_in_dim(small_g, 1 - core, 1, keepdims=False)]
  transfers between devices with their start and end apart: 34 -> 40, of which waited for: 12 -> 14; matrix products, arithmetic and copies ran while one was open for 17% -> 12% of each run, Pallas kernels for 15% -> 32%
where the time goes in v2:
time: 570 us; the launch traced here: 559 us
  Pallas kernels  198 us (35%)
  waiting for transfers between devices  151 us (26%)
  local copies, waits for them, and re-layouts  64.8 us (11%)
  other arithmetic  64.3 us (11%)
  starting transfers between devices  61.9 us (11%)
  between operations  15.2 us (3%)
    pallas_call x4, Pallas kernels, attend_back(): pl.pallas_call(functools.partial(attend_back_body, m, n_ctx, first, block...  61.3 us
    unnamed x188, local copies, waits for them, and re-layouts  59.7 us
    psum x1, waiting for transfers between devices, per_device(): gate_s, up_s = lax.psum((gate_s, up_s), 'ctx')  54.3 us
    pallas_call x2, Pallas kernels, middle(): pl.pallas_call(functools.partial(middle_body, min(rows, 256), len(given))...  34.6 us
    pallas_call x5, Pallas kernels, attend(): pl.pallas_call(functools.partial(attend_body, m, n_ctx, first, last, bloc...  32.4 us
    ppermute x3, waiting for transfers between devices, per_device(): shards[t] = lax.ppermute(shards[t - 1], 'ctx', left)  30.6 us
    pallas_call x7, Pallas kernels, row_call(): pl.pallas_call(body, out_shape=tuple((o[0] for o in outs)), grid=(rows //...  29 us
    ppermute x6, starting transfers between devices, per_device(): got[side] = lax.ppermute(send, 'ctx', [(i, i + side) for i in senders])  27.1 us
  transfers between devices with their start and end apart: 40, of which 14 were waited for; matrix products, arithmetic and copies ran while one was open for 12% of the time, Pallas kernels for 32%

profile of v2, /device:TPU:0, one launch (start us, length us, event | category | flops | bytes accessed | tf_op | source)
XLA Modules:
  0.0 559.2 jit_solution(11403784445570837246)
XLA Ops:
  41.1 5.5 collective-permute-start.3
  55.4 11.8 %collective-permute-done.4 = bf16[1024,512]{1,0:T(8,128)(2,1)} collective-permute-done((bf16[1024,512]{1,0:T(8,128)(2,1)}, bf16[1024,512]{1,0:T(8,128)(2,1)}, u32[]{:S(2)}, u32[]{:S(2)}) %collective-permute-start.4) | collective-permute-done | bytes 1048608 | tf_op jit(solution)/shard_map/ppermute | solution.py:748
  72.7 8.6 %attend.5.rest_0_ = f32[1024,1024]{1,0:T(8,128)S(1)} custom-call(s32[1]{0:T(128)} %bitcast.where, s32[8]{0:T(128)S(1)} %copy-done.78, bf16[1024,512]{1,0:T(8,128)(2,1)S(1)} %get-tuple-element.154.q_ref, bf16[1024,512]{1,0:T(8,128)(2,1)S(1)} %copy-done.38), custom_call_target="tpu_custom_call" | custom-call | flops 67108864 | bytes 196608 | tf_op jit(solution)/shard_map/attend/pallas_call | solution.py:136
  82.7 6.4 %attend.6.rest_0_ = f32[1024,1024]{1,0:T(8,128)S(1)} custom-call(s32[1]{0:T(128)} %bitcast.where, s32[8]{0:T(128)S(1)} %copy-done.78, bf16[1024,512]{1,0:T(8,128)(2,1)S(1)} %get-tuple-element.154.q_ref, bf16[1024,512]{1,0:T(8,128)(2,1)S(1)} %broadcast_select_fusion.kv_ref, f32[1024,1024]{1,0:T(8,128)S(1)} %attend.5.rest_0_), custom_call_target="tpu_custom_call" | custom-call | flops 67108864 | bytes 196608 | tf_op jit(solution)/shard_map/attend/pallas_call | solution.py:136
  101.9 6.4 %attend.7.rest_0_ = f32[1024,1024]{1,0:T(8,128)S(1)} custom-call(s32[1]{0:T(128)} %bitcast.where, s32[8]{0:T(128)S(1)} %copy-done.78, bf16[1024,512]{1,0:T(8,128)(2,1)S(1)} %get-tuple-element.154.q_ref, bf16[1024,512]{1,0:T(8,128)(2,1)S(1)} %select_select_fusion.1.kv_ref, f32[1024,1024]{1,0:T(8,128)S(1)} %copy-done.23), custom_call_target="tpu_custom_call" | custom-call | flops 67108864 | bytes 196608 | tf_op jit(solution)/shard_map/attend/pallas_call | solution.py:136
  108.3 14.4 %collective-permute-done.8 = bf16[1024,512]{1,0:T(8,128)(2,1)} collective-permute-done((bf16[1024,512]{1,0:T(8,128)(2,1)S(1)}, bf16[1024,512]{1,0:T(8,128)(2,1)}, u32[]{:S(2)}, u32[]{:S(2)}) %collective-permute-start.8) | collective-permute-done | bytes 1048608 | tf_op jit(solution)/shard_map/ppermute | solution.py:748
  138.4 5.8 %collective-permute-done.10.other_ref = bf16[1024,256]{1,0:T(8,128)(2,1)S(1)} collective-permute-done((bf16[1024,256]{1,0:T(8,128)(2,1)S(1)}, bf16[1024,256]{1,0:T(8,128)(2,1)S(1)}, u32[]{:S(2)}, u32[]{:S(2)}) %collective-permute-start.10) | collective-permute-done | bytes 524320 | tf_op jit(solution)/shard_map/ppermute | solution.py:610
  162.8 17.2 %middle.2 = (bf16[1024,2304]{1,0:T(8,128)(2,1)S(1)}, bf16[1024,2304]{1,0:T(8,128)(2,1)}, bf16[1024,2304]{1,0:T(8,128)(2,1)}, bf16[512,1024]{1,0:T(8,128)(2,1)S(1)}) custom-call(bf16[1024,1024]{1,0:T(8,128)(2,1)S(1)} %get-tuple-element.170.n_ref.a_ref.z_ref, bf16[1024,1024]{1,0:T(8,128)(2,1)S(1)} %bitcast.102, ...), custom_call_target="tpu_custom_call" | custom-call | flops 188743680 | bytes 331776 | tf_op jit(solution)/shard_map/middle/pallas_call | solution.py:539
  181.4 17.4 %middle.3 = (bf16[1024,2304]{1,0:T(8,128)(2,1)S(1)}, bf16[1024,2304]{1,0:T(8,128)(2,1)}, bf16[1024,2304]{1,0:T(8,128)(2,1)}, bf16[512,1024]{1,0:T(8,128)(2,1)S(1)}) custom-call(bf16[1024,1024]{1,0:T(8,128)(2,1)S(1)} %get-tuple-element.170.n_ref.a_ref.z_ref, ...), custom_call_target="tpu_custom_call", output_to_operand_aliasing={{0}: (5, {}), {1}: (6, {}), {2}: (7, {})} | custom-call | flops 188743680 | bytes 331776 | tf_op jit(solution)/shard_map/middle/pallas_call | solution.py:539
  199.5 6.6 %weight_grad.5 = (bf16[2,256,2304]{2,1,0:T(8,128)(2,1)S(1)}, bf16[2,256,2304]{2,1,0:T(8,128)(2,1)}) custom-call(s32[1]{0:T(128)} %bitcast.11.at_ref, bf16[1024,1024]{1,0:T(8,128)(2,1)S(1)} %bitcast.104, bf16[1024,1024]{1,0:T(8,128)(2,1)S(1)} %bitcast.105, bf16[1024,2304]{1,0:T(8,128)(2,1)S(1)} %get-tuple-element.177.b_ref.h_ref), custom_call_target="tpu_custom_call" | custom-call | flops 75497472 | bytes 180224 | tf_op jit(solution)/shard_map/weight_grad/pallas_call | solution.py:589
  210.3 6.6 %weight_grad.7 = (bf16[2,256,2304]{2,1,0:T(8,128)(2,1)S(1)}, bf16[2,256,2304]{2,1,0:T(8,128)(2,1)}) custom-call(s32[1]{0:T(128)} %bitcast.11.at_ref, bf16[1024,1024]{1,0:T(8,128)(2,1)S(1)} %get-tuple-element.170.n_ref.a_ref.z_ref, bf16[1024,1024]{1,0:T(8,128)(2,1)S(1)} %get-tuple-element.170.n_ref.a_ref.z_ref, bf16[1024,2304]{1,0:T(8,128)(2,1)S(1)} %copy-done.14), custom_call_target="tpu_custom_call" | custom-call | flops 75497472 | bytes 180224 | tf_op jit(solution)/shard_map/weight_grad/pallas_call | solution.py:589
  220.8 6.6 %weight_grad.6 = (bf16[2,256,2304]{2,1,0:T(8,128)(2,1)S(1)}, bf16[2,256,2304]{2,1,0:T(8,128)(2,1)}) custom-call(s32[1]{0:T(128)} %bitcast.11.at_ref, bf16[1024,1024]{1,0:T(8,128)(2,1)S(1)} %get-tuple-element.170.n_ref.a_ref.z_ref, bf16[1024,1024]{1,0:T(8,128)(2,1)S(1)} %get-tuple-element.170.n_ref.a_ref.z_ref, bf16[1024,2304]{1,0:T(8,128)(2,1)S(1)} %copy-done.13), custom_call_target="tpu_custom_call" | custom-call | flops 75497472 | bytes 180224 | tf_op jit(solution)/shard_map/weight_grad/pallas_call | solution.py:589
  227.4 6.4 %down.1 = bf16[1024,1024]{1,0:T(8,128)(2,1)} custom-call(bf16[1024,2304]{1,0:T(8,128)(2,1)S(1)} %get-tuple-element.177.b_ref.h_ref, bf16[2304,1024]{1,0:T(8,128)(2,1)S(1)} %bitcast.109), custom_call_target="tpu_custom_call" | custom-call | flops 75497472 | bytes 147456 | tf_op jit(solution)/shard_map/down/pallas_call | solution.py:562
  259.7 14.1 %attend_back.4 = (f32[1024,512]{1,0:T(8,128)S(1)}, bf16[1024,512]{1,0:T(8,128)(2,1)}) custom-call(s32[1]{0:T(128)} %bitcast.where, s32[8]{0:T(128)S(1)} %copy-done.78, bf16[1024,512]{1,0:T(8,128)(2,1)S(1)} %get-tuple-element.154.q_ref, bf16[1024,512]{1,0:T(8,128)(2,1)S(1)} %get-tuple-element.190.do_ref, bf16[1024,512]{1,0:T(8,128)(2,1)S(1)} %copy-done.25, ...), custom_call_target="tpu_custom_call" | custom-call | flops 134217728 | bytes 196608 | tf_op jit(solution)/shard_map/attend_back/pallas_call | solution.py:208
  285.2 13.8 %attend_back.5 = (f32[1024,512]{1,0:T(8,128)S(1)}, bf16[1024,512]{1,0:T(8,128)(2,1)S(1)}) custom-call(s32[1]{0:T(128)} %bitcast.where, s32[8]{0:T(128)S(1)} %copy-done.78, bf16[1024,512]{1,0:T(8,128)(2,1)S(1)} %get-tuple-element.154.q_ref, bf16[1024,512]{1,0:T(8,128)(2,1)S(1)} %get-tuple-element.190.do_ref, bf16[1024,512]{1,0:T(8,128)(2,1)S(1)} %copy-done.27, ...), custom_call_target="tpu_custom_call" | custom-call | flops 134217728 | bytes 196608 | tf_op jit(solution)/shard_map/attend_back/pallas_call | solution.py:208
  317.4 14.1 %attend_back.6 = (f32[1024,512]{1,0:T(8,128)S(1)}, bf16[1024,512]{1,0:T(8,128)(2,1)S(1)}) custom-call(s32[1]{0:T(128)} %bitcast.where, s32[8]{0:T(128)S(1)} %copy-done.78, bf16[1024,512]{1,0:T(8,128)(2,1)S(1)} %get-tuple-element.154.q_ref, bf16[1024,512]{1,0:T(8,128)(2,1)S(1)} %copy-done.11, bf16[1024,512]{1,0:T(8,128)(2,1)S(1)} %copy-done.29, ...), custom_call_target="tpu_custom_call" | custom-call | flops 134217728 | bytes 196608 | tf_op jit(solution)/shard_map/attend_back/pallas_call | solution.py:208
  331.5 8.9 %collective-permute-done.20 = bf16[1024,512]{1,0:T(8,128)(2,1)} collective-permute-done((bf16[1024,512]{1,0:T(8,128)(2,1)}, bf16[1024,512]{1,0:T(8,128)(2,1)}, u32[]{:S(2)}, u32[]{:S(2)}) %collective-permute-start.20) | collective-permute-done | bytes 1048608 | tf_op jit(solution)/shard_map/ppermute | solution.py:829
  345.2 17.0 %collective-permute-start.24 = (bf16[1024,512]{1,0:T(8,128)(2,1)}, bf16[1024,512]{1,0:T(8,128)(2,1)}, u32[]{:S(2)}, u32[]{:S(2)}) collective-permute-start(bf16[1024,512]{1,0:T(8,128)(2,1)} %get-tuple-element.301), channel_id=1, source_target_pairs={{0,2},{2,4},{4,6},{1,3},{3,5},{5,7},{8,10},{10,12},{12,14},{9,11},... | collective-permute-start | bytes 3145736 | tf_op jit(solution)/shard_map/ppermute | solution.py:829
  379.8 19.3 %attend_back.7 = (f32[1024,512]{1,0:T(8,128)S(1)}, f32[1024,512]{1,0:T(8,128)S(1)}) custom-call(s32[1]{0:T(128)} %bitcast.where, s32[8]{0:T(128)S(1)} %copy-done.78, bf16[1024,512]{1,0:T(8,128)(2,1)S(1)} %get-tuple-element.154.q_ref, bf16[1024,512]{1,0:T(8,128)(2,1)S(1)} %copy-done.12, bf16[1024,512]{1,0:T(8,128)(2,1)S(1)} %copy-done.39, ...), custom_call_target="tpu_custom_call" | custom-call | flops 134217728 | bytes 196608 | tf_op jit(solution)/shard_map/attend_back/pallas_call | solution.py:208
  401.9 8.0 %rope_back.1 = (bf16[1024,1024]{1,0:T(8,128)(2,1)}, f32[8,128]{1,0:T(8,128)}) custom-call(f32[1024,512]{1,0:T(8,128)} %copy-done.52, f32[1024,512]{1,0:T(8,128)} %copy-done.50, f32[1024,256]{1,0:T(8,128)} %copy-done.64, f32[1024,128]{1,0:T(8,128)} %get-tuple-element.136.cos_ref, f32[1024,128]{1,0:T(8,128)} %get-tuple-element.137.sin_ref, ...), custom_call_target="tpu_custom_call" | custom-call | flops 13107200 | bytes 163840 | tf_op jit(solution)/shard_map/rope_back/pallas_call | solution.py:488
  431.4 10.7 %collective-permute-done.33 = bf16[1,544]{1,0:T(2,128)(2,1)S(1)} collective-permute-done((bf16[1,544]{1,0:T(2,128)(2,1)S(1)}, bf16[1,544]{1,0:T(2,128)(2,1)S(1)}, u32[]{:S(2)}, u32[]{:S(2)}) %collective-permute-start.33) | collective-permute-done | bytes 1120 | tf_op jit(solution)/shard_map/ppermute | solution.py:620
  444.4 54.3 %all-reduce.11.cloned.1.call-done = (bf16[256,2304]{1,0:T(8,128)(2,1)}, bf16[256,2304]{1,0:T(8,128)(2,1)}) async-done(((bf16[256,2304]{1,0:T(8,128)(2,1)}, bf16[256,2304]{1,0:T(8,128)(2,1)}), (bf16[256,2304]{1,0:T(8,128)(2,1)}, bf16[256,2304]{1,0:T(8,128)(2,1)})) %all-reduce.11.cloned.1.call-update) | async-done | bytes 2359312 | tf_op jit(solution)/shard_map/psum | solution.py:843
  498.8 6.0 %fusion.6 = bf16[1,1024,1024]{2,1,0:T(8,128)(2,1)} fusion(f32[1024,1024]{1,0:T(8,128)} %copy-done.2, bf16[1024,1024]{1,0:T(8,128)(2,1)} %collective-permute-done.23, bf16[1024,1024]{1,0:T(8,128)(2,1)} %down.1), kind=kLoop, calls=%fused_computation.18 | loop fusion | flops 5242880 | bytes 10485760 | tf_op jit(solution)/shard_map/reshape | solution.py:892
  520.5 25.1 %all-reduce.9.cloned.1.call-done = bf16[272,1536]{1,0:T(8,128)(2,1)} async-done(((bf16[272,1536]{1,0:T(8,128)(2,1)}), bf16[272,1536]{1,0:T(8,128)(2,1)}) %all-reduce.9.cloned.1.call-update) | async-done | bytes 835600 | tf_op jit(solution)/shard_map/psum | solution.py:881
  (349 shorter events, 232.9 us)
Async XLA Ops:
  7.2 91.8 %all-gather.5.cloned.1.call-start = ((), (), s32[]{:S(2)}) async-start(), calls=%async_computation | async-start | bytes 11796480 | tf_op jit(solution)/shard_map/all_gather | solution.py:720
  24.9 113.5 %all-gather.9.cloned.1.call-start = ((), (), s32[]{:S(2)}) async-start(), calls=%async_computation.4 | async-start | bytes 2621440 | tf_op jit(solution)/shard_map/all_gather | solution.py:751
  39.7 121.6 %all-gather.7.cloned.1.call-start = ((), (), s32[]{:S(2)}) async-start(), calls=%async_computation.1 | async-start | bytes 5898240 | tf_op jit(solution)/shard_map/all_gather | solution.py:752
  39.8 27.5 %collective-permute-start.4 = (bf16[1024,512]{1,0:T(8,128)(2,1)}, bf16[1024,512]{1,0:T(8,128)(2,1)}, u32[]{:S(2)}, u32[]{:S(2)}) collective-permute-start(bf16[1024,512]{1,0:T(8,128)(2,1)} %copy-done.37), channel_id=1, source_target_pairs={{2,0},{4,2},{6,4},{3,1},{5,3},{7,5},{10,8},{12,10},{14,12},{11,9},... | collective-permute-start | bytes 3145736 | tf_op jit(solution)/shard_map/ppermute | solution.py:748
  41.1 27.4 %collective-permute-start.3 = (bf16[1024,512]{1,0:T(8,128)(2,1)}, bf16[1024,512]{1,0:T(8,128)(2,1)}, u32[]{:S(2)}, u32[]{:S(2)}) collective-permute-start(bf16[1024,512]{1,0:T(8,128)(2,1)} %copy-done.37), channel_id=1, source_target_pairs={{0,2},{2,4},{4,6},{1,3},{3,5},{5,7},{8,10},{10,12},{12,14},{9,11},... | collective-permute-start | bytes 3145736 | tf_op jit(solution)/shard_map/ppermute | solution.py:747
  68.4 333.3 %all-reduce.7.cloned.1.call-start = ((), (), s32[]{:S(2)}) async-start(), calls=%async_computation.2 | async-start | bytes 2359296 | tf_op jit(solution)/shard_map/psum | solution.py:834
  68.5 27.0 %collective-permute-start.6 = (bf16[1024,512]{1,0:T(8,128)(2,1)}, bf16[1024,512]{1,0:T(8,128)(2,1)S(1)}, u32[]{:S(2)}, u32[]{:S(2)}) collective-permute-start(bf16[1024,512]{1,0:T(8,128)(2,1)} %collective-permute-done.4), channel_id=1, source_target_pairs={{2,0},{4,2},{3,1},{5,3},{10,8},{12,10},{11,9},{13,11},{18,16},{20,... | collective-permute-start | bytes 3145736 | tf_op jit(solution)/shard_map/ppermute | solution.py:748
  69.8 25.7 %collective-permute-start.5 = (bf16[1024,512]{1,0:T(8,128)(2,1)}, bf16[1024,512]{1,0:T(8,128)(2,1)}, u32[]{:S(2)}, u32[]{:S(2)}) collective-permute-start(bf16[1024,512]{1,0:T(8,128)(2,1)} %collective-permute-done.3), channel_id=1, source_target_pairs={{2,4},{4,6},{3,5},{5,7},{10,12},{12,14},{11,13},{13,15},{18,20},{2... | collective-permute-start | bytes 3145736 | tf_op jit(solution)/shard_map/ppermute | solution.py:747
  97.1 25.6 %collective-permute-start.8 = (bf16[1024,512]{1,0:T(8,128)(2,1)S(1)}, bf16[1024,512]{1,0:T(8,128)(2,1)}, u32[]{:S(2)}, u32[]{:S(2)}) collective-permute-start(bf16[1024,512]{1,0:T(8,128)(2,1)S(1)} %collective-permute-done.6), channel_id=1, source_target_pairs={{2,0},{3,1},{10,8},{11,9},{18,16},{19,17},{26,24},{27,25}} | collective-permute-start | bytes 3145736 | tf_op jit(solution)/shard_map/ppermute | solution.py:748
  180.0 27.5 %collective-permute-start.12 = (bf16[512,1024]{1,0:T(8,128)(2,1)S(1)}, bf16[512,1024]{1,0:T(8,128)(2,1)S(1)}, u32[]{:S(2)}, u32[]{:S(2)}) collective-permute-start(bf16[512,1024]{1,0:T(8,128)(2,1)S(1)} %get-tuple-element.161.a_ref), channel_id=1, source_target_pairs={{0,1},{1,0},{2,3},{3,2},{4,5},{5,4},{6,7},{7,6},{8,9},{9,8},{10,11... | collective-permute-start | bytes 3145736 | tf_op jit(solution)/shard_map/ppermute | solution.py:610
  198.8 35.0 %collective-permute-start.11 = (bf16[512,1024]{1,0:T(8,128)(2,1)S(1)}, bf16[512,1024]{1,0:T(8,128)(2,1)}, u32[]{:S(2)}, u32[]{:S(2)}) collective-permute-start(bf16[512,1024]{1,0:T(8,128)(2,1)S(1)} %get-tuple-element.166.a_ref), channel_id=1, source_target_pairs={{0,1},{1,0},{2,3},{3,2},{4,5},{5,4},{6,7},{7,6},{8,9},{9,8},{10,11... | collective-permute-start | bytes 3145736 | tf_op jit(solution)/shard_map/ppermute | solution.py:610
  234.3 43.7 %collective-permute-start.16 = (bf16[2,256,2304]{2,1,0:T(8,128)(2,1)}, bf16[2,256,2304]{2,1,0:T(8,128)(2,1)}, u32[]{:S(2)}, u32[]{:S(2)}) collective-permute-start(bf16[2,256,2304]{2,1,0:T(8,128)(2,1)} %get-tuple-element.200), channel_id=1, source_target_pairs={{0,8},{8,0},{16,24},{24,16},{1,9},{9,1},{17,25},{25,17},{2,10},{10... | collective-permute-start | bytes 7077896 | tf_op jit(solution)/shard_map/ppermute | solution.py:615
  240.4 40.2 %collective-permute-start.15 = (bf16[256,2304]{1,0:T(8,128)(2,1)S(1)}, bf16[256,2304]{1,0:T(8,128)(2,1)S(1)}, u32[]{:S(2)}, u32[]{:S(2)}) collective-permute-start(bf16[256,2304]{1,0:T(8,128)(2,1)S(1)} %fusion.8), channel_id=1, source_target_pairs={{0,16},{8,24},{16,0},{24,8},{1,17},{9,25},{17,1},{25,9},{2,18},{10... | collective-permute-start | bytes 3538952 | tf_op jit(solution)/shard_map/ppermute | solution.py:620
  259.1 54.6 %collective-permute-start.19 = (bf16[256,2304]{1,0:T(8,128)(2,1)}, bf16[256,2304]{1,0:T(8,128)(2,1)}, u32[]{:S(2)}, u32[]{:S(2)}) collective-permute-start(bf16[256,2304]{1,0:T(8,128)(2,1)} %fusion.9), channel_id=1, source_target_pairs={{0,16},{8,24},{16,0},{24,8},{1,17},{9,25},{17,1},{25,9},{2,18},{10... | collective-permute-start | bytes 3538952 | tf_op jit(solution)/shard_map/ppermute | solution.py:620
  304.0 27.5 %collective-permute-start.21 = (bf16[1024,512]{1,0:T(8,128)(2,1)}, bf16[1024,512]{1,0:T(8,128)(2,1)}, u32[]{:S(2)}, u32[]{:S(2)}) collective-permute-start(bf16[1024,512]{1,0:T(8,128)(2,1)} %get-tuple-element.298), channel_id=1, source_target_pairs={{4,2},{6,4},{5,3},{7,5},{12,10},{14,12},{13,11},{15,13},{20,18},{2... | collective-permute-start | bytes 3145736 | tf_op jit(solution)/shard_map/ppermute | solution.py:829
  305.7 34.6 %collective-permute-start.20 = (bf16[1024,512]{1,0:T(8,128)(2,1)}, bf16[1024,512]{1,0:T(8,128)(2,1)}, u32[]{:S(2)}, u32[]{:S(2)}) collective-permute-start(bf16[1024,512]{1,0:T(8,128)(2,1)} %get-tuple-element.299), channel_id=1, source_target_pairs={{0,2},{2,4},{1,3},{3,5},{8,10},{10,12},{9,11},{11,13},{16,18},{18,... | collective-permute-start | bytes 3145736 | tf_op jit(solution)/shard_map/ppermute | solution.py:829
  310.7 58.9 %collective-permute-start.22 = (bf16[256,2304]{1,0:T(8,128)(2,1)}, bf16[256,2304]{1,0:T(8,128)(2,1)}, u32[]{:S(2)}, u32[]{:S(2)}) collective-permute-start(bf16[256,2304]{1,0:T(8,128)(2,1)} %fusion.10), channel_id=1, source_target_pairs={{0,16},{8,24},{16,0},{24,8},{1,17},{9,25},{17,1},{25,9},{2,18},{10... | collective-permute-start | bytes 3538952 | tf_op jit(solution)/shard_map/ppermute | solution.py:620
  312.1 89.7 %collective-permute-start.23 = (bf16[1024,1024]{1,0:T(8,128)(2,1)}, bf16[1024,1024]{1,0:T(8,128)(2,1)}, u32[]{:S(2)}, u32[]{:S(2)}) collective-permute-start(bf16[1024,1024]{1,0:T(8,128)(2,1)} %down.1), channel_id=1, source_target_pairs={{0,1},{1,0},{2,3},{3,2},{4,5},{5,4},{6,7},{7,6},{8,9},{9,8},{10,11... | collective-permute-start | bytes 6291464 | tf_op jit(solution)/shard_map/ppermute | solution.py:610
  313.7 185.1 %all-reduce.11.cloned.1.call-start = ((), (), s32[]{:S(2)}) async-start(), calls=%async_computation.5 | async-start | bytes 4718592 | tf_op jit(solution)/shard_map/psum | solution.py:843
  343.9 57.9 %collective-permute-start.25 = (bf16[1024,512]{1,0:T(8,128)(2,1)}, bf16[1024,512]{1,0:T(8,128)(2,1)}, u32[]{:S(2)}, u32[]{:S(2)}) collective-permute-start(bf16[1024,512]{1,0:T(8,128)(2,1)} %get-tuple-element.300), channel_id=1, source_target_pairs={{2,0},{4,2},{6,4},{3,1},{5,3},{7,5},{10,8},{12,10},{14,12},{11,9},... | collective-permute-start | bytes 3145736 | tf_op jit(solution)/shard_map/ppermute | solution.py:829
  345.2 56.6 %collective-permute-start.24 = (bf16[1024,512]{1,0:T(8,128)(2,1)}, bf16[1024,512]{1,0:T(8,128)(2,1)}, u32[]{:S(2)}, u32[]{:S(2)}) collective-permute-start(bf16[1024,512]{1,0:T(8,128)(2,1)} %get-tuple-element.301), channel_id=1, source_target_pairs={{0,2},{2,4},{4,6},{1,3},{3,5},{5,7},{8,10},{10,12},{12,14},{9,11},... | collective-permute-start | bytes 3145736 | tf_op jit(solution)/shard_map/ppermute | solution.py:829
  374.6 48.2 %collective-permute-start.31 = (bf16[256,512]{1,0:T(8,128)(2,1)}, bf16[256,512]{1,0:T(8,128)(2,1)}, u32[]{:S(2)}, u32[]{:S(2)}) collective-permute-start(bf16[256,512]{1,0:T(8,128)(2,1)} %fusion.18), channel_id=1, source_target_pairs={{0,16},{8,24},{16,0},{24,8},{1,17},{9,25},{17,1},{25,9},{2,18},{10... | collective-permute-start | bytes 786440 | tf_op jit(solution)/shard_map/ppermute | solution.py:620
  401.8 143.8 %all-reduce.9.cloned.1.call-start = ((), (), s32[]{:S(2)}) async-start(), calls=%async_computation.3 | async-start | bytes 1671168 | tf_op jit(solution)/shard_map/psum | solution.py:881
  425.0 90.4 %collective-permute-start.27 = (bf16[1024,1024]{1,0:T(8,128)(2,1)}, bf16[1024,1024]{1,0:T(8,128)(2,1)}, u32[]{:S(2)}, u32[]{:S(2)}) collective-permute-start(bf16[1024,1024]{1,0:T(8,128)(2,1)} %get-tuple-element.231.a_ref), channel_id=1, source_target_pairs={{0,1},{1,0},{2,3},{3,2},{4,5},{5,4},{6,7},{7,6},{8,9},{9,8},{10,11... | collective-permute-start | bytes 6291464 | tf_op jit(solution)/shard_map/ppermute | solution.py:610
  (105 other events, 704.4 us)
Sparse Core Ops, SparseCore 0:
  25.0 65.7 all-gather.4
  92.9 22.5 all-gather.8
  117.1 38.0 all-gather.6
  313.8 82.4 all-reduce.6
  401.9 96.8 all-reduce.10
  501.0 44.5 all-reduce.8

commit v3 on v2

--- a/solution.py
+++ b/solution.py
@@ -26,6 +26,10 @@
     return pl.CostEstimate(
         flops=flops // 64, bytes_accessed=bytes_accessed // 64, transcendentals=0
     )
+
+
+def far(x):
+    return pltpu.with_memory_space_constraint(x, pltpu.HBM)
 
 
 def half(shape, which):
@@ -119,17 +123,17 @@
     in_specs = [pair, pair]
     if not first:
         in_specs.append(pl.BlockSpec((rows, 512), lambda g, *_: (0, g + base)))
-        args.append(acc)
+        args.append(far(acc) if m == n_ctx - 2 else acc)
     if last:
         out_shape = (
             jax.ShapeDtypeStruct((rows, pairs * 256), BF16),
-            jax.ShapeDtypeStruct((rows, pairs * 256), F32),
+            pltpu.HBM((rows, pairs * 256), F32),
             jax.ShapeDtypeStruct((pairs, 8, rows), F32),
         )
         out_specs = (slim, slim, pl.BlockSpec((1, 8, rows), lambda g, *_: (g, 0, 0)))
         scratch = [pltpu.VMEM((rows, 512), F32)]
     else:
-        out_shape = jax.ShapeDtypeStruct((rows, pairs * 512), F32)
+        out_shape = (pltpu.HBM if m > 0 else jax.ShapeDtypeStruct)((rows, pairs * 512), F32)
         out_specs = wide
         scratch = []
     work = 2 * block * block * pairs * 4
@@ -143,7 +147,7 @@
             out_specs=out_specs,
             scratch_shapes=scratch,
         ),
-        compiler_params=pltpu.CompilerParams(vmem_limit_bytes=40 << 20),
+        compiler_params=pltpu.CompilerParams(vmem_limit_bytes=24 << 20),
         cost_estimate=cost(work * 1024, 12 << 20),
         name="attend",
     )(*args)
@@ -203,13 +207,13 @@
     args = [*place, q, do, kv, lse, dlt]
     if not first:
         in_specs.append(slim)
-        args.append(dq)
+        args.append(far(dq))
     work = 2 * block * block * pairs * 4
     return pl.pallas_call(
         functools.partial(attend_back_body, m, n_ctx, first, block),
         out_shape=(
-            jax.ShapeDtypeStruct((rows, pairs * 256), F32),
-            jax.ShapeDtypeStruct((rows, pairs * 256), F32 if m == 0 else BF16),
+            pltpu.HBM((rows, pairs * 256), F32),
+            pltpu.HBM((rows, pairs * 256), F32) if m == 0 else jax.ShapeDtypeStruct((rows, pairs * 256), BF16),
         ),
         grid_spec=pltpu.PrefetchScalarGridSpec(
             num_scalar_prefetch=2,
@@ -218,7 +222,7 @@
             out_specs=(slim, slim),
             scratch_shapes=[pltpu.VMEM((rows, 256), F32), pltpu.VMEM((rows, 256), F32)],
         ),
-        compiler_params=pltpu.CompilerParams(vmem_limit_bytes=40 << 20),
+        compiler_params=pltpu.CompilerParams(vmem_limit_bytes=24 << 20),
         cost_estimate=cost(work * 2048, 12 << 20),
         name="attend_back",
     )(*args)
@@ -277,9 +281,13 @@
 
 
 def row_call(body, name, step, rows, ins, outs, flops, scratch=(), aliases=None, first=0, count=None):
+    ins = list(ins)
     spec = lambda w: pl.BlockSpec((step, w), lambda i: (i + first, 0))
     in_specs = []
-    for array, kind in ins:
+    for n, (array, kind) in enumerate(ins):
+        if isinstance(kind, str) and kind.startswith("far "):
+            kind = kind[4:]
+            ins[n] = (far(array), kind)
         if kind == "rows":
             in_specs.append(spec(array.shape[1]))
         elif kind == "part":
@@ -290,13 +298,13 @@
             in_specs.append(kind)
     return pl.pallas_call(
         body,
-        out_shape=tuple(o[0] for o in outs),
+        out_shape=tuple(pltpu.HBM(o[0].shape, o[0].dtype) if len(o) > 2 else o[0] for o in outs),
         grid=(rows // step if count is None else count,),
         in_specs=in_specs,
         out_specs=tuple(spec(o[0].shape[1]) if o[1] is None else o[1] for o in outs),
         scratch_shapes=list(scratch),
         input_output_aliases=aliases or {},
-        compiler_params=pltpu.CompilerParams(vmem_limit_bytes=40 << 20),
+        compiler_params=pltpu.CompilerParams(vmem_limit_bytes=24 << 20),
         cost_estimate=cost(flops, 1 << 20),
         name=name,
     )(*(array for array, _ in ins))
@@ -309,8 +317,8 @@
     part = pl.BlockSpec((f, r, 2 * kw), lambda i: (0, 0, cols // (2 * kw) - 1))
     return row_call(
         key_body, "project_keys", step, rows,
-        [(x, "rows"), (gain, "whole"), (packed, part), (cos, "rows"), (sin, "rows"), (gains, "whole")],
-        [shape(width, BF16), shape(kw, F32), shape(2 * kw, BF16)],
+        [(x, "far rows"), (gain, "whole"), (packed, part), (cos, "far rows"), (sin, "far rows"), (gains, "whole")],
+        [shape(width, BF16) + ("far",), shape(kw, F32) + ("far",), shape(2 * kw, BF16) + ("far",)],
         rows * width * kw * 4,
     )
 
@@ -322,8 +330,8 @@
     part = pl.BlockSpec((f, r, qw), lambda i: (0, 0, 0))
     return row_call(
         query_body, "project_queries", step, rows,
-        [(n, "rows"), (packed, part), (cos, "rows"), (sin, "rows"), (gains, "whole")],
-        [shape(qw, F32), shape(qw, BF16)],
+        [(n, "far rows"), (packed, part), (cos, "far rows"), (sin, "far rows"), (gains, "whole")],
+        [shape(qw, F32) + ("far",), shape(qw, BF16)],
         rows * width * qw * 2,
     )
 
@@ -362,7 +370,7 @@
     flops = rows * width * width
     so_far = []
     for at, (mine, other) in enumerate(zip(own, others)):
-        ins = [(mine, "rows"), (other, "rows"), (w, "whole")]
+        ins = [(mine, "rows"), (other, "far rows"), (w, "whole")]
         held = [(v, "rows") for v in so_far]
         if at < len(own) - 1:
             so_far = row_call(
@@ -370,8 +378,8 @@
             )
     return row_call(
         functools.partial(join_last_body, at), "join_last", step, rows,
-        ins + [(x, "rows"), (gain, "whole")] + held,
-        [shape(width, F32), shape(width, BF16)],
+        ins + [(x, "far rows"), (gain, "whole")] + held,
+        [shape(width, F32) + ("far",), shape(width, BF16)],
         flops,
     )
 
@@ -419,13 +427,13 @@
     own_w = pl.BlockSpec((w.shape[0], wide, w.shape[2]), lambda i: (0, 0, 0))
     shape = lambda w, t: (jax.ShapeDtypeStruct((rows, w), t), None)
     hbm = pl.BlockSpec(memory_space=pl.ANY)
-    base = [(a, "part"), (b, "part"), (resid, "rows"), (dy, "rows"), (gain, "whole"), (w, own_w), (mix, "rows")]
+    base = [(a, "far part"), (b, "far part"), (resid, "far rows"), (dy, "far rows"), (gain, "whole"), (w, own_w), (mix, "far rows")]
     given = list(given or ())
     return row_call(
         functools.partial(into_body, pairs, len(given)), "into_attention", step, rows,
         base + [(g, hbm) for g in given],
         [
-            shape(width, F32), shape(width, BF16), shape(wide, BF16),
+            shape(width, F32) + ("far",), shape(width, BF16) + ("far",), shape(wide, BF16),
             (jax.ShapeDtypeStruct((pairs, 8, rows), F32), pl.BlockSpec((pairs, 8, step), lambda i: (0, 0, i + first))),
             (jax.ShapeDtypeStruct((8, width), F32), pl.BlockSpec((8, width), lambda i: (0, 0))),
         ],
@@ -447,7 +455,7 @@
     rows, width = x.shape
     return row_call(
         leave_body, "leave", step, rows,
-        [(a, "rows"), (b, "rows"), (x, "rows"), (gain, "whole"), (d, "rows")],
+        [(a, "far rows"), (b, "far rows"), (x, "far rows"), (gain, "whole"), (d, "far rows")],
         [(jax.ShapeDtypeStruct((rows, width), F32), None)],
         rows * width * 16,
     )[0]
@@ -495,9 +503,10 @@
         in_specs=[spec(qw), spec(qw), spec(kw), spec(128), spec(128), fixed]
         + [spec(2 * kw)] * len(dkvs),
         out_specs=(spec(qw + 2 * kw), fixed),
+        compiler_params=pltpu.CompilerParams(vmem_limit_bytes=24 << 20),
         cost_estimate=cost(rows * qw * 1600, rows * qw * 20),
         name="rope_back",
-    )(dq, q_raw, k_raw, cos, sin, gains, *dkvs)
+    )(*map(far, (dq, q_raw, k_raw, cos, sin)), gains, far(dkvs[0]), *dkvs[1:])
 
 
 def middle_body(step, aliased, n_ref, dy_ref, wg_ref, wu_ref, wd_ref, *refs):
@@ -545,10 +554,10 @@
         out_specs=(outs, outs, outs, pl.BlockSpec((rows, width), lambda j: (0, 0))),
         scratch_shapes=[pltpu.VMEM((rows, width), F32)],
         input_output_aliases={5 + k: k for k in range(len(given))},
-        compiler_params=pltpu.CompilerParams(vmem_limit_bytes=40 << 20),
+        compiler_params=pltpu.CompilerParams(vmem_limit_bytes=24 << 20),
         cost_estimate=cost(10 * rows * width * hidden, 6 * (rows * hidden + width * hidden)),
         name="middle",
-    )(n, dy, both, both, wd, *given)
+    )(n, far(dy), far(both), far(both), far(wd), *given)
 
 
 def down_body(h_ref, w_ref, out_ref):
@@ -568,7 +577,7 @@
             pl.BlockSpec((hidden, width), lambda j: (0, 0)),
         ],
         out_specs=pl.BlockSpec((tile, width), lambda j: (j, 0)),
-        compiler_params=pltpu.CompilerParams(vmem_limit_bytes=40 << 20),
+        compiler_params=pltpu.CompilerParams(vmem_limit_bytes=24 << 20),
         cost_estimate=cost(2 * rows * width * hidden, 2 * (rows * hidden + width * hidden)),
         name="down",
     )(h, w)
@@ -588,7 +597,7 @@
     out = pl.BlockSpec((1, block, tile), lambda j, i, c: (i, 0, j))
     return pl.pallas_call(
         grad_body,
-        out_shape=(shape, shape),
+        out_shape=(pltpu.HBM(shape.shape, BF16), pltpu.HBM(shape.shape, BF16)),
         grid_spec=pltpu.PrefetchScalarGridSpec(
             num_scalar_prefetch=1,
             grid=(cols // tile, parts // 2),
@@ -599,7 +608,7 @@
             ],
             out_specs=(out, out),
         ),
-        compiler_params=pltpu.CompilerParams(vmem_limit_bytes=40 << 20),
+        compiler_params=pltpu.CompilerParams(vmem_limit_bytes=24 << 20),
         cost_estimate=cost(2 * rows * width * cols, 2 * (rows * width + rows * cols + width * cols)),
         name="weight_grad",
     )(core.reshape(1), a, a, b)

time: 570 us -> 553 us (0.970)
  local copies, waits for them, and re-layouts: 64.8 us -> 17.6 us
  waiting for transfers between devices: 151 us -> 172 us
  Pallas kernels: 198 us -> 216 us
    unnamed x188 -> x110, local copies, waits for them, and re-layouts: 59.7 us -> 13.8 us
    pallas_call x12, Pallas kernels: 55.2 us -> 65.8 us  [the longest x7 39.3 us: row_call(): pl.pallas_call(body, out_shape=tuple((pltpu.HBM(o[0].shape, o[0].dtype) i...]
  transfers between devices with their start and end apart: 40 -> 40, of which waited for: 14 -> 19; matrix products, arithmetic and copies ran while one was open for 12% -> 11% of each run, Pallas kernels for 32% -> 37%
where the time goes in v3:
time: 553 us; the launch traced here: 543 us
  Pallas kernels  216 us (39%)
  waiting for transfers between devices  172 us (31%)
  other arithmetic  59.8 us (11%)
  starting transfers between devices  58.8 us (11%)
  local copies, waits for them, and re-layouts  17.6 us (3%)
  between operations  15.1 us (3%)
    pallas_call x4, Pallas kernels, attend_back(): pl.pallas_call(functools.partial(attend_back_body, m, n_ctx, first, block...  66.7 us
    psum x1, waiting for transfers between devices, per_device(): gate_s, up_s = lax.psum((gate_s, up_s), 'ctx')  59 us
    pallas_call x7, Pallas kernels, row_call(): pl.pallas_call(body, out_shape=tuple((pltpu.HBM(o[0].shape, o[0].dtype) i...  39.3 us
    pallas_call x5, Pallas kernels, attend(): pl.pallas_call(functools.partial(attend_body, m, n_ctx, first, last, bloc...  35.7 us
    ppermute x3, waiting for transfers between devices, per_device(): shards[t] = lax.ppermute(shards[t - 1], 'ctx', left)  35.2 us
    pallas_call x2, Pallas kernels, middle(): pl.pallas_call(functools.partial(middle_body, min(rows, 256), len(given))...  34.5 us
    psum x1, waiting for transfers between devices, per_device(): last = lax.psum(last, 'ctx')  27.1 us
    ppermute x6, starting transfers between devices, per_device(): got[side] = lax.ppermute(send, 'ctx', [(i, i + side) for i in senders])  26.6 us
  transfers between devices with their start and end apart: 40, of which 19 were waited for; matrix products, arithmetic and copies ran while one was open for 11% of the time, Pallas kernels for 37%

profile of v3, /device:TPU:0, one launch (start us, length us, event | category | flops | bytes accessed | tf_op | source)
XLA Modules:
  0.0 543.1 jit_solution(13678486641949807007)
XLA Ops:
  28.7 6.4 %project_keys.1 = (bf16[1024,1024]{1,0:T(8,128)(2,1)}, f32[1024,256]{1,0:T(8,128)}, bf16[1024,512]{1,0:T(8,128)(2,1)}) custom-call(bf16[1024,1024]{1,0:T(8,128)(2,1)} %bitcast.118, f32[8,1024]{1,0:T(8,128)S(1)} %broadcast_in_dim.42.g_ref, bf16[4,272,1024]{2,1,0:T(8,128)(2,1)S(1)} %bitcast.111, f32[1024,128]{1,0:T(8,128)} %get-tuple-element.136.cos_ref, ...), custom_call_target="tpu_custom_call" | custom-call | flops 16777216 | bytes 16384 | tf_op jit(solution)/shard_map/project_keys/pallas_call | solution.py:299
  48.0 14.6 %collective-permute-done.4 = bf16[1024,512]{1,0:T(8,128)(2,1)} collective-permute-done((bf16[1024,512]{1,0:T(8,128)(2,1)}, bf16[1024,512]{1,0:T(8,128)(2,1)}, u32[]{:S(2)}, u32[]{:S(2)}) %collective-permute-start.4) | collective-permute-done | bytes 1048608 | tf_op jit(solution)/shard_map/ppermute | solution.py:757
  68.1 8.6 %attend.5.rest_0_ = f32[1024,1024]{1,0:T(8,128)S(1)} custom-call(s32[1]{0:T(128)} %bitcast.where, s32[8]{0:T(128)S(1)} %copy-done.25, bf16[1024,512]{1,0:T(8,128)(2,1)S(1)} %get-tuple-element.154.q_ref, bf16[1024,512]{1,0:T(8,128)(2,1)S(1)} %copy-done.16), custom_call_target="tpu_custom_call" | custom-call | flops 67108864 | bytes 196608 | tf_op jit(solution)/shard_map/attend/pallas_call | solution.py:140
  78.0 7.4 %attend.6.rest_0_ = f32[1024,1024]{1,0:T(8,128)} custom-call(s32[1]{0:T(128)} %bitcast.where, s32[8]{0:T(128)S(1)} %copy-done.25, bf16[1024,512]{1,0:T(8,128)(2,1)S(1)} %get-tuple-element.154.q_ref, bf16[1024,512]{1,0:T(8,128)(2,1)S(1)} %broadcast_select_fusion.kv_ref, f32[1024,1024]{1,0:T(8,128)S(1)} %attend.5.rest_0_), custom_call_target="tpu_custom_call" | custom-call | flops 67108864 | bytes 196608 | tf_op jit(solution)/shard_map/attend/pallas_call | solution.py:140
  94.2 8.7 %attend.7.rest_0_ = f32[1024,1024]{1,0:T(8,128)} custom-call(s32[1]{0:T(128)} %bitcast.where, s32[8]{0:T(128)S(1)} %copy-done.25, bf16[1024,512]{1,0:T(8,128)(2,1)S(1)} %get-tuple-element.154.q_ref, bf16[1024,512]{1,0:T(8,128)(2,1)S(1)} %select_select_fusion.1.kv_ref, f32[1024,1024]{1,0:T(8,128)} %attend.6.rest_0_), custom_call_target="tpu_custom_call" | custom-call | flops 67108864 | bytes 196608 | tf_op jit(solution)/shard_map/attend/pallas_call | solution.py:140
  102.9 15.2 %collective-permute-done.8 = bf16[1024,512]{1,0:T(8,128)(2,1)} collective-permute-done((bf16[1024,512]{1,0:T(8,128)(2,1)S(1)}, bf16[1024,512]{1,0:T(8,128)(2,1)}, u32[]{:S(2)}, u32[]{:S(2)}) %collective-permute-start.8) | collective-permute-done | bytes 1048608 | tf_op jit(solution)/shard_map/ppermute | solution.py:757
  132.8 7.2 %collective-permute-done.10.other_ref = bf16[1024,256]{1,0:T(8,128)(2,1)S(1)} collective-permute-done((bf16[1024,256]{1,0:T(8,128)(2,1)S(1)}, bf16[1024,256]{1,0:T(8,128)(2,1)S(1)}, u32[]{:S(2)}, u32[]{:S(2)}) %collective-permute-start.10) | collective-permute-done | bytes 524320 | tf_op jit(solution)/shard_map/ppermute | solution.py:619
  155.2 17.2 %middle.2 = (bf16[1024,2304]{1,0:T(8,128)(2,1)S(1)}, bf16[1024,2304]{1,0:T(8,128)(2,1)S(1)}, bf16[1024,2304]{1,0:T(8,128)(2,1)S(1)}, bf16[512,1024]{1,0:T(8,128)(2,1)S(1)}) custom-call(bf16[1024,1024]{1,0:T(8,128)(2,1)S(1)} %get-tuple-element.170.n_ref.a_ref.z_ref, bf16[1024,1024]{1,0:T(8,128)(2,1)} %bitcast.102, ...), custom_call_target="tpu_custom_call" | custom-call | flops 188743680 | bytes 331776 | tf_op jit(solution)/shard_map/middle/pallas_call | solution.py:548
  174.0 17.3 %middle.3 = (bf16[1024,2304]{1,0:T(8,128)(2,1)S(1)}, bf16[1024,2304]{1,0:T(8,128)(2,1)S(1)}, bf16[1024,2304]{1,0:T(8,128)(2,1)S(1)}, bf16[512,1024]{1,0:T(8,128)(2,1)S(1)}) custom-call(bf16[1024,1024]{1,0:T(8,128)(2,1)S(1)} %get-tuple-element.170.n_ref.a_ref.z_ref, ...), custom_call_target="tpu_custom_call", output_to_operand_aliasing={{0}: (5, {}), {1}: (6, {}), {2}: (7, {})} | custom-call | flops 188743680 | bytes 331776 | tf_op jit(solution)/shard_map/middle/pallas_call | solution.py:548
  192.0 6.7 %weight_grad.5 = (bf16[2,256,2304]{2,1,0:T(8,128)(2,1)}, bf16[2,256,2304]{2,1,0:T(8,128)(2,1)}) custom-call(s32[1]{0:T(128)} %bitcast.11.at_ref, bf16[1024,1024]{1,0:T(8,128)(2,1)S(1)} %bitcast.106, bf16[1024,1024]{1,0:T(8,128)(2,1)S(1)} %bitcast.107, bf16[1024,2304]{1,0:T(8,128)(2,1)S(1)} %get-tuple-element.177.b_ref.h_ref), custom_call_target="tpu_custom_call" | custom-call | flops 75497472 | bytes 180224 | tf_op jit(solution)/shard_map/weight_grad/pallas_call | solution.py:598
  198.7 6.7 %weight_grad.7 = (bf16[2,256,2304]{2,1,0:T(8,128)(2,1)}, bf16[2,256,2304]{2,1,0:T(8,128)(2,1)}) custom-call(s32[1]{0:T(128)} %bitcast.11.at_ref, bf16[1024,1024]{1,0:T(8,128)(2,1)S(1)} %get-tuple-element.170.n_ref.a_ref.z_ref, bf16[1024,1024]{1,0:T(8,128)(2,1)S(1)} %get-tuple-element.170.n_ref.a_ref.z_ref, bf16[1024,2304]{1,0:T(8,128)(2,1)S(1)} %get-tuple-element.174.b_ref), custom_call_target="tpu_custom_call" | custom-call | flops 75497472 | bytes 180224 | tf_op jit(solution)/shard_map/weight_grad/pallas_call | solution.py:598
  205.4 6.6 %weight_grad.6 = (bf16[2,256,2304]{2,1,0:T(8,128)(2,1)}, bf16[2,256,2304]{2,1,0:T(8,128)(2,1)}) custom-call(s32[1]{0:T(128)} %bitcast.11.at_ref, bf16[1024,1024]{1,0:T(8,128)(2,1)S(1)} %get-tuple-element.170.n_ref.a_ref.z_ref, bf16[1024,1024]{1,0:T(8,128)(2,1)S(1)} %get-tuple-element.170.n_ref.a_ref.z_ref, bf16[1024,2304]{1,0:T(8,128)(2,1)S(1)} %get-tuple-element.171.b_ref), custom_call_target="tpu_custom_call" | custom-call | flops 75497472 | bytes 180224 | tf_op jit(solution)/shard_map/weight_grad/pallas_call | solution.py:598
  212.0 6.5 %down.1 = bf16[1024,1024]{1,0:T(8,128)(2,1)} custom-call(bf16[1024,2304]{1,0:T(8,128)(2,1)S(1)} %get-tuple-element.177.b_ref.h_ref, bf16[2304,1024]{1,0:T(8,128)(2,1)S(1)} %bitcast.109), custom_call_target="tpu_custom_call" | custom-call | flops 75497472 | bytes 147456 | tf_op jit(solution)/shard_map/down/pallas_call | solution.py:571
  246.3 14.3 %attend_back.4 = (f32[1024,512]{1,0:T(8,128)}, bf16[1024,512]{1,0:T(8,128)(2,1)}) custom-call(s32[1]{0:T(128)} %bitcast.where, s32[8]{0:T(128)S(1)} %copy-done.25, bf16[1024,512]{1,0:T(8,128)(2,1)S(1)} %get-tuple-element.154.q_ref, bf16[1024,512]{1,0:T(8,128)(2,1)S(1)} %get-tuple-element.190.do_ref, bf16[1024,512]{1,0:T(8,128)(2,1)S(1)} %copy-done.9, ...), custom_call_target="tpu_custom_call" | custom-call | flops 134217728 | bytes 196608 | tf_op jit(solution)/shard_map/attend_back/pallas_call | solution.py:212
  272.3 15.5 %attend_back.5 = (f32[1024,512]{1,0:T(8,128)}, bf16[1024,512]{1,0:T(8,128)(2,1)S(1)}) custom-call(s32[1]{0:T(128)} %bitcast.where, s32[8]{0:T(128)S(1)} %copy-done.25, bf16[1024,512]{1,0:T(8,128)(2,1)S(1)} %get-tuple-element.154.q_ref, bf16[1024,512]{1,0:T(8,128)(2,1)S(1)} %get-tuple-element.190.do_ref, bf16[1024,512]{1,0:T(8,128)(2,1)S(1)} %copy-done.11, ...), custom_call_target="tpu_custom_call" | custom-call | flops 134217728 | bytes 196608 | tf_op jit(solution)/shard_map/attend_back/pallas_call | solution.py:212
  304.9 15.7 %attend_back.6 = (f32[1024,512]{1,0:T(8,128)}, bf16[1024,512]{1,0:T(8,128)(2,1)S(1)}) custom-call(s32[1]{0:T(128)} %bitcast.where, s32[8]{0:T(128)S(1)} %copy-done.25, bf16[1024,512]{1,0:T(8,128)(2,1)S(1)} %get-tuple-element.154.q_ref, bf16[1024,512]{1,0:T(8,128)(2,1)S(1)} %get-tuple-element.190.do_ref, bf16[1024,512]{1,0:T(8,128)(2,1)S(1)} %copy-done.13, ...), custom_call_target="tpu_custom_call" | custom-call | flops 134217728 | bytes 196608 | tf_op jit(solution)/shard_map/attend_back/pallas_call | solution.py:212
  320.5 9.4 %collective-permute-done.20 = bf16[1024,512]{1,0:T(8,128)(2,1)} collective-permute-done((bf16[1024,512]{1,0:T(8,128)(2,1)}, bf16[1024,512]{1,0:T(8,128)(2,1)}, u32[]{:S(2)}, u32[]{:S(2)}) %collective-permute-start.20) | collective-permute-done | bytes 1048608 | tf_op jit(solution)/shard_map/ppermute | solution.py:838
  334.9 14.0 %collective-permute-start.24 = (bf16[1024,512]{1,0:T(8,128)(2,1)}, bf16[1024,512]{1,0:T(8,128)(2,1)}, u32[]{:S(2)}, u32[]{:S(2)}) collective-permute-start(bf16[1024,512]{1,0:T(8,128)(2,1)} %get-tuple-element.301), channel_id=1, source_target_pairs={{0,2},{2,4},{4,6},{1,3},{3,5},{5,7},{8,10},{10,12},{12,14},{9,11},... | collective-permute-start | bytes 3145736 | tf_op jit(solution)/shard_map/ppermute | solution.py:838
  359.0 21.2 %attend_back.7 = (f32[1024,512]{1,0:T(8,128)}, f32[1024,512]{1,0:T(8,128)}) custom-call(s32[1]{0:T(128)} %bitcast.where, s32[8]{0:T(128)S(1)} %copy-done.25, bf16[1024,512]{1,0:T(8,128)(2,1)S(1)} %get-tuple-element.154.q_ref, bf16[1024,512]{1,0:T(8,128)(2,1)S(1)} %get-tuple-element.190.do_ref, bf16[1024,512]{1,0:T(8,128)(2,1)S(1)} %copy-done.17, ...), custom_call_target="tpu_custom_call" | custom-call | flops 134217728 | bytes 196608 | tf_op jit(solution)/shard_map/attend_back/pallas_call | solution.py:212
  385.9 6.8 %rope_back.1 = (bf16[1024,1024]{1,0:T(8,128)(2,1)S(1)}, f32[8,128]{1,0:T(8,128)S(1)}) custom-call(f32[1024,512]{1,0:T(8,128)} %get-tuple-element.221.dq_ref, f32[1024,512]{1,0:T(8,128)} %get-tuple-element.224.q_ref, f32[1024,256]{1,0:T(8,128)} %get-tuple-element.225.k_ref, f32[1024,128]{1,0:T(8,128)} %get-tuple-element.136.cos_ref, ...), custom_call_target="tpu_custom_call" | custom-call | flops 13107200 | bytes 163840 | tf_op jit(solution)/shard_map/rope_back/pallas_call | solution.py:496
  410.6 10.7 %collective-permute-done.33 = bf16[1,544]{1,0:T(2,128)(2,1)S(1)} collective-permute-done((bf16[1,544]{1,0:T(2,128)(2,1)S(1)}, bf16[1,544]{1,0:T(2,128)(2,1)S(1)}, u32[]{:S(2)}, u32[]{:S(2)}) %collective-permute-start.33) | collective-permute-done | bytes 1120 | tf_op jit(solution)/shard_map/ppermute | solution.py:629
  423.6 59.0 %all-reduce.11.cloned.1.call-done = (bf16[256,2304]{1,0:T(8,128)(2,1)}, bf16[256,2304]{1,0:T(8,128)(2,1)}) async-done(((bf16[256,2304]{1,0:T(8,128)(2,1)}, bf16[256,2304]{1,0:T(8,128)(2,1)}), (bf16[256,2304]{1,0:T(8,128)(2,1)}, bf16[256,2304]{1,0:T(8,128)(2,1)})) %all-reduce.11.cloned.1.call-update) | async-done | bytes 2359312 | tf_op jit(solution)/shard_map/psum | solution.py:852
  495.2 7.1 %leave.1 = f32[1024,1024]{1,0:T(8,128)} custom-call(bf16[1024,1024]{1,0:T(8,128)(2,1)} %get-tuple-element.231.a_ref, bf16[1024,1024]{1,0:T(8,128)(2,1)} %collective-permute-done.27.b_ref, bf16[1024,1024]{1,0:T(8,128)(2,1)} %bitcast.120, f32[8,1024]{1,0:T(8,128)S(1)} %broadcast_in_dim.42.g_ref, f32[1024,1024]{1,0:T(8,128)} %get-tuple-element.232.d_ref), custom_call_target="tpu_custom_call" | custom-call | flops 262144 | bytes 16384 | tf_op jit(solution)/shard_map/leave/pallas_call | solution.py:299
  502.3 27.1 %all-reduce.9.cloned.1.call-done = bf16[272,1536]{1,0:T(8,128)(2,1)} async-done(((bf16[272,1536]{1,0:T(8,128)(2,1)}), bf16[272,1536]{1,0:T(8,128)(2,1)}) %all-reduce.9.cloned.1.call-update) | async-done | bytes 835600 | tf_op jit(solution)/shard_map/psum | solution.py:890
  (271 shorter events, 197.9 us)
Async XLA Ops:
  7.2 87.0 %all-gather.5.cloned.1.call-start = ((), (), s32[]{:S(2)}) async-start(), calls=%async_computation | async-start | bytes 11796480 | tf_op jit(solution)/shard_map/all_gather | solution.py:729
  24.9 107.8 %all-gather.9.cloned.1.call-start = ((), (), s32[]{:S(2)}) async-start(), calls=%async_computation.4 | async-start | bytes 2621440 | tf_op jit(solution)/shard_map/all_gather | solution.py:760
  35.1 120.1 %all-gather.7.cloned.1.call-start = ((), (), s32[]{:S(2)}) async-start(), calls=%async_computation.1 | async-start | bytes 5898240 | tf_op jit(solution)/shard_map/all_gather | solution.py:761
  35.2 27.5 %collective-permute-start.4 = (bf16[1024,512]{1,0:T(8,128)(2,1)}, bf16[1024,512]{1,0:T(8,128)(2,1)}, u32[]{:S(2)}, u32[]{:S(2)}) collective-permute-start(bf16[1024,512]{1,0:T(8,128)(2,1)} %get-tuple-element.138.kv_ref), channel_id=1, source_target_pairs={{2,0},{4,2},{6,4},{3,1},{5,3},{7,5},{10,8},{12,10},{14,12},{11,9},... | collective-permute-start | bytes 3145736 | tf_op jit(solution)/shard_map/ppermute | solution.py:757
  36.5 27.3 %collective-permute-start.3 = (bf16[1024,512]{1,0:T(8,128)(2,1)}, bf16[1024,512]{1,0:T(8,128)(2,1)}, u32[]{:S(2)}, u32[]{:S(2)}) collective-permute-start(bf16[1024,512]{1,0:T(8,128)(2,1)} %get-tuple-element.138.kv_ref), channel_id=1, source_target_pairs={{0,2},{2,4},{4,6},{1,3},{3,5},{5,7},{8,10},{10,12},{12,14},{9,11},... | collective-permute-start | bytes 3145736 | tf_op jit(solution)/shard_map/ppermute | solution.py:756
  63.8 318.5 %all-reduce.7.cloned.1.call-start = ((), (), s32[]{:S(2)}) async-start(), calls=%async_computation.2 | async-start | bytes 2359296 | tf_op jit(solution)/shard_map/psum | solution.py:843
  63.9 27.0 %collective-permute-start.6 = (bf16[1024,512]{1,0:T(8,128)(2,1)}, bf16[1024,512]{1,0:T(8,128)(2,1)S(1)}, u32[]{:S(2)}, u32[]{:S(2)}) collective-permute-start(bf16[1024,512]{1,0:T(8,128)(2,1)} %collective-permute-done.4), channel_id=1, source_target_pairs={{2,0},{4,2},{3,1},{5,3},{10,8},{12,10},{11,9},{13,11},{18,16},{20,... | collective-permute-start | bytes 3145736 | tf_op jit(solution)/shard_map/ppermute | solution.py:757
  65.2 25.7 %collective-permute-start.5 = (bf16[1024,512]{1,0:T(8,128)(2,1)}, bf16[1024,512]{1,0:T(8,128)(2,1)}, u32[]{:S(2)}, u32[]{:S(2)}) collective-permute-start(bf16[1024,512]{1,0:T(8,128)(2,1)} %collective-permute-done.3), channel_id=1, source_target_pairs={{2,4},{4,6},{3,5},{5,7},{10,12},{12,14},{11,13},{13,15},{18,20},{2... | collective-permute-start | bytes 3145736 | tf_op jit(solution)/shard_map/ppermute | solution.py:756
  172.4 26.2 %collective-permute-start.12 = (bf16[512,1024]{1,0:T(8,128)(2,1)S(1)}, bf16[512,1024]{1,0:T(8,128)(2,1)S(1)}, u32[]{:S(2)}, u32[]{:S(2)}) collective-permute-start(bf16[512,1024]{1,0:T(8,128)(2,1)S(1)} %get-tuple-element.161.a_ref), channel_id=1, source_target_pairs={{0,1},{1,0},{2,3},{3,2},{4,5},{5,4},{6,7},{7,6},{8,9},{9,8},{10,11... | collective-permute-start | bytes 3145736 | tf_op jit(solution)/shard_map/ppermute | solution.py:619
  191.4 29.0 %collective-permute-start.11 = (bf16[512,1024]{1,0:T(8,128)(2,1)S(1)}, bf16[512,1024]{1,0:T(8,128)(2,1)S(1)}, u32[]{:S(2)}, u32[]{:S(2)}) collective-permute-start(bf16[512,1024]{1,0:T(8,128)(2,1)S(1)} %get-tuple-element.166.a_ref), channel_id=1, source_target_pairs={{0,1},{1,0},{2,3},{3,2},{4,5},{5,4},{6,7},{7,6},{8,9},{9,8},{10,11... | collective-permute-start | bytes 3145736 | tf_op jit(solution)/shard_map/ppermute | solution.py:619
  221.8 44.9 %collective-permute-start.16 = (bf16[2,256,2304]{2,1,0:T(8,128)(2,1)}, bf16[2,256,2304]{2,1,0:T(8,128)(2,1)}, u32[]{:S(2)}, u32[]{:S(2)}) collective-permute-start(bf16[2,256,2304]{2,1,0:T(8,128)(2,1)} %get-tuple-element.200), channel_id=1, source_target_pairs={{0,8},{8,0},{16,24},{24,16},{1,9},{9,1},{17,25},{25,17},{2,10},{10... | collective-permute-start | bytes 7077896 | tf_op jit(solution)/shard_map/ppermute | solution.py:624
  228.1 41.3 %collective-permute-start.15 = (bf16[256,2304]{1,0:T(8,128)(2,1)S(1)}, bf16[256,2304]{1,0:T(8,128)(2,1)S(1)}, u32[]{:S(2)}, u32[]{:S(2)}) collective-permute-start(bf16[256,2304]{1,0:T(8,128)(2,1)S(1)} %fusion.8), channel_id=1, source_target_pairs={{0,16},{8,24},{16,0},{24,8},{1,17},{9,25},{17,1},{25,9},{2,18},{10... | collective-permute-start | bytes 3538952 | tf_op jit(solution)/shard_map/ppermute | solution.py:629
  244.5 56.7 %collective-permute-start.19 = (bf16[256,2304]{1,0:T(8,128)(2,1)}, bf16[256,2304]{1,0:T(8,128)(2,1)}, u32[]{:S(2)}, u32[]{:S(2)}) collective-permute-start(bf16[256,2304]{1,0:T(8,128)(2,1)} %fusion.9), channel_id=1, source_target_pairs={{0,16},{8,24},{16,0},{24,8},{1,17},{9,25},{17,1},{25,9},{2,18},{10... | collective-permute-start | bytes 3538952 | tf_op jit(solution)/shard_map/ppermute | solution.py:629
  260.5 27.3 %collective-permute-start.17 = (bf16[1024,512]{1,0:T(8,128)(2,1)}, bf16[1024,512]{1,0:T(8,128)(2,1)}, u32[]{:S(2)}, u32[]{:S(2)}) collective-permute-start(bf16[1024,512]{1,0:T(8,128)(2,1)} %get-tuple-element.195), channel_id=1, source_target_pairs={{0,2},{1,3},{8,10},{9,11},{16,18},{17,19},{24,26},{25,27}} | collective-permute-start | bytes 3145736 | tf_op jit(solution)/shard_map/ppermute | solution.py:838
  292.1 28.5 %collective-permute-start.21 = (bf16[1024,512]{1,0:T(8,128)(2,1)}, bf16[1024,512]{1,0:T(8,128)(2,1)}, u32[]{:S(2)}, u32[]{:S(2)}) collective-permute-start(bf16[1024,512]{1,0:T(8,128)(2,1)} %get-tuple-element.298), channel_id=1, source_target_pairs={{4,2},{6,4},{5,3},{7,5},{12,10},{14,12},{13,11},{15,13},{20,18},{2... | collective-permute-start | bytes 3145736 | tf_op jit(solution)/shard_map/ppermute | solution.py:838
  293.7 36.3 %collective-permute-start.20 = (bf16[1024,512]{1,0:T(8,128)(2,1)}, bf16[1024,512]{1,0:T(8,128)(2,1)}, u32[]{:S(2)}, u32[]{:S(2)}) collective-permute-start(bf16[1024,512]{1,0:T(8,128)(2,1)} %get-tuple-element.299), channel_id=1, source_target_pairs={{0,2},{2,4},{1,3},{3,5},{8,10},{10,12},{9,11},{11,13},{16,18},{18,... | collective-permute-start | bytes 3145736 | tf_op jit(solution)/shard_map/ppermute | solution.py:838
  299.1 54.2 %collective-permute-start.22 = (bf16[256,2304]{1,0:T(8,128)(2,1)}, bf16[256,2304]{1,0:T(8,128)(2,1)}, u32[]{:S(2)}, u32[]{:S(2)}) collective-permute-start(bf16[256,2304]{1,0:T(8,128)(2,1)} %fusion.10), channel_id=1, source_target_pairs={{0,16},{8,24},{16,0},{24,8},{1,17},{9,25},{17,1},{25,9},{2,18},{10... | collective-permute-start | bytes 3538952 | tf_op jit(solution)/shard_map/ppermute | solution.py:629
  299.7 80.5 %collective-permute-start.23 = (bf16[1024,1024]{1,0:T(8,128)(2,1)}, bf16[1024,1024]{1,0:T(8,128)(2,1)}, u32[]{:S(2)}, u32[]{:S(2)}) collective-permute-start(bf16[1024,1024]{1,0:T(8,128)(2,1)} %down.1), channel_id=1, source_target_pairs={{0,1},{1,0},{2,3},{3,2},{4,5},{5,4},{6,7},{7,6},{8,9},{9,8},{10,11... | collective-permute-start | bytes 6291464 | tf_op jit(solution)/shard_map/ppermute | solution.py:619
  301.2 181.4 %all-reduce.11.cloned.1.call-start = ((), (), s32[]{:S(2)}) async-start(), calls=%async_computation.5 | async-start | bytes 4718592 | tf_op jit(solution)/shard_map/psum | solution.py:852
  333.6 51.1 %collective-permute-start.25 = (bf16[1024,512]{1,0:T(8,128)(2,1)}, bf16[1024,512]{1,0:T(8,128)(2,1)}, u32[]{:S(2)}, u32[]{:S(2)}) collective-permute-start(bf16[1024,512]{1,0:T(8,128)(2,1)} %get-tuple-element.300), channel_id=1, source_target_pairs={{2,0},{4,2},{6,4},{3,1},{5,3},{7,5},{10,8},{12,10},{14,12},{11,9},... | collective-permute-start | bytes 3145736 | tf_op jit(solution)/shard_map/ppermute | solution.py:838
  334.9 51.0 %collective-permute-start.24 = (bf16[1024,512]{1,0:T(8,128)(2,1)}, bf16[1024,512]{1,0:T(8,128)(2,1)}, u32[]{:S(2)}, u32[]{:S(2)}) collective-permute-start(bf16[1024,512]{1,0:T(8,128)(2,1)} %get-tuple-element.301), channel_id=1, source_target_pairs={{0,2},{2,4},{4,6},{1,3},{3,5},{5,7},{8,10},{10,12},{12,14},{9,11},... | collective-permute-start | bytes 3145736 | tf_op jit(solution)/shard_map/ppermute | solution.py:838
  358.4 43.6 %collective-permute-start.31 = (bf16[256,512]{1,0:T(8,128)(2,1)}, bf16[256,512]{1,0:T(8,128)(2,1)}, u32[]{:S(2)}, u32[]{:S(2)}) collective-permute-start(bf16[256,512]{1,0:T(8,128)(2,1)} %fusion.18), channel_id=1, source_target_pairs={{0,16},{8,24},{16,0},{24,8},{1,17},{9,25},{17,1},{25,9},{2,18},{10... | collective-permute-start | bytes 786440 | tf_op jit(solution)/shard_map/ppermute | solution.py:629
  382.4 147.0 %all-reduce.9.cloned.1.call-start = ((), (), s32[]{:S(2)}) async-start(), calls=%async_computation.3 | async-start | bytes 1671168 | tf_op jit(solution)/shard_map/psum | solution.py:890
  404.5 90.8 %collective-permute-start.27 = (bf16[1024,1024]{1,0:T(8,128)(2,1)}, bf16[1024,1024]{1,0:T(8,128)(2,1)}, u32[]{:S(2)}, u32[]{:S(2)}) collective-permute-start(bf16[1024,1024]{1,0:T(8,128)(2,1)} %get-tuple-element.231.a_ref), channel_id=1, source_target_pairs={{0,1},{1,0},{2,3},{3,2},{4,5},{5,4},{6,7},{7,6},{8,9},{9,8},{10,11... | collective-permute-start | bytes 6291464 | tf_op jit(solution)/shard_map/ppermute | solution.py:619
  (66 other events, 586.9 us)
Sparse Core Ops, SparseCore 0:
  25.0 65.7 all-gather.4
  92.9 22.6 all-gather.8
  117.1 38.0 all-gather.6
  301.3 81.0 all-reduce.6
  384.6 97.9 all-reduce.10
  484.8 44.5 all-reduce.8

commit v4 on v3

--- a/solution.py
+++ b/solution.py
@@ -840,16 +840,13 @@
             down_other = swap(tie(down_part, dq))
             down_s = y_sums(*down_c)
             sends += [down_s] + up_c[2]
-            down_s = lax.psum(down_s, "ctx")
         if m == max(n_ctx - 2, 1):
             gate_s = y_sums(*gate_c, dq)
             sends.append(gate_s)
             out_g = weight_grad(tie(d_resid_b, dq), mixed_b, n_fsdp, core)
+            down_s, gate_s = lax.psum((down_s, gate_s), "ctx")
         if m == 1:
-            up_s = y_sums(*up_c, dq)
-            sends += [up_s, *out_g]
-            gate_s, up_s, down_s = lax.optimization_barrier((gate_s, up_s, down_s))
-            gate_s, up_s = lax.psum((gate_s, up_s), "ctx")
+            sends += [*out_g]
         dq = tie(dq, *sends)
     dq, down_other = lax.optimization_barrier((dq, down_other))
     out_s = y_sums(*core_sums(*out_g))
@@ -886,8 +883,9 @@
     last = jnp.concatenate([y_sums(*qkv_c), out_s], axis=1)
     small_s = jnp.pad(small_s, ((0, 15), (0, last.shape[1] - small_s.shape[1])))
     last = jnp.concatenate([last, small_s], axis=0)
-    last, gate_s, up_s = lax.optimization_barrier((last, gate_s, up_s))
-    last = lax.psum(last, "ctx")
+    up_s = y_sums(*up_c)
+    last, up_s, gate_s, down_s = lax.optimization_barrier((last, up_s, gate_s, down_s))
+    last, up_s = lax.psum((last, up_s), "ctx")
     input_grad = leave(normed_part, normed_other, x, gain_attn, d_resid, step)
     last = tie(last, input_grad)
     q_s, k_s, v_s = last[:gs, :qw], last[:gs, qw : qw + kw], last[:gs, qw + kw : qkv_w]

time: 553 us -> 547 us (0.989)
  waiting for transfers between devices: 172 us -> 181 us
  starting transfers between devices: 58.8 us -> 50.2 us
  other arithmetic: 59.8 us -> 52.3 us
    psum x3 -> x2, waiting for transfers between devices: 88.3 us -> 110 us  [the longest x1 68.5 us: per_device(): last, up_s = lax.psum((last, up_s), 'ctx')]
    ppermute x6, waiting for transfers between devices: 12.9 us -> 1.72 us  [per_device(): got[side] = lax.ppermute(send, 'ctx', [(i, i + side) for i in senders])]
    ppermute x6, starting transfers between devices: 26.6 us -> 18.6 us  [per_device(): got[side] = lax.ppermute(send, 'ctx', [(i, i + side) for i in senders])]
    unnamed x110 -> x116, local copies, waits for them, and re-layouts: 13.8 us -> 15.8 us
  transfers between devices with their start and end apart: 40 -> 39, of which waited for: 19 -> 18; matrix products, arithmetic and copies ran while one was open for 11% -> 10% of each run, Pallas kernels for 37% -> 37%
where the time goes in v4:
time: 547 us; the launch traced here: 537 us
  Pallas kernels  216 us (39%)
  waiting for transfers between devices  181 us (33%)
  other arithmetic  52.3 us (10%)
  starting transfers between devices  50.2 us (9%)
  local copies, waits for them, and re-layouts  19.7 us (4%)
  between operations  14.7 us (3%)
    psum x1, waiting for transfers between devices, per_device(): last, up_s = lax.psum((last, up_s), 'ctx')  68.5 us
    pallas_call x4, Pallas kernels, attend_back(): pl.pallas_call(functools.partial(attend_back_body, m, n_ctx, first, block...  66.6 us
    psum x1, waiting for transfers between devices, per_device(): down_s, gate_s = lax.psum((down_s, gate_s), 'ctx')  41.8 us
    pallas_call x7, Pallas kernels, row_call(): pl.pallas_call(body, out_shape=tuple((pltpu.HBM(o[0].shape, o[0].dtype) i...  39.3 us
    pallas_call x5, Pallas kernels, attend(): pl.pallas_call(functools.partial(attend_body, m, n_ctx, first, last, bloc...  35.7 us
    ppermute x3, waiting for transfers between devices, per_device(): shards[t] = lax.ppermute(shards[t - 1], 'ctx', left)  35.2 us
    pallas_call x2, Pallas kernels, middle(): pl.pallas_call(functools.partial(middle_body, min(rows, 256), len(given))...  34.5 us
    pallas_call x5, Pallas kernels, weight_grad(): pl.pallas_call(grad_body, out_shape=(pltpu.HBM(shape.shape, BF16), pltpu....  26.1 us
  transfers between devices with their start and end apart: 39, of which 18 were waited for; matrix products, arithmetic and copies ran while one was open for 10% of the time, Pallas kernels for 37%

profile of v4, /device:TPU:0, one launch (start us, length us, event | category | flops | bytes accessed | tf_op | source)
XLA Modules:
  0.0 537.0 jit_solution(5093673108621850526)
XLA Ops:
  28.7 6.4 %project_keys.1 = (bf16[1024,1024]{1,0:T(8,128)(2,1)}, f32[1024,256]{1,0:T(8,128)}, bf16[1024,512]{1,0:T(8,128)(2,1)}) custom-call(bf16[1024,1024]{1,0:T(8,128)(2,1)} %bitcast.118, f32[8,1024]{1,0:T(8,128)S(1)} %broadcast_in_dim.42.g_ref, bf16[4,272,1024]{2,1,0:T(8,128)(2,1)S(1)} %bitcast.111, f32[1024,128]{1,0:T(8,128)} %get-tuple-element.134.cos_ref, ...), custom_call_target="tpu_custom_call" | custom-call | flops 16777216 | bytes 16384 | tf_op jit(solution)/shard_map/project_keys/pallas_call | solution.py:299
  42.0 6.0 %project_queries.1 = (f32[1024,512]{1,0:T(8,128)}, bf16[1024,512]{1,0:T(8,128)(2,1)S(1)}) custom-call(bf16[1024,1024]{1,0:T(8,128)(2,1)} %get-tuple-element.138.n_ref.a_ref.z_ref, bf16[4,272,1024]{2,1,0:T(8,128)(2,1)S(1)} %bitcast.112, f32[1024,128]{1,0:T(8,128)} %get-tuple-element.134.cos_ref, f32[1024,128]{1,0:T(8,128)} %get-tuple-element.135.sin_ref, ...), custom_call_target="tpu_custom_call" | custom-call | flops 16777216 | bytes 16384 | tf_op jit(solution)/shard_map/project_queries/pallas_call | solution.py:299
  48.0 14.6 %collective-permute-done.4 = bf16[1024,512]{1,0:T(8,128)(2,1)} collective-permute-done((bf16[1024,512]{1,0:T(8,128)(2,1)}, bf16[1024,512]{1,0:T(8,128)(2,1)}, u32[]{:S(2)}, u32[]{:S(2)}) %collective-permute-start.4) | collective-permute-done | bytes 1048608 | tf_op jit(solution)/shard_map/ppermute | solution.py:757
  68.1 8.6 %attend.5.rest_0_ = f32[1024,1024]{1,0:T(8,128)S(1)} custom-call(s32[1]{0:T(128)} %bitcast.where, s32[8]{0:T(128)S(1)} %copy-done.27, bf16[1024,512]{1,0:T(8,128)(2,1)S(1)} %get-tuple-element.152.q_ref, bf16[1024,512]{1,0:T(8,128)(2,1)S(1)} %copy-done.16), custom_call_target="tpu_custom_call" | custom-call | flops 67108864 | bytes 196608 | tf_op jit(solution)/shard_map/attend/pallas_call | solution.py:140
  78.0 7.4 %attend.6.rest_0_ = f32[1024,1024]{1,0:T(8,128)} custom-call(s32[1]{0:T(128)} %bitcast.where, s32[8]{0:T(128)S(1)} %copy-done.27, bf16[1024,512]{1,0:T(8,128)(2,1)S(1)} %get-tuple-element.152.q_ref, bf16[1024,512]{1,0:T(8,128)(2,1)S(1)} %broadcast_select_fusion.kv_ref, f32[1024,1024]{1,0:T(8,128)S(1)} %attend.5.rest_0_), custom_call_target="tpu_custom_call" | custom-call | flops 67108864 | bytes 196608 | tf_op jit(solution)/shard_map/attend/pallas_call | solution.py:140
  94.2 8.7 %attend.7.rest_0_ = f32[1024,1024]{1,0:T(8,128)} custom-call(s32[1]{0:T(128)} %bitcast.where, s32[8]{0:T(128)S(1)} %copy-done.27, bf16[1024,512]{1,0:T(8,128)(2,1)S(1)} %get-tuple-element.152.q_ref, bf16[1024,512]{1,0:T(8,128)(2,1)S(1)} %select_select_fusion.1.kv_ref, f32[1024,1024]{1,0:T(8,128)} %attend.6.rest_0_), custom_call_target="tpu_custom_call" | custom-call | flops 67108864 | bytes 196608 | tf_op jit(solution)/shard_map/attend/pallas_call | solution.py:140
  102.9 15.2 %collective-permute-done.8 = bf16[1024,512]{1,0:T(8,128)(2,1)} collective-permute-done((bf16[1024,512]{1,0:T(8,128)(2,1)S(1)}, bf16[1024,512]{1,0:T(8,128)(2,1)}, u32[]{:S(2)}, u32[]{:S(2)}) %collective-permute-start.8) | collective-permute-done | bytes 1048608 | tf_op jit(solution)/shard_map/ppermute | solution.py:757
  132.8 7.2 %collective-permute-done.10.other_ref = bf16[1024,256]{1,0:T(8,128)(2,1)S(1)} collective-permute-done((bf16[1024,256]{1,0:T(8,128)(2,1)S(1)}, bf16[1024,256]{1,0:T(8,128)(2,1)S(1)}, u32[]{:S(2)}, u32[]{:S(2)}) %collective-permute-start.10) | collective-permute-done | bytes 524320 | tf_op jit(solution)/shard_map/ppermute | solution.py:619
  155.2 17.2 %middle.2 = (bf16[1024,2304]{1,0:T(8,128)(2,1)S(1)}, bf16[1024,2304]{1,0:T(8,128)(2,1)S(1)}, bf16[1024,2304]{1,0:T(8,128)(2,1)S(1)}, bf16[512,1024]{1,0:T(8,128)(2,1)S(1)}) custom-call(bf16[1024,1024]{1,0:T(8,128)(2,1)S(1)} %get-tuple-element.168.n_ref.a_ref.z_ref, bf16[1024,1024]{1,0:T(8,128)(2,1)} %bitcast.102, ...), custom_call_target="tpu_custom_call" | custom-call | flops 188743680 | bytes 331776 | tf_op jit(solution)/shard_map/middle/pallas_call | solution.py:548
  174.0 17.3 %middle.3 = (bf16[1024,2304]{1,0:T(8,128)(2,1)S(1)}, bf16[1024,2304]{1,0:T(8,128)(2,1)S(1)}, bf16[1024,2304]{1,0:T(8,128)(2,1)S(1)}, bf16[512,1024]{1,0:T(8,128)(2,1)S(1)}) custom-call(bf16[1024,1024]{1,0:T(8,128)(2,1)S(1)} %get-tuple-element.168.n_ref.a_ref.z_ref, ...), custom_call_target="tpu_custom_call", output_to_operand_aliasing={{0}: (5, {}), {1}: (6, {}), {2}: (7, {})} | custom-call | flops 188743680 | bytes 331776 | tf_op jit(solution)/shard_map/middle/pallas_call | solution.py:548
  192.0 6.6 %weight_grad.5 = (bf16[2,256,2304]{2,1,0:T(8,128)(2,1)}, bf16[2,256,2304]{2,1,0:T(8,128)(2,1)}) custom-call(s32[1]{0:T(128)} %bitcast.11.at_ref, bf16[1024,1024]{1,0:T(8,128)(2,1)S(1)} %bitcast.106, bf16[1024,1024]{1,0:T(8,128)(2,1)S(1)} %bitcast.107, bf16[1024,2304]{1,0:T(8,128)(2,1)S(1)} %get-tuple-element.175.b_ref.h_ref), custom_call_target="tpu_custom_call" | custom-call | flops 75497472 | bytes 180224 | tf_op jit(solution)/shard_map/weight_grad/pallas_call | solution.py:598
  198.6 6.6 %weight_grad.7 = (bf16[2,256,2304]{2,1,0:T(8,128)(2,1)}, bf16[2,256,2304]{2,1,0:T(8,128)(2,1)}) custom-call(s32[1]{0:T(128)} %bitcast.11.at_ref, bf16[1024,1024]{1,0:T(8,128)(2,1)S(1)} %get-tuple-element.168.n_ref.a_ref.z_ref, bf16[1024,1024]{1,0:T(8,128)(2,1)S(1)} %get-tuple-element.168.n_ref.a_ref.z_ref, bf16[1024,2304]{1,0:T(8,128)(2,1)S(1)} %get-tuple-element.172.b_ref), custom_call_target="tpu_custom_call" | custom-call | flops 75497472 | bytes 180224 | tf_op jit(solution)/shard_map/weight_grad/pallas_call | solution.py:598
  205.3 6.7 %weight_grad.6 = (bf16[2,256,2304]{2,1,0:T(8,128)(2,1)}, bf16[2,256,2304]{2,1,0:T(8,128)(2,1)}) custom-call(s32[1]{0:T(128)} %bitcast.11.at_ref, bf16[1024,1024]{1,0:T(8,128)(2,1)S(1)} %get-tuple-element.168.n_ref.a_ref.z_ref, bf16[1024,1024]{1,0:T(8,128)(2,1)S(1)} %get-tuple-element.168.n_ref.a_ref.z_ref, bf16[1024,2304]{1,0:T(8,128)(2,1)S(1)} %get-tuple-element.169.b_ref), custom_call_target="tpu_custom_call" | custom-call | flops 75497472 | bytes 180224 | tf_op jit(solution)/shard_map/weight_grad/pallas_call | solution.py:598
  211.9 6.5 %down.1 = bf16[1024,1024]{1,0:T(8,128)(2,1)} custom-call(bf16[1024,2304]{1,0:T(8,128)(2,1)S(1)} %get-tuple-element.175.b_ref.h_ref, bf16[2304,1024]{1,0:T(8,128)(2,1)S(1)} %bitcast.109), custom_call_target="tpu_custom_call" | custom-call | flops 75497472 | bytes 147456 | tf_op jit(solution)/shard_map/down/pallas_call | solution.py:571
  245.4 14.0 %attend_back.4 = (f32[1024,512]{1,0:T(8,128)}, bf16[1024,512]{1,0:T(8,128)(2,1)S(1)}) custom-call(s32[1]{0:T(128)} %bitcast.where, s32[8]{0:T(128)S(1)} %copy-done.27, bf16[1024,512]{1,0:T(8,128)(2,1)S(1)} %get-tuple-element.152.q_ref, bf16[1024,512]{1,0:T(8,128)(2,1)S(1)} %get-tuple-element.188.do_ref, bf16[1024,512]{1,0:T(8,128)(2,1)S(1)} %copy-done.9, ...), custom_call_target="tpu_custom_call" | custom-call | flops 134217728 | bytes 196608 | tf_op jit(solution)/shard_map/attend_back/pallas_call | solution.py:212
  269.3 15.5 %attend_back.5 = (f32[1024,512]{1,0:T(8,128)}, bf16[1024,512]{1,0:T(8,128)(2,1)S(1)}) custom-call(s32[1]{0:T(128)} %bitcast.where, s32[8]{0:T(128)S(1)} %copy-done.27, bf16[1024,512]{1,0:T(8,128)(2,1)S(1)} %get-tuple-element.152.q_ref, bf16[1024,512]{1,0:T(8,128)(2,1)S(1)} %get-tuple-element.188.do_ref, bf16[1024,512]{1,0:T(8,128)(2,1)S(1)} %copy-done.11, ...), custom_call_target="tpu_custom_call" | custom-call | flops 134217728 | bytes 196608 | tf_op jit(solution)/shard_map/attend_back/pallas_call | solution.py:212
  298.6 15.7 %attend_back.6 = (f32[1024,512]{1,0:T(8,128)}, bf16[1024,512]{1,0:T(8,128)(2,1)S(1)}) custom-call(s32[1]{0:T(128)} %bitcast.where, s32[8]{0:T(128)S(1)} %copy-done.27, bf16[1024,512]{1,0:T(8,128)(2,1)S(1)} %get-tuple-element.152.q_ref, bf16[1024,512]{1,0:T(8,128)(2,1)S(1)} %get-tuple-element.188.do_ref, bf16[1024,512]{1,0:T(8,128)(2,1)S(1)} %copy-done.13, ...), custom_call_target="tpu_custom_call" | custom-call | flops 134217728 | bytes 196608 | tf_op jit(solution)/shard_map/attend_back/pallas_call | solution.py:212
  319.1 6.4 %collective-permute-start.23 = (bf16[1024,512]{1,0:T(8,128)(2,1)}, bf16[1024,512]{1,0:T(8,128)(2,1)}, u32[]{:S(2)}, u32[]{:S(2)}) collective-permute-start(bf16[1024,512]{1,0:T(8,128)(2,1)} %get-tuple-element.299), channel_id=1, source_target_pairs={{0,2},{2,4},{4,6},{1,3},{3,5},{5,7},{8,10},{10,12},{12,14},{9,11},... | collective-permute-start | bytes 3145736 | tf_op jit(solution)/shard_map/ppermute | solution.py:838
  334.4 21.4 %attend_back.7 = (f32[1024,512]{1,0:T(8,128)}, f32[1024,512]{1,0:T(8,128)}) custom-call(s32[1]{0:T(128)} %bitcast.where, s32[8]{0:T(128)S(1)} %copy-done.27, bf16[1024,512]{1,0:T(8,128)(2,1)S(1)} %get-tuple-element.152.q_ref, bf16[1024,512]{1,0:T(8,128)(2,1)S(1)} %get-tuple-element.188.do_ref, bf16[1024,512]{1,0:T(8,128)(2,1)S(1)} %copy-done.17, ...), custom_call_target="tpu_custom_call" | custom-call | flops 134217728 | bytes 196608 | tf_op jit(solution)/shard_map/attend_back/pallas_call | solution.py:212
  357.2 6.9 %rope_back.1 = (bf16[1024,1024]{1,0:T(8,128)(2,1)S(1)}, f32[8,128]{1,0:T(8,128)S(1)}) custom-call(f32[1024,512]{1,0:T(8,128)} %get-tuple-element.216.dq_ref, f32[1024,512]{1,0:T(8,128)} %get-tuple-element.219.q_ref, f32[1024,256]{1,0:T(8,128)} %get-tuple-element.220.k_ref, f32[1024,128]{1,0:T(8,128)} %get-tuple-element.134.cos_ref, ...), custom_call_target="tpu_custom_call" | custom-call | flops 13107200 | bytes 163840 | tf_op jit(solution)/shard_map/rope_back/pallas_call | solution.py:496
  383.2 10.0 %collective-permute-done.32 = bf16[1,544]{1,0:T(2,128)(2,1)S(1)} collective-permute-done((bf16[1,544]{1,0:T(2,128)(2,1)S(1)}, bf16[1,544]{1,0:T(2,128)(2,1)S(1)}, u32[]{:S(2)}, u32[]{:S(2)}) %collective-permute-start.32) | collective-permute-done | bytes 1120 | tf_op jit(solution)/shard_map/ppermute | solution.py:629
  394.4 41.8 %all-reduce.9.cloned.1.call-done = (bf16[256,2304]{1,0:T(8,128)(2,1)}, bf16[256,2304]{1,0:T(8,128)(2,1)}) async-done(((bf16[256,2304]{1,0:T(8,128)(2,1)}, bf16[256,2304]{1,0:T(8,128)(2,1)}), (bf16[256,2304]{1,0:T(8,128)(2,1)}, bf16[256,2304]{1,0:T(8,128)(2,1)})) %all-reduce.9.cloned.1.call-update) | async-done | bytes 2359312 | tf_op jit(solution)/shard_map/psum | solution.py:847
  446.4 7.1 %leave.1 = f32[1024,1024]{1,0:T(8,128)} custom-call(bf16[1024,1024]{1,0:T(8,128)(2,1)} %get-tuple-element.226.a_ref, bf16[1024,1024]{1,0:T(8,128)(2,1)} %collective-permute-done.26.b_ref, bf16[1024,1024]{1,0:T(8,128)(2,1)} %bitcast.120, f32[8,1024]{1,0:T(8,128)S(1)} %broadcast_in_dim.42.g_ref, f32[1024,1024]{1,0:T(8,128)} %get-tuple-element.227.d_ref), custom_call_target="tpu_custom_call" | custom-call | flops 262144 | bytes 16384 | tf_op jit(solution)/shard_map/leave/pallas_call | solution.py:299
  453.5 68.5 %all-reduce.7.cloned.1.call-done = (bf16[272,1536]{1,0:T(8,128)(2,1)}, bf16[256,2304]{1,0:T(8,128)(2,1)}) async-done(((bf16[272,1536]{1,0:T(8,128)(2,1)}, bf16[256,2304]{1,0:T(8,128)(2,1)}), (bf16[272,1536]{1,0:T(8,128)(2,1)}, bf16[256,2304]{1,0:T(8,128)(2,1)})) %all-reduce.7.cloned.1.call-update) | async-done | bytes 2015248 | tf_op jit(solution)/shard_map/psum | solution.py:888
  (274 shorter events, 179.8 us)
Async XLA Ops:
  7.2 87.0 %all-gather.5.cloned.1.call-start = ((), (), s32[]{:S(2)}) async-start(), calls=%async_computation | async-start | bytes 11796480 | tf_op jit(solution)/shard_map/all_gather | solution.py:729
  24.9 107.9 %all-gather.9.cloned.1.call-start = ((), (), s32[]{:S(2)}) async-start(), calls=%async_computation.2 | async-start | bytes 2621440 | tf_op jit(solution)/shard_map/all_gather | solution.py:760
  35.1 120.1 %all-gather.7.cloned.1.call-start = ((), (), s32[]{:S(2)}) async-start(), calls=%async_computation.1 | async-start | bytes 5898240 | tf_op jit(solution)/shard_map/all_gather | solution.py:761
  35.2 27.5 %collective-permute-start.4 = (bf16[1024,512]{1,0:T(8,128)(2,1)}, bf16[1024,512]{1,0:T(8,128)(2,1)}, u32[]{:S(2)}, u32[]{:S(2)}) collective-permute-start(bf16[1024,512]{1,0:T(8,128)(2,1)} %get-tuple-element.136.kv_ref), channel_id=1, source_target_pairs={{2,0},{4,2},{6,4},{3,1},{5,3},{7,5},{10,8},{12,10},{14,12},{11,9},... | collective-permute-start | bytes 3145736 | tf_op jit(solution)/shard_map/ppermute | solution.py:757
  36.5 27.3 %collective-permute-start.3 = (bf16[1024,512]{1,0:T(8,128)(2,1)}, bf16[1024,512]{1,0:T(8,128)(2,1)}, u32[]{:S(2)}, u32[]{:S(2)}) collective-permute-start(bf16[1024,512]{1,0:T(8,128)(2,1)} %get-tuple-element.136.kv_ref), channel_id=1, source_target_pairs={{0,2},{2,4},{4,6},{1,3},{3,5},{5,7},{8,10},{10,12},{12,14},{9,11},... | collective-permute-start | bytes 3145736 | tf_op jit(solution)/shard_map/ppermute | solution.py:756
  63.8 372.4 %all-reduce.9.cloned.1.call-start = ((), (), s32[]{:S(2)}) async-start(), calls=%async_computation.4 | async-start | bytes 4718592 | tf_op jit(solution)/shard_map/psum | solution.py:847
  63.9 27.0 %collective-permute-start.6 = (bf16[1024,512]{1,0:T(8,128)(2,1)}, bf16[1024,512]{1,0:T(8,128)(2,1)S(1)}, u32[]{:S(2)}, u32[]{:S(2)}) collective-permute-start(bf16[1024,512]{1,0:T(8,128)(2,1)} %collective-permute-done.4), channel_id=1, source_target_pairs={{2,0},{4,2},{3,1},{5,3},{10,8},{12,10},{11,9},{13,11},{18,16},{20,... | collective-permute-start | bytes 3145736 | tf_op jit(solution)/shard_map/ppermute | solution.py:757
  65.2 25.7 %collective-permute-start.5 = (bf16[1024,512]{1,0:T(8,128)(2,1)}, bf16[1024,512]{1,0:T(8,128)(2,1)}, u32[]{:S(2)}, u32[]{:S(2)}) collective-permute-start(bf16[1024,512]{1,0:T(8,128)(2,1)} %collective-permute-done.3), channel_id=1, source_target_pairs={{2,4},{4,6},{3,5},{5,7},{10,12},{12,14},{11,13},{13,15},{18,20},{2... | collective-permute-start | bytes 3145736 | tf_op jit(solution)/shard_map/ppermute | solution.py:756
  92.5 25.6 %collective-permute-start.8 = (bf16[1024,512]{1,0:T(8,128)(2,1)S(1)}, bf16[1024,512]{1,0:T(8,128)(2,1)}, u32[]{:S(2)}, u32[]{:S(2)}) collective-permute-start(bf16[1024,512]{1,0:T(8,128)(2,1)S(1)} %collective-permute-done.6), channel_id=1, source_target_pairs={{2,0},{3,1},{10,8},{11,9},{18,16},{19,17},{26,24},{27,25}} | collective-permute-start | bytes 3145736 | tf_op jit(solution)/shard_map/ppermute | solution.py:757
  172.4 26.2 %collective-permute-start.12 = (bf16[512,1024]{1,0:T(8,128)(2,1)S(1)}, bf16[512,1024]{1,0:T(8,128)(2,1)S(1)}, u32[]{:S(2)}, u32[]{:S(2)}) collective-permute-start(bf16[512,1024]{1,0:T(8,128)(2,1)S(1)} %get-tuple-element.159.a_ref), channel_id=1, source_target_pairs={{0,1},{1,0},{2,3},{3,2},{4,5},{5,4},{6,7},{7,6},{8,9},{9,8},{10,11... | collective-permute-start | bytes 3145736 | tf_op jit(solution)/shard_map/ppermute | solution.py:619
  191.4 29.0 %collective-permute-start.11 = (bf16[512,1024]{1,0:T(8,128)(2,1)S(1)}, bf16[512,1024]{1,0:T(8,128)(2,1)S(1)}, u32[]{:S(2)}, u32[]{:S(2)}) collective-permute-start(bf16[512,1024]{1,0:T(8,128)(2,1)S(1)} %get-tuple-element.164.a_ref), channel_id=1, source_target_pairs={{0,1},{1,0},{2,3},{3,2},{4,5},{5,4},{6,7},{7,6},{8,9},{9,8},{10,11... | collective-permute-start | bytes 3145736 | tf_op jit(solution)/shard_map/ppermute | solution.py:619
  221.8 41.9 %collective-permute-start.16 = (bf16[2,256,2304]{2,1,0:T(8,128)(2,1)}, bf16[2,256,2304]{2,1,0:T(8,128)(2,1)}, u32[]{:S(2)}, u32[]{:S(2)}) collective-permute-start(bf16[2,256,2304]{2,1,0:T(8,128)(2,1)} %get-tuple-element.198), channel_id=1, source_target_pairs={{0,8},{8,0},{16,24},{24,16},{1,9},{9,1},{17,25},{25,17},{2,10},{10... | collective-permute-start | bytes 7077896 | tf_op jit(solution)/shard_map/ppermute | solution.py:624
  228.1 38.3 %collective-permute-start.15 = (bf16[256,2304]{1,0:T(8,128)(2,1)S(1)}, bf16[256,2304]{1,0:T(8,128)(2,1)S(1)}, u32[]{:S(2)}, u32[]{:S(2)}) collective-permute-start(bf16[256,2304]{1,0:T(8,128)(2,1)S(1)} %fusion.8), channel_id=1, source_target_pairs={{0,16},{8,24},{16,0},{24,8},{1,17},{9,25},{17,1},{25,9},{2,18},{10... | collective-permute-start | bytes 3538952 | tf_op jit(solution)/shard_map/ppermute | solution.py:629
  243.6 52.1 %collective-permute-start.19 = (bf16[256,2304]{1,0:T(8,128)(2,1)S(1)}, bf16[256,2304]{1,0:T(8,128)(2,1)S(1)}, u32[]{:S(2)}, u32[]{:S(2)}) collective-permute-start(bf16[256,2304]{1,0:T(8,128)(2,1)S(1)} %fusion.9), channel_id=1, source_target_pairs={{0,16},{8,24},{16,0},{24,8},{1,17},{9,25},{17,1},{25,9},{2,18},{10... | collective-permute-start | bytes 3538952 | tf_op jit(solution)/shard_map/ppermute | solution.py:629
  259.4 25.7 %collective-permute-start.17 = (bf16[1024,512]{1,0:T(8,128)(2,1)S(1)}, bf16[1024,512]{1,0:T(8,128)(2,1)S(1)}, u32[]{:S(2)}, u32[]{:S(2)}) collective-permute-start(bf16[1024,512]{1,0:T(8,128)(2,1)S(1)} %get-tuple-element.193), channel_id=1, source_target_pairs={{0,2},{1,3},{8,10},{9,11},{16,18},{17,19},{24,26},{25,27}} | collective-permute-start | bytes 3145736 | tf_op jit(solution)/shard_map/ppermute | solution.py:838
  287.0 27.2 %collective-permute-start.21 = (bf16[1024,512]{1,0:T(8,128)(2,1)}, bf16[1024,512]{1,0:T(8,128)(2,1)}, u32[]{:S(2)}, u32[]{:S(2)}) collective-permute-start(bf16[1024,512]{1,0:T(8,128)(2,1)} %get-tuple-element.296), channel_id=1, source_target_pairs={{4,2},{6,4},{5,3},{7,5},{12,10},{14,12},{13,11},{15,13},{20,18},{2... | collective-permute-start | bytes 3145736 | tf_op jit(solution)/shard_map/ppermute | solution.py:838
  288.7 25.6 %collective-permute-start.20 = (bf16[1024,512]{1,0:T(8,128)(2,1)}, bf16[1024,512]{1,0:T(8,128)(2,1)}, u32[]{:S(2)}, u32[]{:S(2)}) collective-permute-start(bf16[1024,512]{1,0:T(8,128)(2,1)} %get-tuple-element.297), channel_id=1, source_target_pairs={{0,2},{2,4},{1,3},{3,5},{8,10},{10,12},{9,11},{11,13},{16,18},{18,... | collective-permute-start | bytes 3145736 | tf_op jit(solution)/shard_map/ppermute | solution.py:838
  293.7 38.0 %collective-permute-start.33 = (bf16[256,2304]{1,0:T(8,128)(2,1)}, bf16[256,2304]{1,0:T(8,128)(2,1)}, u32[]{:S(2)}, u32[]{:S(2)}) collective-permute-start(bf16[256,2304]{1,0:T(8,128)(2,1)} %fusion.10), channel_id=1, source_target_pairs={{0,16},{8,24},{16,0},{24,8},{1,17},{9,25},{17,1},{25,9},{2,18},{10... | collective-permute-start | bytes 3538952 | tf_op jit(solution)/shard_map/ppermute | solution.py:629
  294.2 61.6 %collective-permute-start.22 = (bf16[1024,1024]{1,0:T(8,128)(2,1)}, bf16[1024,1024]{1,0:T(8,128)(2,1)}, u32[]{:S(2)}, u32[]{:S(2)}) collective-permute-start(bf16[1024,1024]{1,0:T(8,128)(2,1)} %down.1), channel_id=1, source_target_pairs={{0,1},{1,0},{2,3},{3,2},{4,5},{5,4},{6,7},{7,6},{8,9},{9,8},{10,11... | collective-permute-start | bytes 6291464 | tf_op jit(solution)/shard_map/ppermute | solution.py:619
  317.8 39.4 %collective-permute-start.24 = (bf16[1024,512]{1,0:T(8,128)(2,1)}, bf16[1024,512]{1,0:T(8,128)(2,1)}, u32[]{:S(2)}, u32[]{:S(2)}) collective-permute-start(bf16[1024,512]{1,0:T(8,128)(2,1)} %get-tuple-element.298), channel_id=1, source_target_pairs={{2,0},{4,2},{6,4},{3,1},{5,3},{7,5},{10,8},{12,10},{14,12},{11,9},... | collective-permute-start | bytes 3145736 | tf_op jit(solution)/shard_map/ppermute | solution.py:838
  319.1 38.1 %collective-permute-start.23 = (bf16[1024,512]{1,0:T(8,128)(2,1)}, bf16[1024,512]{1,0:T(8,128)(2,1)}, u32[]{:S(2)}, u32[]{:S(2)}) collective-permute-start(bf16[1024,512]{1,0:T(8,128)(2,1)} %get-tuple-element.299), channel_id=1, source_target_pairs={{0,2},{2,4},{4,6},{1,3},{3,5},{5,7},{8,10},{10,12},{12,14},{9,11},... | collective-permute-start | bytes 3145736 | tf_op jit(solution)/shard_map/ppermute | solution.py:838
  331.7 190.3 %all-reduce.7.cloned.1.call-start = ((), (), s32[]{:S(2)}) async-start(), calls=%async_computation.3 | async-start | bytes 4030464 | tf_op jit(solution)/shard_map/psum | solution.py:888
  333.7 44.6 %collective-permute-start.30 = (bf16[256,512]{1,0:T(8,128)(2,1)}, bf16[256,512]{1,0:T(8,128)(2,1)}, u32[]{:S(2)}, u32[]{:S(2)}) collective-permute-start(bf16[256,512]{1,0:T(8,128)(2,1)} %fusion.18), channel_id=1, source_target_pairs={{0,16},{8,24},{16,0},{24,8},{1,17},{9,25},{17,1},{25,9},{2,18},{10... | collective-permute-start | bytes 786440 | tf_op jit(solution)/shard_map/ppermute | solution.py:629
  382.5 63.9 %collective-permute-start.26 = (bf16[1024,1024]{1,0:T(8,128)(2,1)}, bf16[1024,1024]{1,0:T(8,128)(2,1)}, u32[]{:S(2)}, u32[]{:S(2)}) collective-permute-start(bf16[1024,1024]{1,0:T(8,128)(2,1)} %get-tuple-element.226.a_ref), channel_id=1, source_target_pairs={{0,1},{1,0},{2,3},{3,2},{4,5},{5,4},{6,7},{7,6},{8,9},{9,8},{10,11... | collective-permute-start | bytes 6291464 | tf_op jit(solution)/shard_map/ppermute | solution.py:619
  (68 other events, 521.3 us)
Sparse Core Ops, SparseCore 0:
  25.0 65.7 all-gather.4
  92.9 22.6 all-gather.8
  117.1 38.0 all-gather.6
  331.8 104.4 all-reduce.8
  438.6 83.3 all-reduce.6

commit v5 on v4

--- a/solution.py
+++ b/solution.py
@@ -854,7 +854,8 @@
     output = (tie(resid, dq) + (down_part.astype(F32) + down_other.astype(F32))).astype(BF16)
 
     d_qkv, head_gain = rope_back(dq, q_raw, k_raw, cos, sin, gains, home, step)
-    qkv_c = core_sums(*weight_grad(normed_b, d_qkv, n_fsdp, core))
+    qkv_p = weight_grad(normed_b, d_qkv, n_fsdp, core)
+    qkv_c = core_sums(*lax.optimization_barrier((*qkv_p, gate_s))[:2])
     w_qkv = packed[:, :gs].reshape(n_fsdp * gs, qkv_w)
     normed_part = mm(d_qkv, w_qkv, NT)
 

time: 547 us -> 544 us (level)
  waiting for transfers between devices: 181 us -> 161 us
  starting transfers between devices: 50.2 us -> 66.4 us
    psum x1, waiting for transfers between devices: 41.8 us -> 12.8 us  [per_device(): down_s, gate_s = lax.psum((down_s, gate_s), 'ctx')]
    psum x1, waiting for transfers between devices: 68.5 us -> 42.9 us  [per_device(): last, up_s = lax.psum((last, up_s), 'ctx')]
    ppermute x8, waiting for transfers between devices: 10.4 us -> 35.8 us  [swap(): return lax.ppermute(x, 'tp', [(i, i ^ 1) for i in range(n)])]
    ppermute x6, starting transfers between devices: 18.6 us -> 34.5 us  [per_device(): got[side] = lax.ppermute(send, 'ctx', [(i, i + side) for i in senders])]
    ppermute x6, waiting for transfers between devices: 1.72 us -> 12.8 us  [per_device(): got[side] = lax.ppermute(send, 'ctx', [(i, i + side) for i in senders])]
    unnamed x116 -> x114, local copies, waits for them, and re-layouts: 15.8 us -> 16.9 us
  transfers between devices with their start and end apart: 39 -> 39, of which waited for: 18 -> 19; matrix products, arithmetic and copies ran while one was open for 10% -> 10% of each run, Pallas kernels for 37% -> 37%
where the time goes in v5:
time: 544 us; the launch traced here: 535 us
  Pallas kernels  215 us (40%)
  waiting for transfers between devices  161 us (30%)
  starting transfers between devices  66.4 us (12%)
  other arithmetic  52.4 us (10%)
  local copies, waits for them, and re-layouts  20.8 us (4%)
  between operations  14.7 us (3%)
    pallas_call x4, Pallas kernels, attend_back(): pl.pallas_call(functools.partial(attend_back_body, m, n_ctx, first, block...  66.3 us
    psum x1, waiting for transfers between devices, per_device(): last, up_s = lax.psum((last, up_s), 'ctx')  42.9 us
    pallas_call x7, Pallas kernels, row_call(): pl.pallas_call(body, out_shape=tuple((pltpu.HBM(o[0].shape, o[0].dtype) i...  39.3 us
    ppermute x8, waiting for transfers between devices, swap(): return lax.ppermute(x, 'tp', [(i, i ^ 1) for i in range(n)])  35.8 us
    pallas_call x5, Pallas kernels, attend(): pl.pallas_call(functools.partial(attend_body, m, n_ctx, first, last, bloc...  35.6 us
    ppermute x3, waiting for transfers between devices, per_device(): shards[t] = lax.ppermute(shards[t - 1], 'ctx', left)  35.3 us
    pallas_call x2, Pallas kernels, middle(): pl.pallas_call(functools.partial(middle_body, min(rows, 256), len(given))...  34.5 us
    ppermute x6, starting transfers between devices, per_device(): got[side] = lax.ppermute(send, 'ctx', [(i, i + side) for i in senders])  34.5 us
  transfers between devices with their start and end apart: 39, of which 19 were waited for; matrix products, arithmetic and copies ran while one was open for 10% of the time, Pallas kernels for 37%

profile of v5, /device:TPU:0, one launch (start us, length us, event | category | flops | bytes accessed | tf_op | source)
XLA Modules:
  0.0 534.9 jit_solution(11786945636201659621)
XLA Ops:
  48.0 14.6 %collective-permute-done.4 = bf16[1024,512]{1,0:T(8,128)(2,1)} collective-permute-done((bf16[1024,512]{1,0:T(8,128)(2,1)}, bf16[1024,512]{1,0:T(8,128)(2,1)}, u32[]{:S(2)}, u32[]{:S(2)}) %collective-permute-start.4) | collective-permute-done | bytes 1048608 | tf_op jit(solution)/shard_map/ppermute | solution.py:757
  68.0 8.6 %attend.5.rest_0_ = f32[1024,1024]{1,0:T(8,128)S(1)} custom-call(s32[1]{0:T(128)} %bitcast.where, s32[8]{0:T(128)S(1)} %copy-done.27, bf16[1024,512]{1,0:T(8,128)(2,1)S(1)} %get-tuple-element.154.q_ref, bf16[1024,512]{1,0:T(8,128)(2,1)S(1)} %copy-done.16), custom_call_target="tpu_custom_call" | custom-call | flops 67108864 | bytes 196608 | tf_op jit(solution)/shard_map/attend/pallas_call | solution.py:140
  78.0 7.4 %attend.6.rest_0_ = f32[1024,1024]{1,0:T(8,128)} custom-call(s32[1]{0:T(128)} %bitcast.where, s32[8]{0:T(128)S(1)} %copy-done.27, bf16[1024,512]{1,0:T(8,128)(2,1)S(1)} %get-tuple-element.154.q_ref, bf16[1024,512]{1,0:T(8,128)(2,1)S(1)} %broadcast_select_fusion.kv_ref, f32[1024,1024]{1,0:T(8,128)S(1)} %attend.5.rest_0_), custom_call_target="tpu_custom_call" | custom-call | flops 67108864 | bytes 196608 | tf_op jit(solution)/shard_map/attend/pallas_call | solution.py:140
  94.2 8.7 %attend.7.rest_0_ = f32[1024,1024]{1,0:T(8,128)} custom-call(s32[1]{0:T(128)} %bitcast.where, s32[8]{0:T(128)S(1)} %copy-done.27, bf16[1024,512]{1,0:T(8,128)(2,1)S(1)} %get-tuple-element.154.q_ref, bf16[1024,512]{1,0:T(8,128)(2,1)S(1)} %select_select_fusion.1.kv_ref, f32[1024,1024]{1,0:T(8,128)} %attend.6.rest_0_), custom_call_target="tpu_custom_call" | custom-call | flops 67108864 | bytes 196608 | tf_op jit(solution)/shard_map/attend/pallas_call | solution.py:140
  102.9 15.2 %collective-permute-done.8 = bf16[1024,512]{1,0:T(8,128)(2,1)} collective-permute-done((bf16[1024,512]{1,0:T(8,128)(2,1)S(1)}, bf16[1024,512]{1,0:T(8,128)(2,1)}, u32[]{:S(2)}, u32[]{:S(2)}) %collective-permute-start.8) | collective-permute-done | bytes 1048608 | tf_op jit(solution)/shard_map/ppermute | solution.py:757
  132.7 7.3 %collective-permute-done.10.other_ref = bf16[1024,256]{1,0:T(8,128)(2,1)S(1)} collective-permute-done((bf16[1024,256]{1,0:T(8,128)(2,1)S(1)}, bf16[1024,256]{1,0:T(8,128)(2,1)S(1)}, u32[]{:S(2)}, u32[]{:S(2)}) %collective-permute-start.10) | collective-permute-done | bytes 524320 | tf_op jit(solution)/shard_map/ppermute | solution.py:619
  155.2 17.2 %middle.2 = (bf16[1024,2304]{1,0:T(8,128)(2,1)S(1)}, bf16[1024,2304]{1,0:T(8,128)(2,1)S(1)}, bf16[1024,2304]{1,0:T(8,128)(2,1)S(1)}, bf16[512,1024]{1,0:T(8,128)(2,1)S(1)}) custom-call(bf16[1024,1024]{1,0:T(8,128)(2,1)S(1)} %get-tuple-element.170.n_ref.a_ref.z_ref, bf16[1024,1024]{1,0:T(8,128)(2,1)} %bitcast.102, ...), custom_call_target="tpu_custom_call" | custom-call | flops 188743680 | bytes 331776 | tf_op jit(solution)/shard_map/middle/pallas_call | solution.py:548
  174.0 17.3 %middle.3 = (bf16[1024,2304]{1,0:T(8,128)(2,1)S(1)}, bf16[1024,2304]{1,0:T(8,128)(2,1)S(1)}, bf16[1024,2304]{1,0:T(8,128)(2,1)S(1)}, bf16[512,1024]{1,0:T(8,128)(2,1)S(1)}) custom-call(bf16[1024,1024]{1,0:T(8,128)(2,1)S(1)} %get-tuple-element.170.n_ref.a_ref.z_ref, ...), custom_call_target="tpu_custom_call", output_to_operand_aliasing={{0}: (5, {}), {1}: (6, {}), {2}: (7, {})} | custom-call | flops 188743680 | bytes 331776 | tf_op jit(solution)/shard_map/middle/pallas_call | solution.py:548
  192.0 6.6 %weight_grad.5 = (bf16[2,256,2304]{2,1,0:T(8,128)(2,1)}, bf16[2,256,2304]{2,1,0:T(8,128)(2,1)}) custom-call(s32[1]{0:T(128)} %bitcast.11.at_ref, bf16[1024,1024]{1,0:T(8,128)(2,1)S(1)} %bitcast.106, bf16[1024,1024]{1,0:T(8,128)(2,1)S(1)} %bitcast.107, bf16[1024,2304]{1,0:T(8,128)(2,1)S(1)} %get-tuple-element.177.b_ref.h_ref), custom_call_target="tpu_custom_call" | custom-call | flops 75497472 | bytes 180224 | tf_op jit(solution)/shard_map/weight_grad/pallas_call | solution.py:598
  198.6 6.6 %weight_grad.7 = (bf16[2,256,2304]{2,1,0:T(8,128)(2,1)}, bf16[2,256,2304]{2,1,0:T(8,128)(2,1)}) custom-call(s32[1]{0:T(128)} %bitcast.11.at_ref, bf16[1024,1024]{1,0:T(8,128)(2,1)S(1)} %get-tuple-element.170.n_ref.a_ref.z_ref, bf16[1024,1024]{1,0:T(8,128)(2,1)S(1)} %get-tuple-element.170.n_ref.a_ref.z_ref, bf16[1024,2304]{1,0:T(8,128)(2,1)S(1)} %get-tuple-element.174.b_ref), custom_call_target="tpu_custom_call" | custom-call | flops 75497472 | bytes 180224 | tf_op jit(solution)/shard_map/weight_grad/pallas_call | solution.py:598
  205.3 6.6 %weight_grad.6 = (bf16[2,256,2304]{2,1,0:T(8,128)(2,1)}, bf16[2,256,2304]{2,1,0:T(8,128)(2,1)}) custom-call(s32[1]{0:T(128)} %bitcast.11.at_ref, bf16[1024,1024]{1,0:T(8,128)(2,1)S(1)} %get-tuple-element.170.n_ref.a_ref.z_ref, bf16[1024,1024]{1,0:T(8,128)(2,1)S(1)} %get-tuple-element.170.n_ref.a_ref.z_ref, bf16[1024,2304]{1,0:T(8,128)(2,1)S(1)} %get-tuple-element.171.b_ref), custom_call_target="tpu_custom_call" | custom-call | flops 75497472 | bytes 180224 | tf_op jit(solution)/shard_map/weight_grad/pallas_call | solution.py:598
  211.9 6.5 %down.1 = bf16[1024,1024]{1,0:T(8,128)(2,1)} custom-call(bf16[1024,2304]{1,0:T(8,128)(2,1)S(1)} %get-tuple-element.177.b_ref.h_ref, bf16[2304,1024]{1,0:T(8,128)(2,1)S(1)} %bitcast.109), custom_call_target="tpu_custom_call" | custom-call | flops 75497472 | bytes 147456 | tf_op jit(solution)/shard_map/down/pallas_call | solution.py:571
  245.4 14.0 %attend_back.4 = (f32[1024,512]{1,0:T(8,128)}, bf16[1024,512]{1,0:T(8,128)(2,1)S(1)}) custom-call(s32[1]{0:T(128)} %bitcast.where, s32[8]{0:T(128)S(1)} %copy-done.27, bf16[1024,512]{1,0:T(8,128)(2,1)S(1)} %get-tuple-element.154.q_ref, bf16[1024,512]{1,0:T(8,128)(2,1)S(1)} %get-tuple-element.190.do_ref, bf16[1024,512]{1,0:T(8,128)(2,1)S(1)} %copy-done.9, ...), custom_call_target="tpu_custom_call" | custom-call | flops 134217728 | bytes 196608 | tf_op jit(solution)/shard_map/attend_back/pallas_call | solution.py:212
  269.2 15.7 %attend_back.5 = (f32[1024,512]{1,0:T(8,128)}, bf16[1024,512]{1,0:T(8,128)(2,1)S(1)}) custom-call(s32[1]{0:T(128)} %bitcast.where, s32[8]{0:T(128)S(1)} %copy-done.27, bf16[1024,512]{1,0:T(8,128)(2,1)S(1)} %get-tuple-element.154.q_ref, bf16[1024,512]{1,0:T(8,128)(2,1)S(1)} %get-tuple-element.190.do_ref, bf16[1024,512]{1,0:T(8,128)(2,1)S(1)} %copy-done.11, ...), custom_call_target="tpu_custom_call" | custom-call | flops 134217728 | bytes 196608 | tf_op jit(solution)/shard_map/attend_back/pallas_call | solution.py:212
  299.8 15.3 %attend_back.6 = (f32[1024,512]{1,0:T(8,128)}, bf16[1024,512]{1,0:T(8,128)(2,1)S(1)}) custom-call(s32[1]{0:T(128)} %bitcast.where, s32[8]{0:T(128)S(1)} %copy-done.27, bf16[1024,512]{1,0:T(8,128)(2,1)S(1)} %get-tuple-element.154.q_ref, bf16[1024,512]{1,0:T(8,128)(2,1)S(1)} %get-tuple-element.190.do_ref, bf16[1024,512]{1,0:T(8,128)(2,1)S(1)} %copy-done.13, ...), custom_call_target="tpu_custom_call" | custom-call | flops 134217728 | bytes 196608 | tf_op jit(solution)/shard_map/attend_back/pallas_call | solution.py:212
  315.0 11.5 %collective-permute-done.20 = bf16[1024,512]{1,0:T(8,128)(2,1)} collective-permute-done((bf16[1024,512]{1,0:T(8,128)(2,1)}, bf16[1024,512]{1,0:T(8,128)(2,1)}, u32[]{:S(2)}, u32[]{:S(2)}) %collective-permute-start.20) | collective-permute-done | bytes 1048608 | tf_op jit(solution)/shard_map/ppermute | solution.py:838
  331.4 22.3 %collective-permute-start.23 = (bf16[1024,512]{1,0:T(8,128)(2,1)}, bf16[1024,512]{1,0:T(8,128)(2,1)}, u32[]{:S(2)}, u32[]{:S(2)}) collective-permute-start(bf16[1024,512]{1,0:T(8,128)(2,1)} %get-tuple-element.303), channel_id=1, source_target_pairs={{0,2},{2,4},{4,6},{1,3},{3,5},{5,7},{8,10},{10,12},{12,14},{9,11},... | collective-permute-start | bytes 3145736 | tf_op jit(solution)/shard_map/ppermute | solution.py:838
  362.0 21.3 %attend_back.7 = (f32[1024,512]{1,0:T(8,128)}, f32[1024,512]{1,0:T(8,128)}) custom-call(s32[1]{0:T(128)} %bitcast.where, s32[8]{0:T(128)S(1)} %copy-done.27, bf16[1024,512]{1,0:T(8,128)(2,1)S(1)} %get-tuple-element.154.q_ref, bf16[1024,512]{1,0:T(8,128)(2,1)S(1)} %get-tuple-element.190.do_ref, bf16[1024,512]{1,0:T(8,128)(2,1)S(1)} %copy-done.17, ...), custom_call_target="tpu_custom_call" | custom-call | flops 134217728 | bytes 196608 | tf_op jit(solution)/shard_map/attend_back/pallas_call | solution.py:212
  384.4 6.9 %rope_back.1 = (bf16[1024,1024]{1,0:T(8,128)(2,1)S(1)}, f32[8,128]{1,0:T(8,128)S(1)}) custom-call(f32[1024,512]{1,0:T(8,128)} %get-tuple-element.218.dq_ref, f32[1024,512]{1,0:T(8,128)} %get-tuple-element.221.q_ref, f32[1024,256]{1,0:T(8,128)} %get-tuple-element.222.k_ref, f32[1024,128]{1,0:T(8,128)} %get-tuple-element.136.cos_ref, ...), custom_call_target="tpu_custom_call" | custom-call | flops 13107200 | bytes 163840 | tf_op jit(solution)/shard_map/rope_back/pallas_call | solution.py:496
  401.8 12.8 %all-reduce.9.cloned.1.call-done = (bf16[256,2304]{1,0:T(8,128)(2,1)}, bf16[256,2304]{1,0:T(8,128)(2,1)}) async-done(((bf16[256,2304]{1,0:T(8,128)(2,1)}, bf16[256,2304]{1,0:T(8,128)(2,1)}), (bf16[256,2304]{1,0:T(8,128)(2,1)}, bf16[256,2304]{1,0:T(8,128)(2,1)})) %all-reduce.9.cloned.1.call-update) | async-done | bytes 2359312 | tf_op jit(solution)/shard_map/psum | solution.py:847
  423.9 9.1 %collective-permute-done.32 = bf16[1,544]{1,0:T(2,128)(2,1)S(1)} collective-permute-done((bf16[1,544]{1,0:T(2,128)(2,1)S(1)}, bf16[1,544]{1,0:T(2,128)(2,1)S(1)}, u32[]{:S(2)}, u32[]{:S(2)}) %collective-permute-start.32) | collective-permute-done | bytes 1120 | tf_op jit(solution)/shard_map/ppermute | solution.py:629
  444.5 25.4 %collective-permute-done.26.b_ref = bf16[1024,1024]{1,0:T(8,128)(2,1)} collective-permute-done((bf16[1024,1024]{1,0:T(8,128)(2,1)}, bf16[1024,1024]{1,0:T(8,128)(2,1)}, u32[]{:S(2)}, u32[]{:S(2)}) %collective-permute-start.26) | collective-permute-done | bytes 2097184 | tf_op jit(solution)/shard_map/ppermute | solution.py:619
  469.9 7.0 %leave.1 = f32[1024,1024]{1,0:T(8,128)} custom-call(bf16[1024,1024]{1,0:T(8,128)(2,1)} %get-tuple-element.228.a_ref, bf16[1024,1024]{1,0:T(8,128)(2,1)} %collective-permute-done.26.b_ref, bf16[1024,1024]{1,0:T(8,128)(2,1)} %bitcast.120, f32[8,1024]{1,0:T(8,128)S(1)} %broadcast_in_dim.42.g_ref, f32[1024,1024]{1,0:T(8,128)} %get-tuple-element.229.d_ref), custom_call_target="tpu_custom_call" | custom-call | flops 262144 | bytes 16384 | tf_op jit(solution)/shard_map/leave/pallas_call | solution.py:299
  476.9 42.9 %all-reduce.7.cloned.1.call-done = (bf16[272,1536]{1,0:T(8,128)(2,1)}, bf16[256,2304]{1,0:T(8,128)(2,1)}) async-done(((bf16[272,1536]{1,0:T(8,128)(2,1)}, bf16[256,2304]{1,0:T(8,128)(2,1)}), (bf16[272,1536]{1,0:T(8,128)(2,1)}, bf16[256,2304]{1,0:T(8,128)(2,1)})) %all-reduce.7.cloned.1.call-update) | async-done | bytes 2015248 | tf_op jit(solution)/shard_map/psum | solution.py:889
  (272 shorter events, 193.2 us)
Async XLA Ops:
  7.2 87.0 %all-gather.5.cloned.1.call-start = ((), (), s32[]{:S(2)}) async-start(), calls=%async_computation | async-start | bytes 11796480 | tf_op jit(solution)/shard_map/all_gather | solution.py:729
  24.9 107.8 %all-gather.9.cloned.1.call-start = ((), (), s32[]{:S(2)}) async-start(), calls=%async_computation.2 | async-start | bytes 2621440 | tf_op jit(solution)/shard_map/all_gather | solution.py:760
  35.1 120.1 %all-gather.7.cloned.1.call-start = ((), (), s32[]{:S(2)}) async-start(), calls=%async_computation.1 | async-start | bytes 5898240 | tf_op jit(solution)/shard_map/all_gather | solution.py:761
  35.2 27.5 %collective-permute-start.4 = (bf16[1024,512]{1,0:T(8,128)(2,1)}, bf16[1024,512]{1,0:T(8,128)(2,1)}, u32[]{:S(2)}, u32[]{:S(2)}) collective-permute-start(bf16[1024,512]{1,0:T(8,128)(2,1)} %get-tuple-element.138.kv_ref), channel_id=1, source_target_pairs={{2,0},{4,2},{6,4},{3,1},{5,3},{7,5},{10,8},{12,10},{14,12},{11,9},... | collective-permute-start | bytes 3145736 | tf_op jit(solution)/shard_map/ppermute | solution.py:757
  36.5 27.3 %collective-permute-start.3 = (bf16[1024,512]{1,0:T(8,128)(2,1)}, bf16[1024,512]{1,0:T(8,128)(2,1)}, u32[]{:S(2)}, u32[]{:S(2)}) collective-permute-start(bf16[1024,512]{1,0:T(8,128)(2,1)} %get-tuple-element.138.kv_ref), channel_id=1, source_target_pairs={{0,2},{2,4},{4,6},{1,3},{3,5},{5,7},{8,10},{10,12},{12,14},{9,11},... | collective-permute-start | bytes 3145736 | tf_op jit(solution)/shard_map/ppermute | solution.py:756
  63.8 350.8 %all-reduce.9.cloned.1.call-start = ((), (), s32[]{:S(2)}) async-start(), calls=%async_computation.4 | async-start | bytes 4718592 | tf_op jit(solution)/shard_map/psum | solution.py:847
  63.9 27.0 %collective-permute-start.6 = (bf16[1024,512]{1,0:T(8,128)(2,1)}, bf16[1024,512]{1,0:T(8,128)(2,1)S(1)}, u32[]{:S(2)}, u32[]{:S(2)}) collective-permute-start(bf16[1024,512]{1,0:T(8,128)(2,1)} %collective-permute-done.4), channel_id=1, source_target_pairs={{2,0},{4,2},{3,1},{5,3},{10,8},{12,10},{11,9},{13,11},{18,16},{20,... | collective-permute-start | bytes 3145736 | tf_op jit(solution)/shard_map/ppermute | solution.py:757
  65.2 25.7 %collective-permute-start.5 = (bf16[1024,512]{1,0:T(8,128)(2,1)}, bf16[1024,512]{1,0:T(8,128)(2,1)}, u32[]{:S(2)}, u32[]{:S(2)}) collective-permute-start(bf16[1024,512]{1,0:T(8,128)(2,1)} %collective-permute-done.3), channel_id=1, source_target_pairs={{2,4},{4,6},{3,5},{5,7},{10,12},{12,14},{11,13},{13,15},{18,20},{2... | collective-permute-start | bytes 3145736 | tf_op jit(solution)/shard_map/ppermute | solution.py:756
  92.5 25.6 %collective-permute-start.8 = (bf16[1024,512]{1,0:T(8,128)(2,1)S(1)}, bf16[1024,512]{1,0:T(8,128)(2,1)}, u32[]{:S(2)}, u32[]{:S(2)}) collective-permute-start(bf16[1024,512]{1,0:T(8,128)(2,1)S(1)} %collective-permute-done.6), channel_id=1, source_target_pairs={{2,0},{3,1},{10,8},{11,9},{18,16},{19,17},{26,24},{27,25}} | collective-permute-start | bytes 3145736 | tf_op jit(solution)/shard_map/ppermute | solution.py:757
  172.5 26.2 %collective-permute-start.12 = (bf16[512,1024]{1,0:T(8,128)(2,1)S(1)}, bf16[512,1024]{1,0:T(8,128)(2,1)S(1)}, u32[]{:S(2)}, u32[]{:S(2)}) collective-permute-start(bf16[512,1024]{1,0:T(8,128)(2,1)S(1)} %get-tuple-element.161.a_ref), channel_id=1, source_target_pairs={{0,1},{1,0},{2,3},{3,2},{4,5},{5,4},{6,7},{7,6},{8,9},{9,8},{10,11... | collective-permute-start | bytes 3145736 | tf_op jit(solution)/shard_map/ppermute | solution.py:619
  191.4 29.0 %collective-permute-start.11 = (bf16[512,1024]{1,0:T(8,128)(2,1)S(1)}, bf16[512,1024]{1,0:T(8,128)(2,1)S(1)}, u32[]{:S(2)}, u32[]{:S(2)}) collective-permute-start(bf16[512,1024]{1,0:T(8,128)(2,1)S(1)} %get-tuple-element.166.a_ref), channel_id=1, source_target_pairs={{0,1},{1,0},{2,3},{3,2},{4,5},{5,4},{6,7},{7,6},{8,9},{9,8},{10,11... | collective-permute-start | bytes 3145736 | tf_op jit(solution)/shard_map/ppermute | solution.py:619
  221.8 41.9 %collective-permute-start.16 = (bf16[2,256,2304]{2,1,0:T(8,128)(2,1)}, bf16[2,256,2304]{2,1,0:T(8,128)(2,1)}, u32[]{:S(2)}, u32[]{:S(2)}) collective-permute-start(bf16[2,256,2304]{2,1,0:T(8,128)(2,1)} %get-tuple-element.200), channel_id=1, source_target_pairs={{0,8},{8,0},{16,24},{24,16},{1,9},{9,1},{17,25},{25,17},{2,10},{10... | collective-permute-start | bytes 7077896 | tf_op jit(solution)/shard_map/ppermute | solution.py:624
  228.1 38.3 %collective-permute-start.15 = (bf16[256,2304]{1,0:T(8,128)(2,1)S(1)}, bf16[256,2304]{1,0:T(8,128)(2,1)S(1)}, u32[]{:S(2)}, u32[]{:S(2)}) collective-permute-start(bf16[256,2304]{1,0:T(8,128)(2,1)S(1)} %fusion.8), channel_id=1, source_target_pairs={{0,16},{8,24},{16,0},{24,8},{1,17},{9,25},{17,1},{25,9},{2,18},{10... | collective-permute-start | bytes 3538952 | tf_op jit(solution)/shard_map/ppermute | solution.py:629
  243.6 52.1 %collective-permute-start.19 = (bf16[256,2304]{1,0:T(8,128)(2,1)S(1)}, bf16[256,2304]{1,0:T(8,128)(2,1)S(1)}, u32[]{:S(2)}, u32[]{:S(2)}) collective-permute-start(bf16[256,2304]{1,0:T(8,128)(2,1)S(1)} %fusion.9), channel_id=1, source_target_pairs={{0,16},{8,24},{16,0},{24,8},{1,17},{9,25},{17,1},{25,9},{2,18},{10... | collective-permute-start | bytes 3538952 | tf_op jit(solution)/shard_map/ppermute | solution.py:629
  259.4 25.7 %collective-permute-start.17 = (bf16[1024,512]{1,0:T(8,128)(2,1)S(1)}, bf16[1024,512]{1,0:T(8,128)(2,1)S(1)}, u32[]{:S(2)}, u32[]{:S(2)}) collective-permute-start(bf16[1024,512]{1,0:T(8,128)(2,1)S(1)} %get-tuple-element.195), channel_id=1, source_target_pairs={{0,2},{1,3},{8,10},{9,11},{16,18},{17,19},{24,26},{25,27}} | collective-permute-start | bytes 3145736 | tf_op jit(solution)/shard_map/ppermute | solution.py:838
  287.0 28.0 %collective-permute-start.21 = (bf16[1024,512]{1,0:T(8,128)(2,1)}, bf16[1024,512]{1,0:T(8,128)(2,1)}, u32[]{:S(2)}, u32[]{:S(2)}) collective-permute-start(bf16[1024,512]{1,0:T(8,128)(2,1)} %get-tuple-element.300), channel_id=1, source_target_pairs={{4,2},{6,4},{5,3},{7,5},{12,10},{14,12},{13,11},{15,13},{20,18},{2... | collective-permute-start | bytes 3145736 | tf_op jit(solution)/shard_map/ppermute | solution.py:838
  288.7 37.9 %collective-permute-start.20 = (bf16[1024,512]{1,0:T(8,128)(2,1)}, bf16[1024,512]{1,0:T(8,128)(2,1)}, u32[]{:S(2)}, u32[]{:S(2)}) collective-permute-start(bf16[1024,512]{1,0:T(8,128)(2,1)} %get-tuple-element.301), channel_id=1, source_target_pairs={{0,2},{2,4},{1,3},{3,5},{8,10},{10,12},{9,11},{11,13},{16,18},{18,... | collective-permute-start | bytes 3145736 | tf_op jit(solution)/shard_map/ppermute | solution.py:838
  293.7 66.4 %collective-permute-start.33 = (bf16[256,2304]{1,0:T(8,128)(2,1)}, bf16[256,2304]{1,0:T(8,128)(2,1)}, u32[]{:S(2)}, u32[]{:S(2)}) collective-permute-start(bf16[256,2304]{1,0:T(8,128)(2,1)} %fusion.10), channel_id=1, source_target_pairs={{0,16},{8,24},{16,0},{24,8},{1,17},{9,25},{17,1},{25,9},{2,18},{10... | collective-permute-start | bytes 3538952 | tf_op jit(solution)/shard_map/ppermute | solution.py:629
  294.2 89.1 %collective-permute-start.22 = (bf16[1024,1024]{1,0:T(8,128)(2,1)}, bf16[1024,1024]{1,0:T(8,128)(2,1)}, u32[]{:S(2)}, u32[]{:S(2)}) collective-permute-start(bf16[1024,1024]{1,0:T(8,128)(2,1)} %down.1), channel_id=1, source_target_pairs={{0,1},{1,0},{2,3},{3,2},{4,5},{5,4},{6,7},{7,6},{8,9},{9,8},{10,11... | collective-permute-start | bytes 6291464 | tf_op jit(solution)/shard_map/ppermute | solution.py:619
  298.6 221.3 %all-reduce.7.cloned.1.call-start = ((), (), s32[]{:S(2)}) async-start(), calls=%async_computation.3 | async-start | bytes 4030464 | tf_op jit(solution)/shard_map/psum | solution.py:889
  330.1 53.2 %collective-permute-start.24 = (bf16[1024,512]{1,0:T(8,128)(2,1)}, bf16[1024,512]{1,0:T(8,128)(2,1)}, u32[]{:S(2)}, u32[]{:S(2)}) collective-permute-start(bf16[1024,512]{1,0:T(8,128)(2,1)} %get-tuple-element.302), channel_id=1, source_target_pairs={{2,0},{4,2},{6,4},{3,1},{5,3},{7,5},{10,8},{12,10},{14,12},{11,9},... | collective-permute-start | bytes 3145736 | tf_op jit(solution)/shard_map/ppermute | solution.py:838
  331.4 53.1 %collective-permute-start.23 = (bf16[1024,512]{1,0:T(8,128)(2,1)}, bf16[1024,512]{1,0:T(8,128)(2,1)}, u32[]{:S(2)}, u32[]{:S(2)}) collective-permute-start(bf16[1024,512]{1,0:T(8,128)(2,1)} %get-tuple-element.303), channel_id=1, source_target_pairs={{0,2},{2,4},{4,6},{1,3},{3,5},{5,7},{8,10},{10,12},{12,14},{9,11},... | collective-permute-start | bytes 3145736 | tf_op jit(solution)/shard_map/ppermute | solution.py:838
  362.0 56.2 %collective-permute-start.30 = (bf16[256,512]{1,0:T(8,128)(2,1)}, bf16[256,512]{1,0:T(8,128)(2,1)}, u32[]{:S(2)}, u32[]{:S(2)}) collective-permute-start(bf16[256,512]{1,0:T(8,128)(2,1)} %fusion.18), channel_id=1, source_target_pairs={{0,16},{8,24},{16,0},{24,8},{1,17},{9,25},{17,1},{25,9},{2,18},{10... | collective-permute-start | bytes 786440 | tf_op jit(solution)/shard_map/ppermute | solution.py:629
  422.4 47.5 %collective-permute-start.26 = (bf16[1024,1024]{1,0:T(8,128)(2,1)}, bf16[1024,1024]{1,0:T(8,128)(2,1)}, u32[]{:S(2)}, u32[]{:S(2)}) collective-permute-start(bf16[1024,1024]{1,0:T(8,128)(2,1)} %get-tuple-element.228.a_ref), channel_id=1, source_target_pairs={{0,1},{1,0},{2,3},{3,2},{4,5},{5,4},{6,7},{7,6},{8,9},{9,8},{10,11... | collective-permute-start | bytes 6291464 | tf_op jit(solution)/shard_map/ppermute | solution.py:619
  (67 other events, 572.3 us)
Sparse Core Ops, SparseCore 0:
  25.0 65.7 all-gather.4
  92.9 22.6 all-gather.8
  117.1 38.0 all-gather.6
  298.7 115.8 all-reduce.8
  434.4 85.3 all-reduce.6

commit v6 on v5

--- a/solution.py
+++ b/solution.py
@@ -35,6 +35,11 @@
 def half(shape, which):
     lane = lax.broadcasted_iota(jnp.int32, shape, len(shape) - 1)
     return (lane < HD) if which == 0 else (lane >= HD)
+
+
+def row_sums(pick, x):
+    pick, high = pick.astype(BF16), x.astype(BF16)
+    return mm(pick, high, NT) + mm(pick, (x - high.astype(F32)).astype(BF16), NT)
 
 
 def pieces(m, n_ctx, block, where, order):
@@ -102,9 +107,7 @@
                 a = acc[:, 256 * hh + 128 * r : 256 * hh + 128 * r + 128]
                 out.append(a / pltpu.roll(a, HD, 1))
                 pick = jnp.where((lane == (HD if r == 0 else 0)) & (sub == 2 * hh + r), 1.0, 0.0)
-                total += lax.dot_general(
-                    pick, a, NT, precision=lax.Precision.HIGHEST, preferred_element_type=F32
-                )
+                total += row_sums(pick, a)
             mix = jnp.where(half((rows, 128), 0), out[0], out[1])
             mix_ref[:, 128 * hh : 128 * hh + 128] = mix
             mixb_ref[:, 128 * hh : 128 * hh + 128] = mix.astype(BF16)
@@ -413,10 +416,7 @@
         for hh in range(2):
             c = slice(256 * p + 128 * hh, 256 * p + 128 * hh + 128)
             x = do[:, c].astype(F32) * mix_ref[:, c]
-            total += lax.dot_general(
-                jnp.where(sub == 2 * hh + lane, 1.0, 0.0), x, NT,
-                precision=lax.Precision.HIGHEST, preferred_element_type=F32,
-            )
+            total += row_sums(jnp.where(sub == 2 * hh + lane, 1.0, 0.0), x)
         dlt_ref[p] = total
 
 

time: 544 us -> 545 us (level)
  no operation moved by 1% of the time
where the time goes in v6:
time: 545 us; the launch traced here: 535 us
  Pallas kernels  214 us (39%)
  waiting for transfers between devices  163 us (30%)
  starting transfers between devices  66.3 us (12%)
  other arithmetic  52.4 us (10%)
  local copies, waits for them, and re-layouts  20.6 us (4%)
  between operations  14.7 us (3%)
    pallas_call x4, Pallas kernels, attend_back(): pl.pallas_call(functools.partial(attend_back_body, m, n_ctx, first, block...  66.3 us
    psum x1, waiting for transfers between devices, per_device(): last, up_s = lax.psum((last, up_s), 'ctx')  42.9 us
    pallas_call x7, Pallas kernels, row_call(): pl.pallas_call(body, out_shape=tuple((pltpu.HBM(o[0].shape, o[0].dtype) i...  38.5 us
    ppermute x8, waiting for transfers between devices, swap(): return lax.ppermute(x, 'tp', [(i, i ^ 1) for i in range(n)])  37.2 us
    ppermute x3, waiting for transfers between devices, per_device(): shards[t] = lax.ppermute(shards[t - 1], 'ctx', left)  35.3 us
    pallas_call x2, Pallas kernels, middle(): pl.pallas_call(functools.partial(middle_body, min(rows, 256), len(given))...  34.9 us
    ppermute x6, starting transfers between devices, per_device(): got[side] = lax.ppermute(send, 'ctx', [(i, i + side) for i in senders])  34.6 us
    pallas_call x5, Pallas kernels, attend(): pl.pallas_call(functools.partial(attend_body, m, n_ctx, first, last, bloc...  34.4 us
  transfers between devices with their start and end apart: 39, of which 19 were waited for; matrix products, arithmetic and copies ran while one was open for 10% of the time, Pallas kernels for 37%

profile of v6, /device:TPU:0, one launch (start us, length us, event | category | flops | bytes accessed | tf_op | source)
XLA Modules:
  0.0 534.9 jit_solution(500997747505732681)
XLA Ops:
  28.7 6.4 %project_keys.1 = (bf16[1024,1024]{1,0:T(8,128)(2,1)}, f32[1024,256]{1,0:T(8,128)}, bf16[1024,512]{1,0:T(8,128)(2,1)}) custom-call(bf16[1024,1024]{1,0:T(8,128)(2,1)} %bitcast.118, f32[8,1024]{1,0:T(8,128)S(1)} %broadcast_in_dim.42.g_ref, bf16[4,272,1024]{2,1,0:T(8,128)(2,1)S(1)} %bitcast.111, f32[1024,128]{1,0:T(8,128)} %get-tuple-element.136.cos_ref, ...), custom_call_target="tpu_custom_call" | custom-call | flops 16777216 | bytes 16384 | tf_op jit(solution)/shard_map/project_keys/pallas_call | solution.py:302
  48.0 14.6 %collective-permute-done.4 = bf16[1024,512]{1,0:T(8,128)(2,1)} collective-permute-done((bf16[1024,512]{1,0:T(8,128)(2,1)}, bf16[1024,512]{1,0:T(8,128)(2,1)}, u32[]{:S(2)}, u32[]{:S(2)}) %collective-permute-start.4) | collective-permute-done | bytes 1048608 | tf_op jit(solution)/shard_map/ppermute | solution.py:757
  68.0 8.6 %attend.5.rest_0_ = f32[1024,1024]{1,0:T(8,128)S(1)} custom-call(s32[1]{0:T(128)} %bitcast.where, s32[8]{0:T(128)S(1)} %copy-done.27, bf16[1024,512]{1,0:T(8,128)(2,1)S(1)} %get-tuple-element.154.q_ref, bf16[1024,512]{1,0:T(8,128)(2,1)S(1)} %copy-done.16), custom_call_target="tpu_custom_call" | custom-call | flops 67108864 | bytes 196608 | tf_op jit(solution)/shard_map/attend/pallas_call | solution.py:143
  78.0 7.4 %attend.6.rest_0_ = f32[1024,1024]{1,0:T(8,128)} custom-call(s32[1]{0:T(128)} %bitcast.where, s32[8]{0:T(128)S(1)} %copy-done.27, bf16[1024,512]{1,0:T(8,128)(2,1)S(1)} %get-tuple-element.154.q_ref, bf16[1024,512]{1,0:T(8,128)(2,1)S(1)} %broadcast_select_fusion.kv_ref, f32[1024,1024]{1,0:T(8,128)S(1)} %attend.5.rest_0_), custom_call_target="tpu_custom_call" | custom-call | flops 67108864 | bytes 196608 | tf_op jit(solution)/shard_map/attend/pallas_call | solution.py:143
  94.2 8.7 %attend.7.rest_0_ = f32[1024,1024]{1,0:T(8,128)} custom-call(s32[1]{0:T(128)} %bitcast.where, s32[8]{0:T(128)S(1)} %copy-done.27, bf16[1024,512]{1,0:T(8,128)(2,1)S(1)} %get-tuple-element.154.q_ref, bf16[1024,512]{1,0:T(8,128)(2,1)S(1)} %select_select_fusion.1.kv_ref, f32[1024,1024]{1,0:T(8,128)} %attend.6.rest_0_), custom_call_target="tpu_custom_call" | custom-call | flops 67108864 | bytes 196608 | tf_op jit(solution)/shard_map/attend/pallas_call | solution.py:143
  102.9 15.2 %collective-permute-done.8 = bf16[1024,512]{1,0:T(8,128)(2,1)} collective-permute-done((bf16[1024,512]{1,0:T(8,128)(2,1)S(1)}, bf16[1024,512]{1,0:T(8,128)(2,1)}, u32[]{:S(2)}, u32[]{:S(2)}) %collective-permute-start.8) | collective-permute-done | bytes 1048608 | tf_op jit(solution)/shard_map/ppermute | solution.py:757
  131.3 8.0 %collective-permute-done.10.other_ref = bf16[1024,256]{1,0:T(8,128)(2,1)S(1)} collective-permute-done((bf16[1024,256]{1,0:T(8,128)(2,1)S(1)}, bf16[1024,256]{1,0:T(8,128)(2,1)S(1)}, u32[]{:S(2)}, u32[]{:S(2)}) %collective-permute-start.10) | collective-permute-done | bytes 524320 | tf_op jit(solution)/shard_map/ppermute | solution.py:619
  155.2 17.6 %middle.2 = (bf16[1024,2304]{1,0:T(8,128)(2,1)S(1)}, bf16[1024,2304]{1,0:T(8,128)(2,1)S(1)}, bf16[1024,2304]{1,0:T(8,128)(2,1)S(1)}, bf16[512,1024]{1,0:T(8,128)(2,1)S(1)}) custom-call(bf16[1024,1024]{1,0:T(8,128)(2,1)S(1)} %get-tuple-element.170.n_ref.a_ref.z_ref, bf16[1024,1024]{1,0:T(8,128)(2,1)} %bitcast.102, ...), custom_call_target="tpu_custom_call" | custom-call | flops 188743680 | bytes 331776 | tf_op jit(solution)/shard_map/middle/pallas_call | solution.py:548
  174.4 17.3 %middle.3 = (bf16[1024,2304]{1,0:T(8,128)(2,1)S(1)}, bf16[1024,2304]{1,0:T(8,128)(2,1)S(1)}, bf16[1024,2304]{1,0:T(8,128)(2,1)S(1)}, bf16[512,1024]{1,0:T(8,128)(2,1)S(1)}) custom-call(bf16[1024,1024]{1,0:T(8,128)(2,1)S(1)} %get-tuple-element.170.n_ref.a_ref.z_ref, ...), custom_call_target="tpu_custom_call", output_to_operand_aliasing={{0}: (5, {}), {1}: (6, {}), {2}: (7, {})} | custom-call | flops 188743680 | bytes 331776 | tf_op jit(solution)/shard_map/middle/pallas_call | solution.py:548
  192.4 6.6 %weight_grad.5 = (bf16[2,256,2304]{2,1,0:T(8,128)(2,1)}, bf16[2,256,2304]{2,1,0:T(8,128)(2,1)}) custom-call(s32[1]{0:T(128)} %bitcast.11.at_ref, bf16[1024,1024]{1,0:T(8,128)(2,1)S(1)} %bitcast.106, bf16[1024,1024]{1,0:T(8,128)(2,1)S(1)} %bitcast.107, bf16[1024,2304]{1,0:T(8,128)(2,1)S(1)} %get-tuple-element.177.b_ref.h_ref), custom_call_target="tpu_custom_call" | custom-call | flops 75497472 | bytes 180224 | tf_op jit(solution)/shard_map/weight_grad/pallas_call | solution.py:598
  199.0 6.6 %weight_grad.7 = (bf16[2,256,2304]{2,1,0:T(8,128)(2,1)}, bf16[2,256,2304]{2,1,0:T(8,128)(2,1)}) custom-call(s32[1]{0:T(128)} %bitcast.11.at_ref, bf16[1024,1024]{1,0:T(8,128)(2,1)S(1)} %get-tuple-element.170.n_ref.a_ref.z_ref, bf16[1024,1024]{1,0:T(8,128)(2,1)S(1)} %get-tuple-element.170.n_ref.a_ref.z_ref, bf16[1024,2304]{1,0:T(8,128)(2,1)S(1)} %get-tuple-element.174.b_ref), custom_call_target="tpu_custom_call" | custom-call | flops 75497472 | bytes 180224 | tf_op jit(solution)/shard_map/weight_grad/pallas_call | solution.py:598
  205.7 6.6 %weight_grad.6 = (bf16[2,256,2304]{2,1,0:T(8,128)(2,1)}, bf16[2,256,2304]{2,1,0:T(8,128)(2,1)}) custom-call(s32[1]{0:T(128)} %bitcast.11.at_ref, bf16[1024,1024]{1,0:T(8,128)(2,1)S(1)} %get-tuple-element.170.n_ref.a_ref.z_ref, bf16[1024,1024]{1,0:T(8,128)(2,1)S(1)} %get-tuple-element.170.n_ref.a_ref.z_ref, bf16[1024,2304]{1,0:T(8,128)(2,1)S(1)} %get-tuple-element.171.b_ref), custom_call_target="tpu_custom_call" | custom-call | flops 75497472 | bytes 180224 | tf_op jit(solution)/shard_map/weight_grad/pallas_call | solution.py:598
  245.4 14.0 %attend_back.4 = (f32[1024,512]{1,0:T(8,128)}, bf16[1024,512]{1,0:T(8,128)(2,1)S(1)}) custom-call(s32[1]{0:T(128)} %bitcast.where, s32[8]{0:T(128)S(1)} %copy-done.27, bf16[1024,512]{1,0:T(8,128)(2,1)S(1)} %get-tuple-element.154.q_ref, bf16[1024,512]{1,0:T(8,128)(2,1)S(1)} %get-tuple-element.190.do_ref, bf16[1024,512]{1,0:T(8,128)(2,1)S(1)} %copy-done.9, ...), custom_call_target="tpu_custom_call" | custom-call | flops 134217728 | bytes 196608 | tf_op jit(solution)/shard_map/attend_back/pallas_call | solution.py:215
  269.3 15.7 %attend_back.5 = (f32[1024,512]{1,0:T(8,128)}, bf16[1024,512]{1,0:T(8,128)(2,1)S(1)}) custom-call(s32[1]{0:T(128)} %bitcast.where, s32[8]{0:T(128)S(1)} %copy-done.27, bf16[1024,512]{1,0:T(8,128)(2,1)S(1)} %get-tuple-element.154.q_ref, bf16[1024,512]{1,0:T(8,128)(2,1)S(1)} %get-tuple-element.190.do_ref, bf16[1024,512]{1,0:T(8,128)(2,1)S(1)} %copy-done.11, ...), custom_call_target="tpu_custom_call" | custom-call | flops 134217728 | bytes 196608 | tf_op jit(solution)/shard_map/attend_back/pallas_call | solution.py:215
  299.8 15.3 %attend_back.6 = (f32[1024,512]{1,0:T(8,128)}, bf16[1024,512]{1,0:T(8,128)(2,1)S(1)}) custom-call(s32[1]{0:T(128)} %bitcast.where, s32[8]{0:T(128)S(1)} %copy-done.27, bf16[1024,512]{1,0:T(8,128)(2,1)S(1)} %get-tuple-element.154.q_ref, bf16[1024,512]{1,0:T(8,128)(2,1)S(1)} %get-tuple-element.190.do_ref, bf16[1024,512]{1,0:T(8,128)(2,1)S(1)} %copy-done.13, ...), custom_call_target="tpu_custom_call" | custom-call | flops 134217728 | bytes 196608 | tf_op jit(solution)/shard_map/attend_back/pallas_call | solution.py:215
  315.1 11.5 %collective-permute-done.20 = bf16[1024,512]{1,0:T(8,128)(2,1)} collective-permute-done((bf16[1024,512]{1,0:T(8,128)(2,1)}, bf16[1024,512]{1,0:T(8,128)(2,1)}, u32[]{:S(2)}, u32[]{:S(2)}) %collective-permute-start.20) | collective-permute-done | bytes 1048608 | tf_op jit(solution)/shard_map/ppermute | solution.py:838
  331.4 22.3 %collective-permute-start.23 = (bf16[1024,512]{1,0:T(8,128)(2,1)}, bf16[1024,512]{1,0:T(8,128)(2,1)}, u32[]{:S(2)}, u32[]{:S(2)}) collective-permute-start(bf16[1024,512]{1,0:T(8,128)(2,1)} %get-tuple-element.303), channel_id=1, source_target_pairs={{0,2},{2,4},{4,6},{1,3},{3,5},{5,7},{8,10},{10,12},{12,14},{9,11},... | collective-permute-start | bytes 3145736 | tf_op jit(solution)/shard_map/ppermute | solution.py:838
  362.1 21.3 %attend_back.7 = (f32[1024,512]{1,0:T(8,128)}, f32[1024,512]{1,0:T(8,128)}) custom-call(s32[1]{0:T(128)} %bitcast.where, s32[8]{0:T(128)S(1)} %copy-done.27, bf16[1024,512]{1,0:T(8,128)(2,1)S(1)} %get-tuple-element.154.q_ref, bf16[1024,512]{1,0:T(8,128)(2,1)S(1)} %get-tuple-element.190.do_ref, bf16[1024,512]{1,0:T(8,128)(2,1)S(1)} %copy-done.17, ...), custom_call_target="tpu_custom_call" | custom-call | flops 134217728 | bytes 196608 | tf_op jit(solution)/shard_map/attend_back/pallas_call | solution.py:215
  384.6 6.9 %rope_back.1 = (bf16[1024,1024]{1,0:T(8,128)(2,1)S(1)}, f32[8,128]{1,0:T(8,128)S(1)}) custom-call(f32[1024,512]{1,0:T(8,128)} %get-tuple-element.218.dq_ref, f32[1024,512]{1,0:T(8,128)} %get-tuple-element.221.q_ref, f32[1024,256]{1,0:T(8,128)} %get-tuple-element.222.k_ref, f32[1024,128]{1,0:T(8,128)} %get-tuple-element.136.cos_ref, ...), custom_call_target="tpu_custom_call" | custom-call | flops 13107200 | bytes 163840 | tf_op jit(solution)/shard_map/rope_back/pallas_call | solution.py:496
  402.0 12.7 %all-reduce.9.cloned.1.call-done = (bf16[256,2304]{1,0:T(8,128)(2,1)}, bf16[256,2304]{1,0:T(8,128)(2,1)}) async-done(((bf16[256,2304]{1,0:T(8,128)(2,1)}, bf16[256,2304]{1,0:T(8,128)(2,1)}), (bf16[256,2304]{1,0:T(8,128)(2,1)}, bf16[256,2304]{1,0:T(8,128)(2,1)})) %all-reduce.9.cloned.1.call-update) | async-done | bytes 2359312 | tf_op jit(solution)/shard_map/psum | solution.py:847
  423.9 9.2 %collective-permute-done.32 = bf16[1,544]{1,0:T(2,128)(2,1)S(1)} collective-permute-done((bf16[1,544]{1,0:T(2,128)(2,1)S(1)}, bf16[1,544]{1,0:T(2,128)(2,1)S(1)}, u32[]{:S(2)}, u32[]{:S(2)}) %collective-permute-start.32) | collective-permute-done | bytes 1120 | tf_op jit(solution)/shard_map/ppermute | solution.py:629
  444.5 25.4 %collective-permute-done.26.b_ref = bf16[1024,1024]{1,0:T(8,128)(2,1)} collective-permute-done((bf16[1024,1024]{1,0:T(8,128)(2,1)}, bf16[1024,1024]{1,0:T(8,128)(2,1)}, u32[]{:S(2)}, u32[]{:S(2)}) %collective-permute-start.26) | collective-permute-done | bytes 2097184 | tf_op jit(solution)/shard_map/ppermute | solution.py:619
  469.9 7.0 %leave.1 = f32[1024,1024]{1,0:T(8,128)} custom-call(bf16[1024,1024]{1,0:T(8,128)(2,1)} %get-tuple-element.228.a_ref, bf16[1024,1024]{1,0:T(8,128)(2,1)} %collective-permute-done.26.b_ref, bf16[1024,1024]{1,0:T(8,128)(2,1)} %bitcast.120, f32[8,1024]{1,0:T(8,128)S(1)} %broadcast_in_dim.42.g_ref, f32[1024,1024]{1,0:T(8,128)} %get-tuple-element.229.d_ref), custom_call_target="tpu_custom_call" | custom-call | flops 262144 | bytes 16384 | tf_op jit(solution)/shard_map/leave/pallas_call | solution.py:302
  476.9 42.9 %all-reduce.7.cloned.1.call-done = (bf16[272,1536]{1,0:T(8,128)(2,1)}, bf16[256,2304]{1,0:T(8,128)(2,1)}) async-done(((bf16[272,1536]{1,0:T(8,128)(2,1)}, bf16[256,2304]{1,0:T(8,128)(2,1)}), (bf16[272,1536]{1,0:T(8,128)(2,1)}, bf16[256,2304]{1,0:T(8,128)(2,1)})) %all-reduce.7.cloned.1.call-update) | async-done | bytes 2015248 | tf_op jit(solution)/shard_map/psum | solution.py:889
  (272 shorter events, 192.3 us)
Async XLA Ops:
  7.2 87.0 %all-gather.5.cloned.1.call-start = ((), (), s32[]{:S(2)}) async-start(), calls=%async_computation | async-start | bytes 11796480 | tf_op jit(solution)/shard_map/all_gather | solution.py:729
  24.9 106.4 %all-gather.9.cloned.1.call-start = ((), (), s32[]{:S(2)}) async-start(), calls=%async_computation.2 | async-start | bytes 2621440 | tf_op jit(solution)/shard_map/all_gather | solution.py:760
  35.1 120.1 %all-gather.7.cloned.1.call-start = ((), (), s32[]{:S(2)}) async-start(), calls=%async_computation.1 | async-start | bytes 5898240 | tf_op jit(solution)/shard_map/all_gather | solution.py:761
  35.2 27.5 %collective-permute-start.4 = (bf16[1024,512]{1,0:T(8,128)(2,1)}, bf16[1024,512]{1,0:T(8,128)(2,1)}, u32[]{:S(2)}, u32[]{:S(2)}) collective-permute-start(bf16[1024,512]{1,0:T(8,128)(2,1)} %get-tuple-element.138.kv_ref), channel_id=1, source_target_pairs={{2,0},{4,2},{6,4},{3,1},{5,3},{7,5},{10,8},{12,10},{14,12},{11,9},... | collective-permute-start | bytes 3145736 | tf_op jit(solution)/shard_map/ppermute | solution.py:757
  36.5 27.3 %collective-permute-start.3 = (bf16[1024,512]{1,0:T(8,128)(2,1)}, bf16[1024,512]{1,0:T(8,128)(2,1)}, u32[]{:S(2)}, u32[]{:S(2)}) collective-permute-start(bf16[1024,512]{1,0:T(8,128)(2,1)} %get-tuple-element.138.kv_ref), channel_id=1, source_target_pairs={{0,2},{2,4},{4,6},{1,3},{3,5},{5,7},{8,10},{10,12},{12,14},{9,11},... | collective-permute-start | bytes 3145736 | tf_op jit(solution)/shard_map/ppermute | solution.py:756
  63.8 350.8 %all-reduce.9.cloned.1.call-start = ((), (), s32[]{:S(2)}) async-start(), calls=%async_computation.4 | async-start | bytes 4718592 | tf_op jit(solution)/shard_map/psum | solution.py:847
  63.9 27.0 %collective-permute-start.6 = (bf16[1024,512]{1,0:T(8,128)(2,1)}, bf16[1024,512]{1,0:T(8,128)(2,1)S(1)}, u32[]{:S(2)}, u32[]{:S(2)}) collective-permute-start(bf16[1024,512]{1,0:T(8,128)(2,1)} %collective-permute-done.4), channel_id=1, source_target_pairs={{2,0},{4,2},{3,1},{5,3},{10,8},{12,10},{11,9},{13,11},{18,16},{20,... | collective-permute-start | bytes 3145736 | tf_op jit(solution)/shard_map/ppermute | solution.py:757
  65.2 25.7 %collective-permute-start.5 = (bf16[1024,512]{1,0:T(8,128)(2,1)}, bf16[1024,512]{1,0:T(8,128)(2,1)}, u32[]{:S(2)}, u32[]{:S(2)}) collective-permute-start(bf16[1024,512]{1,0:T(8,128)(2,1)} %collective-permute-done.3), channel_id=1, source_target_pairs={{2,4},{4,6},{3,5},{5,7},{10,12},{12,14},{11,13},{13,15},{18,20},{2... | collective-permute-start | bytes 3145736 | tf_op jit(solution)/shard_map/ppermute | solution.py:756
  92.5 25.6 %collective-permute-start.8 = (bf16[1024,512]{1,0:T(8,128)(2,1)S(1)}, bf16[1024,512]{1,0:T(8,128)(2,1)}, u32[]{:S(2)}, u32[]{:S(2)}) collective-permute-start(bf16[1024,512]{1,0:T(8,128)(2,1)S(1)} %collective-permute-done.6), channel_id=1, source_target_pairs={{2,0},{3,1},{10,8},{11,9},{18,16},{19,17},{26,24},{27,25}} | collective-permute-start | bytes 3145736 | tf_op jit(solution)/shard_map/ppermute | solution.py:757
  172.9 26.2 %collective-permute-start.12 = (bf16[512,1024]{1,0:T(8,128)(2,1)S(1)}, bf16[512,1024]{1,0:T(8,128)(2,1)S(1)}, u32[]{:S(2)}, u32[]{:S(2)}) collective-permute-start(bf16[512,1024]{1,0:T(8,128)(2,1)S(1)} %get-tuple-element.161.a_ref), channel_id=1, source_target_pairs={{0,1},{1,0},{2,3},{3,2},{4,5},{5,4},{6,7},{7,6},{8,9},{9,8},{10,11... | collective-permute-start | bytes 3145736 | tf_op jit(solution)/shard_map/ppermute | solution.py:619
  191.8 29.0 %collective-permute-start.11 = (bf16[512,1024]{1,0:T(8,128)(2,1)S(1)}, bf16[512,1024]{1,0:T(8,128)(2,1)S(1)}, u32[]{:S(2)}, u32[]{:S(2)}) collective-permute-start(bf16[512,1024]{1,0:T(8,128)(2,1)S(1)} %get-tuple-element.166.a_ref), channel_id=1, source_target_pairs={{0,1},{1,0},{2,3},{3,2},{4,5},{5,4},{6,7},{7,6},{8,9},{9,8},{10,11... | collective-permute-start | bytes 3145736 | tf_op jit(solution)/shard_map/ppermute | solution.py:619
  222.2 41.5 %collective-permute-start.16 = (bf16[2,256,2304]{2,1,0:T(8,128)(2,1)}, bf16[2,256,2304]{2,1,0:T(8,128)(2,1)}, u32[]{:S(2)}, u32[]{:S(2)}) collective-permute-start(bf16[2,256,2304]{2,1,0:T(8,128)(2,1)} %get-tuple-element.200), channel_id=1, source_target_pairs={{0,8},{8,0},{16,24},{24,16},{1,9},{9,1},{17,25},{25,17},{2,10},{10... | collective-permute-start | bytes 7077896 | tf_op jit(solution)/shard_map/ppermute | solution.py:624
  228.5 37.9 %collective-permute-start.15 = (bf16[256,2304]{1,0:T(8,128)(2,1)S(1)}, bf16[256,2304]{1,0:T(8,128)(2,1)S(1)}, u32[]{:S(2)}, u32[]{:S(2)}) collective-permute-start(bf16[256,2304]{1,0:T(8,128)(2,1)S(1)} %fusion.8), channel_id=1, source_target_pairs={{0,16},{8,24},{16,0},{24,8},{1,17},{9,25},{17,1},{25,9},{2,18},{10... | collective-permute-start | bytes 3538952 | tf_op jit(solution)/shard_map/ppermute | solution.py:629
  243.6 52.1 %collective-permute-start.19 = (bf16[256,2304]{1,0:T(8,128)(2,1)S(1)}, bf16[256,2304]{1,0:T(8,128)(2,1)S(1)}, u32[]{:S(2)}, u32[]{:S(2)}) collective-permute-start(bf16[256,2304]{1,0:T(8,128)(2,1)S(1)} %fusion.9), channel_id=1, source_target_pairs={{0,16},{8,24},{16,0},{24,8},{1,17},{9,25},{17,1},{25,9},{2,18},{10... | collective-permute-start | bytes 3538952 | tf_op jit(solution)/shard_map/ppermute | solution.py:629
  259.4 25.7 %collective-permute-start.17 = (bf16[1024,512]{1,0:T(8,128)(2,1)S(1)}, bf16[1024,512]{1,0:T(8,128)(2,1)S(1)}, u32[]{:S(2)}, u32[]{:S(2)}) collective-permute-start(bf16[1024,512]{1,0:T(8,128)(2,1)S(1)} %get-tuple-element.195), channel_id=1, source_target_pairs={{0,2},{1,3},{8,10},{9,11},{16,18},{17,19},{24,26},{25,27}} | collective-permute-start | bytes 3145736 | tf_op jit(solution)/shard_map/ppermute | solution.py:838
  287.0 28.0 %collective-permute-start.21 = (bf16[1024,512]{1,0:T(8,128)(2,1)}, bf16[1024,512]{1,0:T(8,128)(2,1)}, u32[]{:S(2)}, u32[]{:S(2)}) collective-permute-start(bf16[1024,512]{1,0:T(8,128)(2,1)} %get-tuple-element.300), channel_id=1, source_target_pairs={{4,2},{6,4},{5,3},{7,5},{12,10},{14,12},{13,11},{15,13},{20,18},{2... | collective-permute-start | bytes 3145736 | tf_op jit(solution)/shard_map/ppermute | solution.py:838
  288.7 37.9 %collective-permute-start.20 = (bf16[1024,512]{1,0:T(8,128)(2,1)}, bf16[1024,512]{1,0:T(8,128)(2,1)}, u32[]{:S(2)}, u32[]{:S(2)}) collective-permute-start(bf16[1024,512]{1,0:T(8,128)(2,1)} %get-tuple-element.301), channel_id=1, source_target_pairs={{0,2},{2,4},{1,3},{3,5},{8,10},{10,12},{9,11},{11,13},{16,18},{18,... | collective-permute-start | bytes 3145736 | tf_op jit(solution)/shard_map/ppermute | solution.py:838
  293.7 66.4 %collective-permute-start.33 = (bf16[256,2304]{1,0:T(8,128)(2,1)}, bf16[256,2304]{1,0:T(8,128)(2,1)}, u32[]{:S(2)}, u32[]{:S(2)}) collective-permute-start(bf16[256,2304]{1,0:T(8,128)(2,1)} %fusion.10), channel_id=1, source_target_pairs={{0,16},{8,24},{16,0},{24,8},{1,17},{9,25},{17,1},{25,9},{2,18},{10... | collective-permute-start | bytes 3538952 | tf_op jit(solution)/shard_map/ppermute | solution.py:629
  294.2 89.1 %collective-permute-start.22 = (bf16[1024,1024]{1,0:T(8,128)(2,1)}, bf16[1024,1024]{1,0:T(8,128)(2,1)}, u32[]{:S(2)}, u32[]{:S(2)}) collective-permute-start(bf16[1024,1024]{1,0:T(8,128)(2,1)} %down.1), channel_id=1, source_target_pairs={{0,1},{1,0},{2,3},{3,2},{4,5},{5,4},{6,7},{7,6},{8,9},{9,8},{10,11... | collective-permute-start | bytes 6291464 | tf_op jit(solution)/shard_map/ppermute | solution.py:619
  298.6 221.3 %all-reduce.7.cloned.1.call-start = ((), (), s32[]{:S(2)}) async-start(), calls=%async_computation.3 | async-start | bytes 4030464 | tf_op jit(solution)/shard_map/psum | solution.py:889
  330.1 53.3 %collective-permute-start.24 = (bf16[1024,512]{1,0:T(8,128)(2,1)}, bf16[1024,512]{1,0:T(8,128)(2,1)}, u32[]{:S(2)}, u32[]{:S(2)}) collective-permute-start(bf16[1024,512]{1,0:T(8,128)(2,1)} %get-tuple-element.302), channel_id=1, source_target_pairs={{2,0},{4,2},{6,4},{3,1},{5,3},{7,5},{10,8},{12,10},{14,12},{11,9},... | collective-permute-start | bytes 3145736 | tf_op jit(solution)/shard_map/ppermute | solution.py:838
  331.4 53.2 %collective-permute-start.23 = (bf16[1024,512]{1,0:T(8,128)(2,1)}, bf16[1024,512]{1,0:T(8,128)(2,1)}, u32[]{:S(2)}, u32[]{:S(2)}) collective-permute-start(bf16[1024,512]{1,0:T(8,128)(2,1)} %get-tuple-element.303), channel_id=1, source_target_pairs={{0,2},{2,4},{4,6},{1,3},{3,5},{5,7},{8,10},{10,12},{12,14},{9,11},... | collective-permute-start | bytes 3145736 | tf_op jit(solution)/shard_map/ppermute | solution.py:838
  362.1 56.1 %collective-permute-start.30 = (bf16[256,512]{1,0:T(8,128)(2,1)}, bf16[256,512]{1,0:T(8,128)(2,1)}, u32[]{:S(2)}, u32[]{:S(2)}) collective-permute-start(bf16[256,512]{1,0:T(8,128)(2,1)} %fusion.18), channel_id=1, source_target_pairs={{0,16},{8,24},{16,0},{24,8},{1,17},{9,25},{17,1},{25,9},{2,18},{10... | collective-permute-start | bytes 786440 | tf_op jit(solution)/shard_map/ppermute | solution.py:629
  422.4 47.5 %collective-permute-start.26 = (bf16[1024,1024]{1,0:T(8,128)(2,1)}, bf16[1024,1024]{1,0:T(8,128)(2,1)}, u32[]{:S(2)}, u32[]{:S(2)}) collective-permute-start(bf16[1024,1024]{1,0:T(8,128)(2,1)} %get-tuple-element.228.a_ref), channel_id=1, source_target_pairs={{0,1},{1,0},{2,3},{3,2},{4,5},{5,4},{6,7},{7,6},{8,9},{9,8},{10,11... | collective-permute-start | bytes 6291464 | tf_op jit(solution)/shard_map/ppermute | solution.py:619
  (67 other events, 571.4 us)
Sparse Core Ops, SparseCore 0:
  25.0 65.7 all-gather.4
  92.9 22.6 all-gather.8
  117.1 38.0 all-gather.6
  298.7 115.8 all-reduce.8
  434.5 85.3 all-reduce.6
